TPU v7x, 32 devices: a whole 2x2x4 slice. The times are simulated.
32 devices in a mesh: dp: 8 (over y, x, core), tensor: 4 (over z).
Axes of the slice: x: 2, y: 2, z: 4, core: 2. Of those that a mesh axis runs over, the one named last changes fastest.
Arguments:
- inputs: bfloat16 [2, 8192, 1536], P(None, ('dp', 'tensor')), may hold values from -6 to 6
- seq_lengths: int32 [16], replicated, may hold values from 256 to 1024, as said below
- seq_assign: int32 [2, 8], P(None, 'dp'), may hold values from 0 to 15, as said below
- norm1_gain: float32 [1536], replicated, may hold values from 0.25 to 1.75
- w_query: bfloat16 [1536, 1536], P('dp', 'tensor'), may hold values from -0.15625 to 0.15625
- w_key: bfloat16 [1536, 1536], P('dp', 'tensor'), may hold values from -0.15625 to 0.15625
- w_value: bfloat16 [1536, 1536], P('dp', 'tensor'), may hold values from -0.15625 to 0.15625
- w_forget: bfloat16 [1536, 24], P('dp', 'tensor'), may hold values from -0.15625 to 0.15625
- forget_bias: float32 [24], replicated, may hold values from 3 to 9
- w_out: bfloat16 [1536, 1536], P('tensor', 'dp'), may hold values from -0.875 to 0.875
- norm2_gain: float32 [1536], replicated, may hold values from 0.25 to 1.75
- w_gate: bfloat16 [1536, 4096], P('dp', 'tensor'), may hold values from -0.15625 to 0.15625
- w_up: bfloat16 [1536, 4096], P('dp', 'tensor'), may hold values from -0.15625 to 0.15625
- w_down: bfloat16 [4096, 1536], P('tensor', 'dp'), may hold values from -0.1875 to 0.1875
- out_grad: bfloat16 [2, 8192, 1536], P(None, ('dp', 'tensor')), may hold values from -6 to 6
Outputs:
- outputs: bfloat16 [2, 8192, 1536], P(None, ('dp', 'tensor'))
- input_grad: bfloat16 [2, 8192, 1536], P(None, ('dp', 'tensor'))
- norm1_gain_grad: float32 [1536], replicated
- w_query_grad: float32 [1536, 1536], P('dp', 'tensor')
- w_key_grad: float32 [1536, 1536], P('dp', 'tensor')
- w_value_grad: float32 [1536, 1536], P('dp', 'tensor')
- w_forget_grad: float32 [1536, 24], P('dp', 'tensor')
- forget_bias_grad: float32 [24], replicated
- w_out_grad: float32 [1536, 1536], P('tensor', 'dp')
- norm2_gain_grad: float32 [1536], replicated
- w_gate_grad: float32 [1536, 4096], P('dp', 'tensor')
- w_up_grad: float32 [1536, 4096], P('dp', 'tensor')
- w_down_grad: float32 [4096, 1536], P('tensor', 'dp')
Inputs may be any that keep to these rules, and one draw needn't show every extreme that they name: `seq_lengths`: each sequence's valid slots are a prefix of its 1024 slots; some sequence has exactly 1024 valid slots and another exactly 256. `seq_assign`: A permutation of the 16 sequence numbers: every sequence occupies exactly one block.
All inputs are finite; a program needn't handle non-finite values.
Results may differ from a plain program's by a relative error of at most 0.015.
Values may be sent and summed in bfloat16 or wider, within the bound.
A program may use at most 256 MiB of HBM per device.

v0:
```python
import jax
import jax.numpy as jnp
from jax import lax
from jax.sharding import PartitionSpec as P

EPS = 1e-06
NEG_BIG = -1e30
WEIGHT_DIMS = (0, 0, 0, 0, 1, 0, 0, 1)


def row_scale(tokens):
    return lax.rsqrt(jnp.mean(tokens * tokens, axis=-1, keepdims=True) + EPS)


def norm_back(tokens, scaling, gain, grad_out):
    weighted = grad_out * gain
    cubed = scaling * scaling * scaling
    return scaling * weighted - tokens * cubed * jnp.mean(weighted * tokens, axis=-1, keepdims=True)


def fetch_weights(w_query, w_key, w_value, w_forget, w_out, w_gate, w_up, w_down):
    return (
        lax.all_gather(w_query, "dp", axis=0, tiled=True),
        lax.all_gather(w_key, "dp", axis=0, tiled=True),
        lax.all_gather(w_value, "dp", axis=0, tiled=True),
        lax.all_gather(w_forget, "dp", axis=0, tiled=True),
        lax.all_gather(w_out, "dp", axis=1, tiled=True),
        lax.all_gather(w_gate, "dp", axis=0, tiled=True),
        lax.all_gather(w_up, "dp", axis=0, tiled=True),
        lax.all_gather(w_down, "dp", axis=1, tiled=True),
    )


def reduce_weights(grad_terms):
    return (
        lax.psum_scatter(grad_terms[0], "dp", scatter_dimension=0, tiled=True),
        lax.psum_scatter(grad_terms[1], "dp", scatter_dimension=0, tiled=True),
        lax.psum_scatter(grad_terms[2], "dp", scatter_dimension=0, tiled=True),
        lax.psum_scatter(grad_terms[3], "dp", scatter_dimension=0, tiled=True),
        lax.psum_scatter(grad_terms[4], "dp", scatter_dimension=1, tiled=True),
        lax.psum_scatter(grad_terms[5], "dp", scatter_dimension=0, tiled=True),
        lax.psum_scatter(grad_terms[6], "dp", scatter_dimension=0, tiled=True),
        lax.psum_scatter(grad_terms[7], "dp", scatter_dimension=1, tiled=True),
    )


def spread_rows(row_block):
    return lax.all_gather(row_block, "tensor", axis=0, tiled=True)


def collect_rows(row_terms):
    return lax.psum_scatter(row_terms, "tensor", scatter_dimension=0, tiled=True)


def spread_grads(row_block):
    return lax.all_gather(row_block, "tensor", axis=0, tiled=True)


def collect_grads(row_terms):
    return lax.psum_scatter(row_terms, "tensor", scatter_dimension=0, tiled=True)


def block_scores(query_rows, key_rows, cumul_rows, cumul_gate, offset, key_ok):
    raw_dot = (
        jnp.einsum("ihd,jhd->hij", query_rows, key_rows, preferred_element_type=jnp.float32) * 0.125
    )
    scores = raw_dot + cumul_rows.T[:, :, None] - cumul_gate.T[:, None, :]
    query_pos = offset + jnp.arange(query_rows.shape[0])
    key_pos = jnp.arange(key_rows.shape[0])
    allowed = (key_pos[None, :] <= query_pos[:, None]) & key_ok[None, :]
    return jnp.where(allowed[None], scores, NEG_BIG)


def attend_forward(queries, key_rows, value_rows, cumul_gate, key_ok, block_rows):
    seq_rows = queries.shape[0]
    mixed_parts = []
    total_parts = []
    for offset in range(0, seq_rows, block_rows):
        query_rows = queries[offset : offset + block_rows]
        scores = block_scores(
            query_rows,
            key_rows,
            cumul_gate[offset : offset + block_rows],
            cumul_gate,
            offset,
            key_ok,
        )
        row_max = jnp.max(scores, axis=-1, keepdims=True)
        shifted = jnp.exp(scores - row_max)
        row_sum = jnp.sum(shifted, axis=-1, keepdims=True)
        attn_probs = (shifted / row_sum).astype(jnp.bfloat16)
        mixed_parts.append(
            jnp.einsum("hij,jhd->ihd", attn_probs, value_rows, preferred_element_type=jnp.float32)
        )
        total_parts.append(row_max + jnp.log(row_sum))
    return (jnp.concatenate(mixed_parts, axis=0), jnp.concatenate(total_parts, axis=1))


def attend_backward(
    queries, key_rows, value_rows, cumul_gate, key_ok, log_total, grad_mixed, block_rows
):
    seq_rows = queries.shape[0]
    grad_keys = jnp.zeros(key_rows.shape, jnp.float32)
    grad_values = jnp.zeros(value_rows.shape, jnp.float32)
    key_side = jnp.zeros((key_rows.shape[1], seq_rows), jnp.float32)
    query_parts = []
    query_side = []
    for offset in range(0, seq_rows, block_rows):
        query_rows = queries[offset : offset + block_rows]
        grad_rows = grad_mixed[offset : offset + block_rows]
        scores = block_scores(
            query_rows,
            key_rows,
            cumul_gate[offset : offset + block_rows],
            cumul_gate,
            offset,
            key_ok,
        )
        attn_probs = jnp.exp(scores - log_total[:, offset : offset + block_rows])
        grad_probs = jnp.einsum(
            "ihd,jhd->hij", grad_rows, value_rows, preferred_element_type=jnp.float32
        )
        row_dot = jnp.sum(attn_probs * grad_probs, axis=-1, keepdims=True)
        grad_scores = attn_probs * (grad_probs - row_dot)
        query_side.append(jnp.sum(grad_scores, axis=-1))
        key_side = key_side + jnp.sum(grad_scores, axis=1)
        grad_low = grad_scores.astype(jnp.bfloat16)
        grad_values = grad_values + jnp.einsum(
            "hij,ihd->jhd",
            attn_probs.astype(jnp.bfloat16),
            grad_rows,
            preferred_element_type=jnp.float32,
        )
        query_parts.append(
            jnp.einsum("hij,jhd->ihd", grad_low, key_rows, preferred_element_type=jnp.float32)
            * 0.125
        )
        grad_keys = (
            grad_keys
            + jnp.einsum("hij,ihd->jhd", grad_low, query_rows, preferred_element_type=jnp.float32)
            * 0.125
        )
    grad_cumul = (jnp.concatenate(query_side, axis=1) - key_side).T
    return (jnp.concatenate(query_parts, axis=0), grad_keys, grad_values, grad_cumul)


def widened(shape, along, spread):
    if along == 0:
        return (shape[0] * spread, shape[1])
    return (shape[0], shape[1] * spread)


def body(
    inputs,
    seq_lengths,
    seq_assign,
    norm1_gain,
    w_query,
    w_key,
    w_value,
    w_forget,
    forget_bias,
    w_out,
    norm2_gain,
    w_gate,
    w_up,
    w_down,
    out_grad,
):
    f32 = jnp.float32
    bf16 = jnp.bfloat16
    part_rows = inputs.shape[1]
    tensor_ways = lax.axis_size("tensor")
    seq_rows = part_rows * tensor_ways
    block_rows = min(512, seq_rows)
    tensor_pos = lax.axis_index("tensor")
    heads_here = w_forget.shape[1]
    head_size = w_query.shape[1] // heads_here
    bias_here = lax.dynamic_slice_in_dim(forget_bias, tensor_pos * heads_here, heads_here)
    seq_ids = seq_assign[:, 0]
    number = seq_lengths.shape[0]
    lengths_here = jnp.sum(
        jnp.where(seq_ids[:, None] == jnp.arange(number)[None, :], seq_lengths[None, :], 0), axis=1
    )
    local_pos = tensor_pos * part_rows + jnp.arange(part_rows)
    whole_pos = jnp.arange(seq_rows)
    shards = (w_query, w_key, w_value, w_forget, w_out, w_gate, w_up, w_down)
    spread = lax.axis_size("dp")
    grad_init = tuple(
        (
            jnp.zeros(widened(shard.shape, along, spread), f32)
            for shard, along in zip(shards, WEIGHT_DIMS)
        )
    )
    small_init = (
        jnp.zeros(norm1_gain.shape, f32),
        jnp.zeros((heads_here,), f32),
        jnp.zeros(norm2_gain.shape, f32),
    )

    def heads_view(matrix):
        return matrix.reshape(seq_rows, heads_here, head_size)

    def micro_step(carried, micro_item):
        grad_acc, small_acc = carried
        tokens_low, cot_low, length = micro_item
        rows_in = tokens_low.astype(f32)
        valid_here = (local_pos < length).astype(f32)[:, None]
        key_ok = whole_pos < length
        valid_whole = key_ok.astype(f32)[:, None]
        forward_weights = fetch_weights(
            w_query, w_key, w_value, w_forget, w_out, w_gate, w_up, w_down
        )
        full_query, full_key, full_value, full_forget, full_out, full_gate, full_up, full_down = (
            forward_weights
        )
        scale_one = row_scale(rows_in)
        normed_one = spread_rows((rows_in * scale_one * norm1_gain).astype(bf16))
        queries = heads_view(
            jnp.dot(normed_one, full_query, preferred_element_type=f32).astype(bf16)
        )
        key_rows = heads_view(
            jnp.dot(normed_one, full_key, preferred_element_type=f32).astype(bf16)
        )
        value_rows = heads_view(
            jnp.dot(normed_one, full_value, preferred_element_type=f32).astype(bf16)
        )
        forget_logit = jnp.dot(normed_one, full_forget, preferred_element_type=f32) + bias_here
        cumul_gate = jnp.cumsum(jax.nn.log_sigmoid(forget_logit), axis=0)
        mixed_rows, log_total = attend_forward(
            queries, key_rows, value_rows, cumul_gate, key_ok, block_rows
        )
        mixed_low = (mixed_rows.reshape(seq_rows, -1) * valid_whole).astype(bf16)
        hidden_in = rows_in + collect_rows(jnp.dot(mixed_low, full_out, preferred_element_type=f32))
        scale_two = row_scale(hidden_in)
        normed_two = spread_rows((hidden_in * scale_two * norm2_gain).astype(bf16))
        gate_pre = jnp.dot(normed_two, full_gate, preferred_element_type=f32)
        up_pre = jnp.dot(normed_two, full_up, preferred_element_type=f32)
        gate_sig = jax.nn.sigmoid(gate_pre)
        gate_act = gate_pre * gate_sig
        inner_low = (gate_act * up_pre).astype(bf16)
        ffn_rows = collect_rows(jnp.dot(inner_low, full_down, preferred_element_type=f32))
        out_rows = (valid_here * (hidden_in + ffn_rows)).astype(bf16)
        back_weights = fetch_weights(w_query, w_key, w_value, w_forget, w_out, w_gate, w_up, w_down)
        full_query, full_key, full_value, full_forget, full_out, full_gate, full_up, full_down = (
            back_weights
        )
        cotangent = cot_low.astype(f32)
        grad_ffn = spread_grads((valid_here * cotangent).astype(bf16))
        grad_inner = jnp.einsum("sd,fd->sf", grad_ffn, full_down, preferred_element_type=f32)
        grad_down = jnp.einsum("sf,sd->fd", inner_low, grad_ffn, preferred_element_type=f32)
        slope = gate_sig * (1.0 + gate_pre * (1.0 - gate_sig))
        grad_gate = (grad_inner * up_pre * slope).astype(bf16)
        grad_up = (grad_inner * gate_act).astype(bf16)
        grad_wgate = jnp.einsum("sd,sf->df", normed_two, grad_gate, preferred_element_type=f32)
        grad_wup = jnp.einsum("sd,sf->df", normed_two, grad_up, preferred_element_type=f32)
        two_terms = jnp.einsum(
            "sf,df->sd", grad_gate, full_gate, preferred_element_type=f32
        ) + jnp.einsum("sf,df->sd", grad_up, full_up, preferred_element_type=f32)
        grad_normed_two = collect_grads(two_terms)
        gain_two = jnp.sum(grad_normed_two * hidden_in * scale_two, axis=0)
        grad_hidden = valid_here * cotangent + norm_back(
            hidden_in, scale_two, norm2_gain, grad_normed_two
        )
        grad_attn = spread_grads(grad_hidden.astype(bf16))
        grad_wout = jnp.einsum("sh,sd->hd", mixed_low, grad_attn, preferred_element_type=f32)
        grad_mixed = jnp.einsum(
            "sd,hd->sh", grad_attn, full_out, preferred_element_type=f32
        ).astype(bf16) * valid_whole.astype(bf16)
        grad_q, grad_k, grad_v, grad_cumul = attend_backward(
            queries,
            key_rows,
            value_rows,
            cumul_gate,
            key_ok,
            log_total,
            heads_view(grad_mixed),
            block_rows,
        )
        grad_logf = jnp.flip(jnp.cumsum(jnp.flip(grad_cumul, 0), axis=0), 0)
        grad_logit = grad_logf * jax.nn.sigmoid(-forget_logit)
        bias_term = jnp.sum(grad_logit, axis=0)
        logit_low = grad_logit.astype(bf16)
        query_low = grad_q.reshape(seq_rows, -1).astype(bf16)
        key_low = grad_k.reshape(seq_rows, -1).astype(bf16)
        value_low = grad_v.reshape(seq_rows, -1).astype(bf16)
        one_terms = jnp.einsum("sh,dh->sd", query_low, full_query, preferred_element_type=f32)
        one_terms = one_terms + jnp.einsum(
            "sh,dh->sd", key_low, full_key, preferred_element_type=f32
        )
        one_terms = one_terms + jnp.einsum(
            "sh,dh->sd", value_low, full_value, preferred_element_type=f32
        )
        one_terms = one_terms + jnp.einsum(
            "sh,dh->sd", logit_low, full_forget, preferred_element_type=f32
        )
        grad_normed_one = collect_grads(one_terms)
        grad_wquery = jnp.einsum("sd,sh->dh", normed_one, query_low, preferred_element_type=f32)
        grad_wkey = jnp.einsum("sd,sh->dh", normed_one, key_low, preferred_element_type=f32)
        grad_wvalue = jnp.einsum("sd,sh->dh", normed_one, value_low, preferred_element_type=f32)
        grad_wforget = jnp.einsum("sd,sh->dh", normed_one, logit_low, preferred_element_type=f32)
        gain_one = jnp.sum(grad_normed_one * rows_in * scale_one, axis=0)
        grad_rows = (
            grad_hidden + norm_back(rows_in, scale_one, norm1_gain, grad_normed_one)
        ).astype(bf16)
        micro_grads = (
            grad_wquery,
            grad_wkey,
            grad_wvalue,
            grad_wforget,
            grad_wout,
            grad_wgate,
            grad_wup,
            grad_down,
        )
        grad_acc = tuple((left + right for left, right in zip(grad_acc, micro_grads)))
        small_acc = (small_acc[0] + gain_one, small_acc[1] + bias_term, small_acc[2] + gain_two)
        return ((grad_acc, small_acc), (out_rows, grad_rows))

    (grad_acc, small_acc), (outputs, input_grad) = lax.scan(
        micro_step, (grad_init, small_init), (inputs, out_grad, lengths_here)
    )
    weight_grads = reduce_weights(grad_acc)
    bias_full = lax.dynamic_update_slice_in_dim(
        jnp.zeros(forget_bias.shape, f32), small_acc[1], tensor_pos * heads_here, 0
    )
    gain_one_sum, bias_sum, gain_two_sum = lax.psum(
        (small_acc[0], bias_full, small_acc[2]), ("dp", "tensor")
    )
    return (
        outputs,
        input_grad,
        gain_one_sum,
        weight_grads[0],
        weight_grads[1],
        weight_grads[2],
        weight_grads[3],
        bias_sum,
        weight_grads[4],
        gain_two_sum,
        weight_grads[5],
        weight_grads[6],
        weight_grads[7],
    )


def solution(mesh):
    return jax.shard_map(
        body,
        mesh=mesh,
        in_specs=(
            P(None, ("dp", "tensor"), None),
            P(),
            P(None, "dp"),
            P(),
            P("dp", "tensor"),
            P("dp", "tensor"),
            P("dp", "tensor"),
            P("dp", "tensor"),
            P(),
            P("tensor", "dp"),
            P(),
            P("dp", "tensor"),
            P("dp", "tensor"),
            P("tensor", "dp"),
            P(None, ("dp", "tensor"), None),
        ),
        out_specs=(
            P(None, ("dp", "tensor"), None),
            P(None, ("dp", "tensor"), None),
            P(),
            P("dp", "tensor"),
            P("dp", "tensor"),
            P("dp", "tensor"),
            P("dp", "tensor"),
            P(),
            P("tensor", "dp"),
            P(),
            P("dp", "tensor"),
            P("dp", "tensor"),
            P("tensor", "dp"),
        ),
        check_vma=False,
    )
```

profile of v0, /device:TPU:0, one launch (start us, length us, event | category | flops | bytes accessed | tf_op | source)
XLA Modules:
  0.0 2340.0 jit_solution(12627288775017756879)
XLA Ops:
  10.3 1902.0 %while.35 = (s32[]{:T(128)}, f32[1536,384]{1,0:T(8,128)}, f32[1536,384]{1,0:T(8,128)}, f32[1536,384]{1,0:T(8,128)}, f32[1536,6]{0,1:T(8,128)}, /*index=5*/f32[38...) while((s32[]{:T(128)}, f32[1536,384]{1,0:T(8,128)}, ...), condition=%wide.region_27.28_spmd.clone, body=%wide.region_1.27_spmd.clone.sunk | while | flops 48574210048 | bytes 1269308928 | solution.py:320
  33.6 48.3 %all-gather.16.cloned.1.call-done = bf16[1024,1536]{1,0:T(8,128)(2,1)} async-done(((bf16[256,1536]{1,0:T(8,128)(2,1)}), bf16[1024,1536]{1,0:T(8,128)(2,1)}) %all-gather.16.cloned.1.call-update) | async-done | bytes 3145744 | tf_op jit(solution)/shard_map/while/body/eval_jaxpr/all_gather | solution.py:48
  193.5 106.9 %reduce-scatter.31.cloned.1.call-done = f32[256,1536]{1,0:T(8,128)} async-done(((f32[1024,1536]{1,0:T(8,128)}), f32[256,1536]{1,0:T(8,128)}) %reduce-scatter.31.cloned.1.call-update) | async-done | bytes 1572880 | tf_op jit(solution)/shard_map/while/body/eval_jaxpr/reduce_scatter | solution.py:52
  304.6 62.0 %all-gather.30.cloned.1.call-done = bf16[1024,1536]{1,0:T(8,128)(2,1)} async-done(((bf16[256,1536]{1,0:T(8,128)(2,1)}), bf16[1024,1536]{1,0:T(8,128)(2,1)}) %all-gather.30.cloned.1.call-update) | async-done | bytes 3145744 | tf_op jit(solution)/shard_map/while/body/eval_jaxpr/all_gather | solution.py:56
  366.6 32.7 %all-gather.32.cloned.1.call-done = bf16[1024,1536]{0,1:T(8,128)(2,1)} async-done(((bf16[1024,192]{0,1:T(8,128)(2,1)}), bf16[1024,1536]{0,1:T(8,128)(2,1)}) %all-gather.32.cloned.1.call-update) | async-done | bytes 3145744 | tf_op jit(solution)/shard_map/while/body/eval_jaxpr/all_gather | solution.py:30
  433.4 65.5 %all-gather.26.cloned.1.call-done = bf16[1024,1536]{1,0:T(8,128)(2,1)} async-done(((bf16[256,1536]{1,0:T(8,128)(2,1)}), bf16[1024,1536]{1,0:T(8,128)(2,1)}) %all-gather.26.cloned.1.call-update) | async-done | bytes 3145744 | tf_op jit(solution)/shard_map/while/body/eval_jaxpr/all_gather | solution.py:48
  552.4 110.9 %reduce-scatter.33.cloned.1.call-done = f32[256,1536]{1,0:T(8,128)} async-done(((f32[1024,1536]{1,0:T(8,128)}), f32[256,1536]{1,0:T(8,128)}) %reduce-scatter.33.cloned.1.call-update) | async-done | bytes 1572880 | tf_op jit(solution)/shard_map/while/body/eval_jaxpr/reduce_scatter | solution.py:60
  678.5 54.1 %all-gather.36.cloned.1.call-done = bf16[1024,1536]{1,0:T(8,128)(2,1)} async-done(((bf16[256,1536]{1,0:T(8,128)(2,1)}), bf16[1024,1536]{1,0:T(8,128)(2,1)}) %all-gather.36.cloned.1.call-update) | async-done | bytes 3145744 | tf_op jit(solution)/shard_map/while/body/eval_jaxpr/all_gather | solution.py:56
  863.9 93.8 %reduce-scatter.35.cloned.1.call-done = f32[256,1536]{1,0:T(8,128)} async-done(((f32[1024,1536]{1,0:T(8,128)}), f32[256,1536]{1,0:T(8,128)}) %reduce-scatter.35.cloned.1.call-update) | async-done | bytes 1572880 | tf_op jit(solution)/shard_map/while/body/eval_jaxpr/reduce_scatter | solution.py:60
  982.6 47.7 %all-gather.16.cloned.1.call-done = bf16[1024,1536]{1,0:T(8,128)(2,1)} async-done(((bf16[256,1536]{1,0:T(8,128)(2,1)}), bf16[1024,1536]{1,0:T(8,128)(2,1)}) %all-gather.16.cloned.1.call-update) | async-done | bytes 3145744 | tf_op jit(solution)/shard_map/while/body/eval_jaxpr/all_gather | solution.py:48
  1141.7 107.1 %reduce-scatter.31.cloned.1.call-done = f32[256,1536]{1,0:T(8,128)} async-done(((f32[1024,1536]{1,0:T(8,128)}), f32[256,1536]{1,0:T(8,128)}) %reduce-scatter.31.cloned.1.call-update) | async-done | bytes 1572880 | tf_op jit(solution)/shard_map/while/body/eval_jaxpr/reduce_scatter | solution.py:52
  1252.4 62.5 %all-gather.30.cloned.1.call-done = bf16[1024,1536]{1,0:T(8,128)(2,1)} async-done(((bf16[256,1536]{1,0:T(8,128)(2,1)}), bf16[1024,1536]{1,0:T(8,128)(2,1)}) %all-gather.30.cloned.1.call-update) | async-done | bytes 3145744 | tf_op jit(solution)/shard_map/while/body/eval_jaxpr/all_gather | solution.py:56
  1314.9 32.7 %all-gather.32.cloned.1.call-done = bf16[1024,1536]{0,1:T(8,128)(2,1)} async-done(((bf16[1024,192]{0,1:T(8,128)(2,1)}), bf16[1024,1536]{0,1:T(8,128)(2,1)}) %all-gather.32.cloned.1.call-update) | async-done | bytes 3145744 | tf_op jit(solution)/shard_map/while/body/eval_jaxpr/all_gather | solution.py:30
  1381.6 65.6 %all-gather.26.cloned.1.call-done = bf16[1024,1536]{1,0:T(8,128)(2,1)} async-done(((bf16[256,1536]{1,0:T(8,128)(2,1)}), bf16[1024,1536]{1,0:T(8,128)(2,1)}) %all-gather.26.cloned.1.call-update) | async-done | bytes 3145744 | tf_op jit(solution)/shard_map/while/body/eval_jaxpr/all_gather | solution.py:48
  1500.7 110.9 %reduce-scatter.33.cloned.1.call-done = f32[256,1536]{1,0:T(8,128)} async-done(((f32[1024,1536]{1,0:T(8,128)}), f32[256,1536]{1,0:T(8,128)}) %reduce-scatter.33.cloned.1.call-update) | async-done | bytes 1572880 | tf_op jit(solution)/shard_map/while/body/eval_jaxpr/reduce_scatter | solution.py:60
  1626.7 54.1 %all-gather.36.cloned.1.call-done = bf16[1024,1536]{1,0:T(8,128)(2,1)} async-done(((bf16[256,1536]{1,0:T(8,128)(2,1)}), bf16[1024,1536]{1,0:T(8,128)(2,1)}) %all-gather.36.cloned.1.call-update) | async-done | bytes 3145744 | tf_op jit(solution)/shard_map/while/body/eval_jaxpr/all_gather | solution.py:56
  1819.8 86.2 %reduce-scatter.35.cloned.1.call-done = f32[256,1536]{1,0:T(8,128)} async-done(((f32[1024,1536]{1,0:T(8,128)}), f32[256,1536]{1,0:T(8,128)}) %reduce-scatter.35.cloned.1.call-update) | async-done | bytes 1572880 | tf_op jit(solution)/shard_map/while/body/eval_jaxpr/reduce_scatter | solution.py:60
  1927.2 41.1 %all-reduce = (f32[1536]{0:T(1024)}, f32[24]{0:T(128)}, f32[1536]{0:T(1024)}) all-reduce(f32[1536]{0:T(1024)S(1)} %copy-done.74, f32[24]{0:T(128)S(1)} %dynamic_update_slice.10, f32[1536]{0:T(1024)S(1)} %copy-done.71), channel_id=1, replica_groups=mesh['dp'=8,'tensor'=4] {'dp','tensor'}, use_global_device_ids=true, to_apply=%region_28.29 | all-reduce | flops 3096 | bytes 24768 | tf_op jit(solution)/shard_map/psum | solution.py:327
  1997.5 46.0 %reduce-scatter.17.cloned.1.call-done = f32[192,384]{1,0:T(8,128)} async-done(((f32[1536,384]{1,0:T(8,128)}), f32[192,384]{1,0:T(8,128)}) %reduce-scatter.17.cloned.1.call-update) | async-done | bytes 294928 | tf_op jit(solution)/shard_map/reduce_scatter | solution.py:37
  2043.5 46.1 %reduce-scatter.19.cloned.1.call-done = f32[192,384]{1,0:T(8,128)} async-done(((f32[1536,384]{1,0:T(8,128)}), f32[192,384]{1,0:T(8,128)}) %reduce-scatter.19.cloned.1.call-update) | async-done | bytes 294928 | tf_op jit(solution)/shard_map/reduce_scatter | solution.py:38
  2089.7 46.2 %reduce-scatter.21.cloned.1.call-done = f32[384,192]{0,1:T(8,128)} async-done(((f32[384,1536]{0,1:T(8,128)}), f32[384,192]{0,1:T(8,128)}) %reduce-scatter.21.cloned.1.call-update) | async-done | bytes 294928 | tf_op jit(solution)/shard_map/reduce_scatter | solution.py:40
  2135.9 65.6 %reduce-scatter.23.cloned.1.call-done = f32[192,1024]{1,0:T(8,128)} async-done(((f32[1536,1024]{1,0:T(8,128)}), f32[192,1024]{1,0:T(8,128)}) %reduce-scatter.23.cloned.1.call-update) | async-done | bytes 786448 | tf_op jit(solution)/shard_map/reduce_scatter | solution.py:41
  2201.4 65.4 %reduce-scatter.25.cloned.1.call-done = f32[192,1024]{1,0:T(8,128)} async-done(((f32[1536,1024]{1,0:T(8,128)}), f32[192,1024]{1,0:T(8,128)}) %reduce-scatter.25.cloned.1.call-update) | async-done | bytes 786448 | tf_op jit(solution)/shard_map/reduce_scatter | solution.py:42
  2266.9 65.4 %reduce-scatter.27.cloned.1.call-done = f32[1024,192]{0,1:T(8,128)} async-done(((f32[1024,1536]{0,1:T(8,128)}), f32[1024,192]{0,1:T(8,128)}) %reduce-scatter.27.cloned.1.call-update) | async-done | bytes 786448 | tf_op jit(solution)/shard_map/reduce_scatter | solution.py:43
  (685 shorter events, 801.1 us)
Async XLA Ops:
  18.2 282.2 %reduce-scatter.31.cloned.1.call-start = ((), (), s32[]{:S(2)}) async-start(), calls=%async_computation.25 | async-start | bytes 7864320 | tf_op jit(solution)/shard_map/while/body/eval_jaxpr/reduce_scatter | solution.py:52
  189.5 177.1 %all-gather.30.cloned.1.call-start = ((), (), s32[]{:S(2)}) async-start(), calls=%async_computation.28 | async-start | bytes 3932160 | tf_op jit(solution)/shard_map/while/body/eval_jaxpr/all_gather | solution.py:56
  192.0 207.3 %all-gather.32.cloned.1.call-start = ((), (), s32[]{:S(2)}) async-start(), calls=%async_computation.29 | async-start | bytes 3538944 | tf_op jit(solution)/shard_map/while/body/eval_jaxpr/all_gather | solution.py:30
  192.7 240.7 %all-gather.28.cloned.1.call-start = ((), (), s32[]{:S(2)}) async-start(), calls=%async_computation.27 | async-start | bytes 3538944 | tf_op jit(solution)/shard_map/while/body/eval_jaxpr/all_gather | solution.py:28
  193.5 305.4 %all-gather.26.cloned.1.call-start = ((), (), s32[]{:S(2)}) async-start(), calls=%async_computation.26 | async-start | bytes 3932160 | tf_op jit(solution)/shard_map/while/body/eval_jaxpr/all_gather | solution.py:48
  303.2 228.4 %all-gather.34.cloned.1.call-start = ((), (), s32[]{:S(2)}) async-start(), calls=%async_computation.30 | async-start | bytes 3538944 | tf_op jit(solution)/shard_map/while/body/eval_jaxpr/all_gather | solution.py:29
  304.0 359.4 %reduce-scatter.33.cloned.1.call-start = ((), (), s32[]{:S(2)}) async-start(), calls=%async_computation.31 | async-start | bytes 7864320 | tf_op jit(solution)/shard_map/while/body/eval_jaxpr/reduce_scatter | solution.py:60
  552.4 180.2 %all-gather.36.cloned.1.call-start = ((), (), s32[]{:S(2)}) async-start(), calls=%async_computation.32 | async-start | bytes 3932160 | tf_op jit(solution)/shard_map/while/body/eval_jaxpr/all_gather | solution.py:56
  668.5 176.8 %reduce-scatter.37.cloned.1.call-start = ((), (), s32[]{:S(2)}) async-start(), calls=%async_computation.34 | async-start | bytes 7864320 | tf_op jit(solution)/shard_map/while/body/eval_jaxpr/reduce_scatter | solution.py:52
  677.1 280.5 %reduce-scatter.35.cloned.1.call-start = ((), (), s32[]{:S(2)}) async-start(), calls=%async_computation.33 | async-start | bytes 7864320 | tf_op jit(solution)/shard_map/while/body/eval_jaxpr/reduce_scatter | solution.py:60
  968.7 280.0 %reduce-scatter.31.cloned.1.call-start = ((), (), s32[]{:S(2)}) async-start(), calls=%async_computation.25 | async-start | bytes 7864320 | tf_op jit(solution)/shard_map/while/body/eval_jaxpr/reduce_scatter | solution.py:52
  1137.8 177.1 %all-gather.30.cloned.1.call-start = ((), (), s32[]{:S(2)}) async-start(), calls=%async_computation.28 | async-start | bytes 3932160 | tf_op jit(solution)/shard_map/while/body/eval_jaxpr/all_gather | solution.py:56
  1140.3 207.3 %all-gather.32.cloned.1.call-start = ((), (), s32[]{:S(2)}) async-start(), calls=%async_computation.29 | async-start | bytes 3538944 | tf_op jit(solution)/shard_map/while/body/eval_jaxpr/all_gather | solution.py:30
  1141.1 240.5 %all-gather.28.cloned.1.call-start = ((), (), s32[]{:S(2)}) async-start(), calls=%async_computation.27 | async-start | bytes 3538944 | tf_op jit(solution)/shard_map/while/body/eval_jaxpr/all_gather | solution.py:28
  1141.6 305.6 %all-gather.26.cloned.1.call-start = ((), (), s32[]{:S(2)}) async-start(), calls=%async_computation.26 | async-start | bytes 3932160 | tf_op jit(solution)/shard_map/while/body/eval_jaxpr/all_gather | solution.py:48
  1251.6 228.2 %all-gather.34.cloned.1.call-start = ((), (), s32[]{:S(2)}) async-start(), calls=%async_computation.30 | async-start | bytes 3538944 | tf_op jit(solution)/shard_map/while/body/eval_jaxpr/all_gather | solution.py:29
  1252.1 359.4 %reduce-scatter.33.cloned.1.call-start = ((), (), s32[]{:S(2)}) async-start(), calls=%async_computation.31 | async-start | bytes 7864320 | tf_op jit(solution)/shard_map/while/body/eval_jaxpr/reduce_scatter | solution.py:60
  1500.6 180.2 %all-gather.36.cloned.1.call-start = ((), (), s32[]{:S(2)}) async-start(), calls=%async_computation.32 | async-start | bytes 3932160 | tf_op jit(solution)/shard_map/while/body/eval_jaxpr/all_gather | solution.py:56
  1616.7 182.4 %reduce-scatter.37.cloned.1.call-start = ((), (), s32[]{:S(2)}) async-start(), calls=%async_computation.34 | async-start | bytes 7864320 | tf_op jit(solution)/shard_map/while/body/eval_jaxpr/reduce_scatter | solution.py:52
  1625.4 280.7 %reduce-scatter.35.cloned.1.call-start = ((), (), s32[]{:S(2)}) async-start(), calls=%async_computation.33 | async-start | bytes 7864320 | tf_op jit(solution)/shard_map/while/body/eval_jaxpr/reduce_scatter | solution.py:60
  1916.3 219.6 %reduce-scatter.21.cloned.1.call-start = ((), (), s32[]{:S(2)}) async-start(), calls=%async_computation.15 | async-start | bytes 2654208 | tf_op jit(solution)/shard_map/reduce_scatter | solution.py:40
  1918.3 283.1 %reduce-scatter.23.cloned.1.call-start = ((), (), s32[]{:S(2)}) async-start(), calls=%async_computation.16 | async-start | bytes 7077888 | tf_op jit(solution)/shard_map/reduce_scatter | solution.py:41
  1919.0 347.9 %reduce-scatter.25.cloned.1.call-start = ((), (), s32[]{:S(2)}) async-start(), calls=%async_computation.17 | async-start | bytes 7077888 | tf_op jit(solution)/shard_map/reduce_scatter | solution.py:42
  1919.6 412.7 %reduce-scatter.27.cloned.1.call-start = ((), (), s32[]{:S(2)}) async-start(), calls=%async_computation.18 | async-start | bytes 7077888 | tf_op jit(solution)/shard_map/reduce_scatter | solution.py:43
  (206 other events, 5365.3 us)
Sparse Core Ops, SparseCore 0:
  15.6 66.1 all-gather.15
  159.6 24.0 all-gather.23
  189.6 110.7 reduce-scatter.30
  302.5 63.9 all-gather.29
  368.4 30.8 all-gather.31
  401.2 32.1 all-gather.27
  435.4 63.4 all-gather.25
  500.8 30.8 all-gather.33
  552.5 110.7 reduce-scatter.32
  668.6 63.9 all-gather.35
  734.7 109.4 reduce-scatter.36
  846.3 111.2 reduce-scatter.34
  966.3 63.9 all-gather.15
  1107.9 24.0 all-gather.23
  1137.9 110.7 reduce-scatter.30
  1250.9 63.9 all-gather.29
  1316.8 30.8 all-gather.31
  1349.4 32.1 all-gather.27
  1383.7 63.4 all-gather.25
  1448.9 30.8 all-gather.33
  1500.7 110.7 reduce-scatter.32
  1616.8 63.9 all-gather.35
  1683.1 109.4 reduce-scatter.36
  1794.7 111.2 reduce-scatter.34
  (6 shorter events, 140.5 us)
Sparse Core Ops, SparseCore 1:
  1915.9 35.5 reduce-scatter.28
  1955.2 42.2 reduce-scatter.14
  2001.3 42.2 reduce-scatter.16
  2047.5 42.1 reduce-scatter.18
  2093.6 42.2 reduce-scatter.20
  2139.8 61.6 reduce-scatter.22
  2205.3 61.6 reduce-scatter.24
  2270.7 61.6 reduce-scatter.26
where the time goes:
time: 2340 us
  waiting for transfers between devices  1720 us (74%)
  matrix products  332 us (14%)
  other arithmetic  120 us (5%)
  local copies, waits for them, and re-layouts  78.7 us (3%)
  blocking collectives  60.7 us (3%)
    reduce_scatter x4, waiting for transfers between devices, collect_grads(): lax.psum_scatter(row_terms, 'tensor', scatter_dimension=0, tiled=True)  402 us
    all_gather x4, waiting for transfers between devices, spread_grads(): return lax.all_gather(row_block, 'tensor', axis=0, tiled=True)  233 us
    all_gather x4, waiting for transfers between devices, spread_rows(): return lax.all_gather(row_block, 'tensor', axis=0, tiled=True)  227 us
    reduce_scatter x4, waiting for transfers between devices, collect_rows(): lax.psum_scatter(row_terms, 'tensor', scatter_dimension=0, tiled=True)  214 us
    reduce_scatter x1, waiting for transfers between devices, reduce_weights(): lax.psum_scatter(grad_terms[5], 'dp', scatter_dimension=0, tiled=True)  65.6 us
    all_gather x2, waiting for transfers between devices, fetch_weights(): lax.all_gather(w_down, 'dp', axis=1, tiled=True)  65.5 us
    reduce_scatter x1, waiting for transfers between devices, reduce_weights(): lax.psum_scatter(grad_terms[7], 'dp', scatter_dimension=1, tiled=True)  65.4 us
    reduce_scatter x1, waiting for transfers between devices, reduce_weights(): lax.psum_scatter(grad_terms[6], 'dp', scatter_dimension=0, tiled=True)  65.4 us
  transfers between devices with their start and end apart: 38, of which 35 were waited for; matrix products, arithmetic and copies ran while one was open for 18% of the time, Pallas kernels for 0%

commit v1 on v0

v1 whole, which is shorter than its diff:
```python
import functools

import jax
import jax.numpy as jnp
from jax import lax
from jax.experimental import pallas as pl
from jax.experimental.pallas import tpu as pltpu
from jax.sharding import PartitionSpec as P

EPS = 1e-06
NEG_BIG = -1e30
F32 = jnp.float32
BF16 = jnp.bfloat16
FORGET_PAD = 16
UNIT_BLOCK = 256
VMEM_BYTES = 60 << 20


def row_scale(tokens):
    return lax.rsqrt(jnp.mean(tokens * tokens, axis=-1, keepdims=True) + EPS)


def norm_back(tokens, scaling, gain, grad_out):
    weighted = grad_out * gain
    cubed = scaling * scaling * scaling
    return scaling * weighted - tokens * cubed * jnp.mean(weighted * tokens, axis=-1, keepdims=True)


def dot_first(left, right):
    return lax.dot_general(left, right, (((0,), (0,)), ((), ())), preferred_element_type=F32)

def nt(a, b):
    return lax.dot_general(a, b, (((1,), (1,)), ((), ())), preferred_element_type=F32)

def nn(a, b):
    return lax.dot_general(a, b, (((1,), (0,)), ((), ())), preferred_element_type=F32)

def pieces(x):
    top = x.astype(BF16).astype(F32)
    rest = x - top
    mid = rest.astype(BF16).astype(F32)
    return top, mid, rest - mid

def side(lane, base, values, rest):
    for n, value in enumerate(values):
        rest = jnp.where(lane == base + n, value, rest)
    return rest

def gate_column(c_ref, which, length, rows):
    col = c_ref[0, :, which : which + 1]
    pos = lax.broadcasted_iota(jnp.int32, (rows, 1), 0)
    return jnp.where(pos < length, -col, NEG_BIG)

def attn_fwd_kernel(len_ref, q_ref, k_ref, v_ref, c_ref, o_ref, l_ref, *, blk):
    rows, wide = q_ref.shape
    hd = wide // 2
    length = len_ref[0]
    lane = lax.broadcasted_iota(jnp.int32, (rows, wide), 1)
    lane_b = lax.broadcasted_iota(jnp.int32, (blk, wide), 1)
    q = q_ref[...].astype(F32) * 0.125
    k = k_ref[...].astype(F32)
    v = v_ref[...].astype(F32)
    heads = []
    for h in range(2):
        inside = (lane < hd) if h == 0 else (lane >= hd)
        base = hd if h == 0 else 0
        bias = jnp.broadcast_to(gate_column(c_ref, h, length, rows), (rows, wide))
        kx = jnp.where(inside, k, side(lane, base, pieces(bias), 0.0)).astype(BF16)
        qx = jnp.where(inside, q, side(lane, base, (1.0, 1.0, 1.0), 0.0)).astype(BF16)
        vx = jnp.where(inside, v, 1.0).astype(BF16)
        heads.append((qx, kx, vx))
    tri = lax.broadcasted_iota(jnp.int32, (blk, blk), 1) <= lax.broadcasted_iota(jnp.int32, (blk, blk), 0)
    for i in range(rows // blk):
        lo, hi = i * blk, (i + 1) * blk
        got = []
        for h in range(2):
            qx, kx, vx = heads[h]
            s_d = jnp.where(tri, nt(qx[lo:hi], kx[lo:hi]), NEG_BIG)
            m = jnp.max(s_d, axis=1, keepdims=True)
            if i:
                s_o = nt(qx[lo:hi], kx[:lo])
                m = jnp.maximum(m, jnp.max(s_o, axis=1, keepdims=True))
            r = nn(jnp.exp(s_d - m).astype(BF16), vx[lo:hi])
            if i:
                r = r + nn(jnp.exp(s_o - m).astype(BF16), vx[:lo])
            total = pltpu.roll(r, hd, 1)
            got.append((r / total, m + jnp.log(total)))
        pos = lo + lax.broadcasted_iota(jnp.int32, (blk, wide), 0)
        o = jnp.where(lane_b < hd, got[0][0], got[1][0])
        o_ref[lo:hi, :] = jnp.where(pos < length, o, 0.0).astype(BF16)
        l_ref[lo:hi, :] = jnp.where(lane_b < hd, got[0][1], got[1][1])

def attn_fwd(length, q, k, v, c, blk=256):
    rows, cols = q.shape
    pairs = cols // 128
    spec = pl.BlockSpec((rows, 128), lambda p: (0, p))
    return pl.pallas_call(
        functools.partial(attn_fwd_kernel, blk=blk),
        grid=(pairs,),
        in_specs=[pl.BlockSpec(memory_space=pltpu.SMEM), spec, spec, spec,
                  pl.BlockSpec((1, rows, 2), lambda p: (p, 0, 0))],
        out_specs=[spec, spec],
        out_shape=[jax.ShapeDtypeStruct((rows, cols), BF16), jax.ShapeDtypeStruct((rows, cols), F32)],
        compiler_params=pltpu.CompilerParams(vmem_limit_bytes=VMEM_BYTES),
        cost_estimate=pl.CostEstimate(flops=rows*rows*128*4*pairs*2, bytes_accessed=rows*cols*12, transcendentals=rows*rows*pairs),
    )(length, q, k, v, c)

def attn_bwd_kernel(len_ref, q_ref, k_ref, v_ref, c_ref, l_ref, o_ref, g_ref, dq_ref, dk_ref, dv_ref, dc_ref, acc_k, acc_v, *, blk):
    rows, wide = q_ref.shape
    hd = wide // 2
    length = len_ref[0]
    lane = lax.broadcasted_iota(jnp.int32, (rows, wide), 1)
    q = q_ref[...].astype(F32) * 0.125
    k = k_ref[...].astype(F32)
    v = v_ref[...].astype(F32)
    g = g_ref[...].astype(F32)
    go = g * o_ref[...].astype(F32)
    tri = lax.broadcasted_iota(jnp.int32, (blk, blk), 0) <= lax.broadcasted_iota(jnp.int32, (blk, blk), 1)
    res = []
    for h in range(2):
        inside = (lane < hd) if h == 0 else (lane >= hd)
        base = hd if h == 0 else 0
        bias = jnp.broadcast_to(gate_column(c_ref, h, length, rows), (rows, wide))
        logt = l_ref[...]
        logt = jnp.where(inside, pltpu.roll(logt, hd, 1), logt)
        other = pltpu.roll(l_ref[...], hd, 1)
        logt = jnp.where(inside, l_ref[...], other)
        dot_o = jnp.broadcast_to(jnp.sum(jnp.where(inside, go, 0.0), axis=1, keepdims=True), (rows, wide))
        kx = jnp.where(inside, k, side(lane, base, pieces(bias) + (1.0, 1.0, 1.0), 0.0)).astype(BF16)
        qx = jnp.where(inside, q, side(lane, base, (1.0, 1.0, 1.0) + pieces(-logt), 0.0)).astype(BF16)
        vx = jnp.where(inside, v, side(lane, base, (1.0, 1.0, 1.0), 0.0)).astype(BF16)
        gx = jnp.where(inside, g, side(lane, base, pieces(-dot_o), 0.0)).astype(BF16)
        kt = kx.T
        dq_parts = []
        for i in range(rows // blk):
            lo, hi = i * blk, (i + 1) * blk
            dqt = None
            for a, b, diag in ((lo, hi, True),) + (((0, lo, False),) if i else ()):
                s = nt(kx[a:b], qx[lo:hi])
                if diag:
                    s = jnp.where(tri, s, NEG_BIG)
                p = jnp.exp(s)
                ds = (p * nt(vx[a:b], gx[lo:hi])).astype(BF16)
                dv = nn(p.astype(BF16), g_ref[lo:hi, :])
                dk = nn(ds, qx[lo:hi])
                t = nn(kt[:, a:b], ds)
                dqt = t if dqt is None else dqt + t
                if diag:
                    acc_v[a:b, :] = dv
                    acc_k[a:b, :] = dk
                else:
                    acc_v[a:b, :] += dv
                    acc_k[a:b, :] += dk
            dq_parts.append(dqt.T)
        dq = jnp.concatenate(dq_parts, axis=0)
        dk = acc_k[...]
        res.append((dq, dk, acc_v[...], dq - pltpu.roll(dk, 3, 1)))
    first = lane < hd
    dq_ref[...] = jnp.where(first, res[0][0] * 0.125, res[1][0] * 0.125).astype(BF16)
    dk_ref[...] = jnp.where(first, res[0][1], res[1][1]).astype(BF16)
    dv_ref[...] = jnp.where(first, res[0][2], res[1][2]).astype(BF16)
    dc_ref[...] = jnp.where(first, res[1][3], res[0][3])

def attn_bwd(length, q, k, v, c, l, o, g, blk=256):
    rows, cols = q.shape
    pairs = cols // 128
    spec = pl.BlockSpec((rows, 128), lambda p: (0, p))
    low = jax.ShapeDtypeStruct((rows, cols), BF16)
    dq, dk, dv, dc = pl.pallas_call(
        functools.partial(attn_bwd_kernel, blk=blk),
        grid=(pairs,),
        in_specs=[pl.BlockSpec(memory_space=pltpu.SMEM), spec, spec, spec,
                  pl.BlockSpec((1, rows, 2), lambda p: (p, 0, 0)), spec, spec, spec],
        out_specs=[spec]*4,
        out_shape=[low, low, low, jax.ShapeDtypeStruct((rows, cols), F32)],
        scratch_shapes=[pltpu.VMEM((rows, 128), F32)]*2,
        compiler_params=pltpu.CompilerParams(vmem_limit_bytes=VMEM_BYTES),
        cost_estimate=pl.CostEstimate(flops=rows*rows*128*10*pairs*2, bytes_accessed=rows*cols*24, transcendentals=rows*rows*pairs),
    )(length, q, k, v, c, l, o, g)
    d3 = dc.reshape(rows, pairs, 128)
    grad_cumul = jnp.stack([d3[:, :, 67], d3[:, :, 3]], axis=2).reshape(rows, 2 * pairs)
    return dq, dk, dv, grad_cumul


def whole(array):
    return pl.BlockSpec(array.shape, lambda *_: (0,) * array.ndim, pipeline_mode=pl.Buffered(1))


def cost(flops, arrays, more=0):
    size = sum(a.size * a.dtype.itemsize for a in arrays)
    return pl.CostEstimate(flops=flops, bytes_accessed=size + more, transcendentals=0)


def joined(refs, lo=None, hi=None):
    if lo is None:
        return jnp.concatenate([r[...] for r in refs], axis=1)
    return jnp.concatenate([r[lo:hi, :] for r in refs], axis=1)


def project_kernel(x_ref, *refs, shard):
    w_refs, (q_ref, k_ref, v_ref, f_ref) = refs[:-4], refs[-4:]
    step = w_refs[0].shape[0] // 2
    x = x_ref[...]
    for kind, out in enumerate((q_ref, k_ref, v_ref)):
        rows = [joined(w_refs, t * step + kind * shard, t * step + (kind + 1) * shard) for t in range(2)]
        out[...] = nt(x, jnp.concatenate(rows, axis=0)).astype(BF16)
    rows = [joined(w_refs, t * step + 3 * shard, (t + 1) * step) for t in range(2)]
    f_ref[0] = nt(x, jnp.concatenate(rows, axis=0))


def project(x, weights, shard, few):
    rows = x.shape[0]
    step = weights[0].shape[0] // 2
    low = jax.ShapeDtypeStruct((rows, 4 * shard), BF16)
    spec = pl.BlockSpec((rows, 2 * shard), lambda i: (0, i))
    pad = step // 2 - 3 * shard
    q, k, v, f = pl.pallas_call(
        functools.partial(project_kernel, shard=shard),
        grid=(2,),
        in_specs=[whole(x)]
        + [pl.BlockSpec((step, w.shape[1]), lambda i: (i, 0)) for w in weights],
        out_specs=[spec, spec, spec, pl.BlockSpec((1, rows, 2 * pad), lambda i: (i, 0, 0))],
        out_shape=[low, low, low, jax.ShapeDtypeStruct((2, rows, 2 * pad), F32)],
        compiler_params=pltpu.CompilerParams(vmem_limit_bytes=VMEM_BYTES),
        cost_estimate=cost(2 * rows * x.shape[1] * 4 * step // 2, [x, *weights, low, low, low]),
        name="project",
    )(x, *weights)
    logits = f.reshape(2, rows, 2, pad)[..., :few].transpose(1, 0, 2, 3).reshape(rows, 4 * few)
    return q, k, v, logits


def combine_kernel(core_ref, left_ref, *refs):
    w_refs, (give_ref, keep_ref) = refs[:-2], refs[-2:]
    step = pl.program_id(0)
    wide = w_refs[0].shape[1]
    for out, cond in ((give_ref, step < 2), (keep_ref, step >= 2)):

        @pl.when(cond)
        def _():
            for n, w in enumerate(w_refs):
                out[:, n * wide : (n + 1) * wide] = nn(left_ref[...], w[...]).astype(out.dtype)


def combine(core, left, weights):
    rows = left.shape[0]
    wide = weights[0].shape[1] * len(weights)
    block = rows // 4

    def place(i, core_ref):
        mine = core_ref[0]
        return (jnp.where(i < 2, (1 - mine) * 2 + i, mine * 2 + i - 2), 0)

    outs = [
        jax.ShapeDtypeStruct((rows // 2, wide), BF16),
        jax.ShapeDtypeStruct((rows // 2, wide), F32),
    ]
    return pl.pallas_call(
        combine_kernel,
        grid_spec=pltpu.PrefetchScalarGridSpec(
            num_scalar_prefetch=1,
            grid=(4,),
            in_specs=[pl.BlockSpec((block, left.shape[1]), place)] + [whole(w) for w in weights],
            out_specs=[
                pl.BlockSpec((block, wide), lambda i, c: (jnp.minimum(i, 1), 0)),
                pl.BlockSpec((block, wide), lambda i, c: (jnp.maximum(i - 2, 0), 0)),
            ],
        ),
        out_shape=outs,
        compiler_params=pltpu.CompilerParams(vmem_limit_bytes=VMEM_BYTES),
        cost_estimate=cost(2 * rows * left.shape[1] * wide, [left, *weights, *outs]),
        name="combine",
    )(core.reshape(1), left, *weights)


def spread_kernel(len_ref, x_ref, *refs):
    w_refs, out_ref = refs[:-1], refs[-1]
    rows = x_ref.shape[0]
    got = nt(x_ref[...], joined(w_refs))
    pos = pl.program_id(0) * rows + lax.broadcasted_iota(jnp.int32, got.shape, 0)
    out_ref[...] = jnp.where(pos < len_ref[0], got, 0.0).astype(BF16)


def spread(length, x, weights):
    rows, wide = x.shape[0], weights[0].shape[0]
    block = rows // 4
    out = jax.ShapeDtypeStruct((rows, wide), BF16)
    return pl.pallas_call(
        spread_kernel,
        grid=(4,),
        in_specs=[
            pl.BlockSpec(memory_space=pltpu.SMEM),
            pl.BlockSpec((block, x.shape[1]), lambda i: (i, 0)),
        ]
        + [whole(w) for w in weights],
        out_specs=pl.BlockSpec((block, wide), lambda i: (i, 0)),
        out_shape=out,
        compiler_params=pltpu.CompilerParams(vmem_limit_bytes=VMEM_BYTES),
        cost_estimate=cost(2 * rows * x.shape[1] * wide, [x, *weights, out]),
        name="spread",
    )(length, x, *weights)


def inner_kernel(x_ref, *refs):
    w_refs, (gate_ref, up_ref, inner_ref) = refs[:-3], refs[-3:]
    both = nt(x_ref[...], joined(w_refs))
    gate, up = both[:, :UNIT_BLOCK], both[:, UNIT_BLOCK:]
    gate_ref[...] = gate
    up_ref[...] = up
    inner_ref[...] = (gate * jax.nn.sigmoid(gate) * up).astype(BF16)


def inner_units(x, weights):
    rows = x.shape[0]
    total = weights[0].shape[0] // 2
    spec = pl.BlockSpec((rows, UNIT_BLOCK), lambda i: (0, i))
    outs = [jax.ShapeDtypeStruct((rows, total), t) for t in (F32, F32, BF16)]
    return pl.pallas_call(
        inner_kernel,
        grid=(total // UNIT_BLOCK,),
        in_specs=[whole(x)]
        + [pl.BlockSpec((2 * UNIT_BLOCK, w.shape[1]), lambda i: (i, 0)) for w in weights],
        out_specs=[spec] * 3,
        out_shape=outs,
        compiler_params=pltpu.CompilerParams(vmem_limit_bytes=VMEM_BYTES),
        cost_estimate=cost(4 * rows * x.shape[1] * total, [x, *weights, *outs]),
        name="inner_units",
    )(x, *weights)


def inner_back_kernel(core_ref, x_ref, gate_ref, up_ref, *refs):
    pieces_here = (len(refs) - 4) // 2
    down_refs, two_refs = refs[:pieces_here], refs[pieces_here : 2 * pieces_here]
    pre_ref, give_ref, keep_ref, total = refs[2 * pieces_here :]
    step = pl.program_id(0)
    grad = nt(x_ref[...], joined(down_refs))
    gate, up = gate_ref[...], up_ref[...]
    sig = jax.nn.sigmoid(gate)
    grad_gate = (grad * up * (sig * (1.0 + gate * (1.0 - sig)))).astype(BF16)
    grad_up = (grad * (gate * sig)).astype(BF16)
    pre = jnp.concatenate([grad_gate, grad_up], axis=1)
    pre_ref[...] = pre
    wide = two_refs[0].shape[1]
    for n, w in enumerate(two_refs):
        cols = slice(n * wide, (n + 1) * wide)
        part = nn(pre, w[...])

        @pl.when(step == 0)
        def _():
            total[:, cols] = part

        @pl.when(step > 0)
        def _():
            total[:, cols] += part

    @pl.when(step == pl.num_programs(0) - 1)
    def _():
        half = give_ref.shape[0]
        core = core_ref[0]
        give_ref[...] = total[pl.ds(pl.multiple_of((1 - core) * half, half), half), :].astype(BF16)
        keep_ref[...] = total[pl.ds(pl.multiple_of(core * half, half), half), :]


def inner_back(core, x, gate, up, down, two):
    rows, cols = x.shape
    total = gate.shape[1]
    spec = pl.BlockSpec((rows, UNIT_BLOCK), lambda i: (0, i))
    outs = [
        jax.ShapeDtypeStruct((rows, 2 * total), BF16),
        jax.ShapeDtypeStruct((rows // 2, cols), BF16),
        jax.ShapeDtypeStruct((rows // 2, cols), F32),
    ]
    return pl.pallas_call(
        inner_back_kernel,
        grid=(total // UNIT_BLOCK,),
        in_specs=[pl.BlockSpec(memory_space=pltpu.SMEM), whole(x), spec, spec]
        + [pl.BlockSpec((UNIT_BLOCK, w.shape[1]), lambda i: (i, 0)) for w in down]
        + [pl.BlockSpec((2 * UNIT_BLOCK, w.shape[1]), lambda i: (i, 0)) for w in two],
        out_specs=[
            pl.BlockSpec((rows, 2 * UNIT_BLOCK), lambda i: (0, i)),
            whole(outs[1]),
            whole(outs[2]),
        ],
        out_shape=outs,
        scratch_shapes=[pltpu.VMEM((rows, cols), F32)],
        compiler_params=pltpu.CompilerParams(vmem_limit_bytes=VMEM_BYTES),
        cost_estimate=cost(6 * rows * cols * total, [x, gate, up, *down, *two, *outs]),
        name="inner_back",
    )(core.reshape(1), x, gate, up, *down, *two)


class Plan:
    def __init__(self, ways_dp, ways_tensor):
        self.ways_dp = ways_dp
        self.ways_tensor = ways_tensor
        self.chips = ways_dp // 2
        self.bits = self.chips.bit_length() - 1
        assert self.chips == 1 << self.bits and ways_tensor == 4
        dp = lax.axis_index("dp")
        self.chip = dp // 2
        self.core = dp % 2
        self.place = lax.axis_index("tensor")
        self.core_perm = [(i, i ^ 1) for i in range(ways_dp)]

    def swap_core(self, array):
        return lax.ppermute(array, "dp", self.core_perm)

    def swap_chip(self, array, bit):
        perm = [(i, i ^ (2 << bit)) for i in range(self.ways_dp)]
        return lax.ppermute(array, "dp", perm)

    def route(self, turn):
        pairs = []
        for chip in range(self.chips):
            for core in range(2):
                for z in range(4):
                    micro = (z + turn) % 2
                    source = (2 * chip + core) * 4 + z
                    target = (2 * chip + z // 2) * 4 + 2 * micro + core
                    pairs.append((source, target))
        return pairs

    def by_chip(self, array):
        lead = array.shape[:-1]
        wide = array.shape[-1] // self.chips
        parts = [
            lax.dynamic_slice_in_dim(array, (self.chip ^ r) * wide, wide, axis=-1)
            for r in range(self.chips)
        ]
        return jnp.concatenate(parts, axis=-1).reshape(*lead, -1)

    def to_chip(self, array):
        got = []
        for turn in range(2):
            micro = (self.place + turn) % 2
            part = lax.dynamic_index_in_dim(array, micro, 0, keepdims=False)
            got.append(lax.ppermute(self.by_chip(part), ("dp", "tensor"), self.route(turn)))
        first = self.place // 2 == 0
        return jnp.concatenate(
            [jnp.where(first, got[0], got[1]), jnp.where(first, got[1], got[0])], axis=0
        )

    def from_chip(self, array):
        rows = array.shape[0] // 2
        got = []
        for turn in range(2):
            block = (self.place // 2 + turn) % 2
            part = lax.dynamic_slice_in_dim(array, block * rows, rows, axis=0)
            back = [(b, a) for a, b in self.route(turn)]
            got.append(lax.ppermute(self.by_chip(part), ("dp", "tensor"), back))
        first = self.place % 2 == 0
        return jnp.stack([jnp.where(first, got[0], got[1]), jnp.where(first, got[1], got[0])])

    def both_rows(self, half):
        other = self.swap_core(half)
        first = self.core == 0
        return jnp.concatenate(
            [jnp.where(first, half, other), jnp.where(first, other, half)], axis=0
        )

    def sum_rows(self, give, keep):
        return keep + self.swap_core(give).astype(F32)

    def line_gather(self, shard):
        mine = lax.dynamic_index_in_dim(shard, self.core, 0, keepdims=False)
        theirs = lax.dynamic_index_in_dim(shard, 1 - self.core, 0, keepdims=False)
        other = self.swap_core(theirs)
        first = self.core == 0
        pair = jnp.concatenate(
            [jnp.where(first, mine, other), jnp.where(first, other, mine)], axis=1
        )
        return lax.all_gather(pair, "tensor", axis=0, tiled=True)

    def chip_gather(self, own):
        half = own.shape[0] // 2
        if self.bits == 2:
            by_x = self.swap_chip(own, 0)
            by_y = self.swap_chip(own, 1)
            far_top = self.swap_chip(by_x[:half], 1)
            far_low = self.swap_chip(by_y[half:], 0)
            return [own, by_x, by_y, jnp.concatenate([far_top, far_low], axis=0)]
        parts = [own]
        for bit in range(self.bits):
            parts = parts + [self.swap_chip(p, bit) for p in parts]
        return [jnp.concatenate(parts, axis=1)]

    def reduce_weight(self, left, right):
        wide = right.shape[1] // self.chips
        rows = left.shape[1]
        half = rows // 2

        def term(r, lo=0, hi=rows):
            return dot_first(left[:, lo:hi], right[:, r * wide : (r + 1) * wide])

        if self.bits == 2:
            far_top = self.swap_chip(term(3, 0, half).astype(BF16), 1)
            far_low = self.swap_chip(term(3, half, rows).astype(BF16), 0)
            send_x = jnp.concatenate(
                [
                    (term(1, 0, half) + far_top.astype(F32)).astype(BF16),
                    term(1, half, rows).astype(BF16),
                ],
                axis=0,
            )
            send_y = jnp.concatenate(
                [
                    term(2, 0, half).astype(BF16),
                    (term(2, half, rows) + far_low.astype(F32)).astype(BF16),
                ],
                axis=0,
            )
            by_x = self.swap_chip(send_x, 0)
            by_y = self.swap_chip(send_y, 1)
            total = term(0) + by_x.astype(F32) + by_y.astype(F32)
        else:
            parts = [term(r) for r in range(self.chips)]
            for bit in reversed(range(self.bits)):
                keep, give = parts[: 1 << bit], parts[1 << bit :]
                parts = [
                    k + self.swap_chip(g.astype(BF16), bit).astype(F32) for k, g in zip(keep, give)
                ]
            total = parts[0]
        pair = lax.psum_scatter(total.astype(BF16), "tensor", scatter_dimension=0, tiled=True)
        narrow = wide // 2
        mine = lax.dynamic_slice_in_dim(pair, self.core * narrow, narrow, axis=1)
        theirs = lax.dynamic_slice_in_dim(pair, (1 - self.core) * narrow, narrow, axis=1)
        other = self.swap_core(theirs)
        first = self.core == 0
        return jnp.stack([jnp.where(first, mine, other), jnp.where(first, other, mine)]).astype(F32)

    def sum_all(self, vector):
        vector = vector + self.swap_core(vector)
        for bit in range(self.bits):
            vector = vector + self.swap_chip(vector, bit)
        for bit in range(2):
            perm = [(z, z ^ (1 << bit)) for z in range(4)]
            vector = vector + lax.ppermute(vector, "tensor", perm)
        return vector


def split_columns(matrix):
    return matrix.T.reshape(2, matrix.shape[1] // 2, matrix.shape[0])


def split_rows(matrix):
    return matrix.reshape(2, matrix.shape[0] // 2, matrix.shape[1])


def body(
    inputs,
    seq_lengths,
    seq_assign,
    norm1_gain,
    w_query,
    w_key,
    w_value,
    w_forget,
    forget_bias,
    w_out,
    norm2_gain,
    w_gate,
    w_up,
    w_down,
    out_grad,
):
    plan = Plan(lax.axis_size("dp"), lax.axis_size("tensor"))
    core, place = plan.core, plan.place
    part_rows = inputs.shape[1]
    seq_rows = part_rows * 4
    half_rows = seq_rows // 2
    heads_shard = w_forget.shape[1] // 2
    heads_here = heads_shard * 4
    shard_cols = w_query.shape[1] // 2
    blocks = w_gate.shape[1] // 2 // UNIT_BLOCK

    def by_block(matrix):
        return split_columns(matrix).reshape(2, blocks, 1, UNIT_BLOCK, matrix.shape[0])

    forget_part = jnp.pad(
        split_columns(w_forget), ((0, 0), (0, FORGET_PAD - heads_shard), (0, 0))
    )
    line_one = plan.line_gather(
        jnp.concatenate(
            [split_columns(w_query), split_columns(w_key), split_columns(w_value), forget_part],
            axis=1,
        )
    )
    full_one = plan.chip_gather(line_one)
    rows_in = plan.to_chip(inputs).astype(F32)
    two_part = jnp.concatenate([by_block(w_gate), by_block(w_up)], axis=2)
    line_mid = plan.line_gather(
        jnp.concatenate(
            [split_rows(w_out), two_part.reshape(2, -1, two_part.shape[-1])], axis=1
        )
    )
    line_mid = line_mid.reshape(4, -1, line_mid.shape[-1])
    full_out = plan.chip_gather(line_mid[:, :shard_cols].reshape(4 * shard_cols, -1))
    full_two = plan.chip_gather(
        line_mid[:, shard_cols:].reshape(-1, line_mid.shape[-1])
    )
    full_down = plan.chip_gather(plan.line_gather(split_rows(w_down)))
    cotangent = plan.to_chip(out_grad).astype(F32)

    other_assign = plan.swap_core(seq_assign)
    assign_both = jnp.where(
        core == 0,
        jnp.concatenate([seq_assign, other_assign], axis=1),
        jnp.concatenate([other_assign, seq_assign], axis=1),
    ).reshape(4)
    seq_id = jnp.sum(jnp.where(jnp.arange(4) == place, assign_both, 0))
    length = jnp.sum(jnp.where(jnp.arange(seq_lengths.shape[0]) == seq_id, seq_lengths, 0))
    count = length.reshape(1)
    valid_here = (core * half_rows + jnp.arange(half_rows) < length).astype(F32)[:, None]

    gain_one = plan.by_chip(norm1_gain)
    gain_two = plan.by_chip(norm2_gain)
    bias_here = lax.dynamic_index_in_dim(
        forget_bias.reshape(4, 2, heads_shard), core, 1, keepdims=False
    ).reshape(-1)

    scale_one = row_scale(rows_in)
    normed_one = plan.both_rows((rows_in * scale_one * gain_one).astype(BF16))
    queries, key_rows, value_rows, logits = project(normed_one, full_one, shard_cols, heads_shard)
    forget_logit = logits + bias_here
    cumul_gate = jnp.cumsum(jax.nn.log_sigmoid(forget_logit), axis=0)
    gate_pairs = cumul_gate.reshape(seq_rows, heads_here // 2, 2).transpose(1, 0, 2)
    mixed_low, log_total = attn_fwd(count, queries, key_rows, value_rows, gate_pairs)
    hidden_in = rows_in + plan.sum_rows(*combine(core, mixed_low, full_out))

    scale_two = row_scale(hidden_in)
    normed_two = plan.both_rows((hidden_in * scale_two * gain_two).astype(BF16))
    gate_pre, up_pre, inner_low = inner_units(normed_two, full_two)
    grad_ffn = plan.both_rows((valid_here * cotangent).astype(BF16))
    down_shard = plan.reduce_weight(inner_low, grad_ffn)
    ffn_rows = plan.sum_rows(*combine(core, inner_low, full_down))
    outputs = plan.from_chip((valid_here * (hidden_in + ffn_rows)).astype(BF16))

    grad_pre, give_two, keep_two = inner_back(
        core, grad_ffn, gate_pre, up_pre, full_down, full_two
    )
    two_shard = plan.reduce_weight(grad_pre, normed_two)
    grad_normed_two = plan.sum_rows(give_two, keep_two)
    gain_two_term = jnp.sum(grad_normed_two * hidden_in * scale_two, axis=0)
    grad_hidden = valid_here * cotangent + norm_back(
        hidden_in, scale_two, gain_two, grad_normed_two
    )

    grad_attn = plan.both_rows(grad_hidden.astype(BF16))
    out_shard = plan.reduce_weight(mixed_low, grad_attn)
    grad_mixed = spread(count, grad_attn, full_out)
    query_low, key_low, value_low, grad_cumul = attn_bwd(
        count, queries, key_rows, value_rows, gate_pairs, log_total, mixed_low, grad_mixed
    )
    grad_logf = jnp.flip(jnp.cumsum(jnp.flip(grad_cumul, 0), axis=0), 0)
    grad_logit = grad_logf * jax.nn.sigmoid(-forget_logit)
    bias_term = jnp.sum(grad_logit, axis=0)
    grad_one = jnp.concatenate(
        [
            query_low.reshape(seq_rows, 4, shard_cols),
            key_low.reshape(seq_rows, 4, shard_cols),
            value_low.reshape(seq_rows, 4, shard_cols),
            jnp.pad(
                grad_logit.astype(BF16).reshape(seq_rows, 4, heads_shard),
                ((0, 0), (0, 0), (0, FORGET_PAD - heads_shard)),
            ),
        ],
        axis=2,
    ).reshape(seq_rows, -1)
    one_shard = plan.reduce_weight(grad_one, normed_one)
    grad_normed_one = plan.sum_rows(*combine(core, grad_one, full_one))
    gain_one_term = jnp.sum(grad_normed_one * rows_in * scale_one, axis=0)
    input_grad = plan.from_chip(
        (grad_hidden + norm_back(rows_in, scale_one, gain_one, grad_normed_one)).astype(BF16)
    )

    bias_full = jnp.where(
        (jnp.arange(2) == core)[None, :, None], bias_term.reshape(4, 1, heads_shard), 0.0
    ).reshape(-1)
    wide = norm1_gain.shape[0]
    small = plan.sum_all(
        jnp.concatenate([plan.by_chip(gain_one_term), plan.by_chip(gain_two_term), bias_full])
    )

    two_shard = two_shard.reshape(2, blocks, 2, UNIT_BLOCK, -1)

    def columns(shard):
        return shard.reshape(-1, shard.shape[-1]).T

    def rows(shard):
        return shard.reshape(-1, shard.shape[-1])

    return (
        outputs,
        input_grad,
        small[:wide],
        columns(one_shard[:, :shard_cols]),
        columns(one_shard[:, shard_cols : 2 * shard_cols]),
        columns(one_shard[:, 2 * shard_cols : 3 * shard_cols]),
        columns(one_shard[:, 3 * shard_cols : 3 * shard_cols + heads_shard]),
        small[2 * wide :],
        rows(out_shard),
        small[wide : 2 * wide],
        columns(two_shard[:, :, 0]),
        columns(two_shard[:, :, 1]),
        rows(down_shard),
    )


def solution(mesh):
    return jax.shard_map(
        body,
        mesh=mesh,
        in_specs=(
            P(None, ("dp", "tensor"), None),
            P(),
            P(None, "dp"),
            P(),
            P("dp", "tensor"),
            P("dp", "tensor"),
            P("dp", "tensor"),
            P("dp", "tensor"),
            P(),
            P("tensor", "dp"),
            P(),
            P("dp", "tensor"),
            P("dp", "tensor"),
            P("tensor", "dp"),
            P(None, ("dp", "tensor"), None),
        ),
        out_specs=(
            P(None, ("dp", "tensor"), None),
            P(None, ("dp", "tensor"), None),
            P(),
            P("dp", "tensor"),
            P("dp", "tensor"),
            P("dp", "tensor"),
            P("dp", "tensor"),
            P(),
            P("tensor", "dp"),
            P(),
            P("dp", "tensor"),
            P("dp", "tensor"),
            P("tensor", "dp"),
        ),
        check_vma=False,
    )
```

time: 2340 us -> 984 us (0.42)
  waiting for transfers between devices: 1720 us -> 464 us
  matrix products: 332 us -> 79.9 us
  Pallas kernels: 0 us -> 198 us
  starting transfers between devices: 2.35 us -> 63.5 us
  blocking collectives: 60.7 us -> 0 us
  other arithmetic: 120 us -> 72.2 us
    reduce_scatter x15 -> x4, waiting for transfers between devices: 978 us -> 0.03 us  [reduce_weight(): lax.psum_scatter(total.astype(BF16), 'tensor', scatter_dimension=0, tiled...]
    all_gather x22 -> x3, waiting for transfers between devices: 734 us -> 43 us  [line_gather(): return lax.all_gather(pair, 'tensor', axis=0, tiled=True)]
    ppermute x0 -> x61, waiting for transfers between devices: none -> 421 us  [the longest x34 318 us: swap_chip(): return lax.ppermute(array, 'dp', perm)]
    dot_general x72 -> x28, matrix products: 332 us -> 79.9 us  [dot_first(): lax.dot_general(left, right, (((0,), (0,)), ((), ())), preferred_element_...]
    pallas_call x0 -> x9, Pallas kernels: none -> 198 us  [the longest x1 57.8 us: inner_back(): pl.pallas_call(inner_back_kernel, grid=(total // UNIT_BLOCK,), in_specs=[...]
    ppermute x0 -> x61, starting transfers between devices: none -> 62.8 us  [the longest x34 38 us: swap_chip(): return lax.ppermute(array, 'dp', perm)]
    reduce_sum x13 -> x5, other arithmetic: 61 us -> 8.79 us  [the longest x1 3.23 us: body(): gain_one_term = jnp.sum(grad_normed_one * rows_in * scale_one, axis=0)]
    while x388 -> x0, local copies, waits for them, and re-layouts: 47.9 us -> none
  transfers between devices with their start and end apart: 38 -> 68, of which waited for: 35 -> 30; matrix products, arithmetic and copies ran while one was open for 18% -> 20% of each run, Pallas kernels for 0% -> 12%
where the time goes in v1:
time: 984 us; the launch traced here: 969 us
  waiting for transfers between devices  464 us (47%)
  Pallas kernels  198 us (20%)
  matrix products  79.9 us (8%)
  local copies, waits for them, and re-layouts  75.3 us (8%)
  other arithmetic  72.2 us (7%)
  starting transfers between devices  63.5 us (6%)
  between operations  16.1 us (2%)
    ppermute x34, waiting for transfers between devices, swap_chip(): return lax.ppermute(array, 'dp', perm)  318 us
    dot_general x28, matrix products, dot_first(): lax.dot_general(left, right, (((0,), (0,)), ((), ())), preferred_element_...  79.9 us
    ppermute x2, waiting for transfers between devices, sum_all(): vector = vector + lax.ppermute(vector, 'tensor', perm)  61.9 us
    pallas_call x1, Pallas kernels, inner_back(): pl.pallas_call(inner_back_kernel, grid=(total // UNIT_BLOCK,), in_specs=[...  57.8 us
    all_gather x3, waiting for transfers between devices, line_gather(): return lax.all_gather(pair, 'tensor', axis=0, tiled=True)  43 us
    pallas_call x3, Pallas kernels, combine(): pl.pallas_call(combine_kernel, grid_spec=pltpu.PrefetchScalarGridSpec(num...  38.8 us
    ppermute x34, starting transfers between devices, swap_chip(): return lax.ppermute(array, 'dp', perm)  38 us
    ppermute x4, waiting for transfers between devices, to_chip(): lax.ppermute(self.by_chip(part), ('dp', 'tensor'), self.route(turn))  36.8 us
  transfers between devices with their start and end apart: 68, of which 30 were waited for; matrix products, arithmetic and copies ran while one was open for 20% of the time, Pallas kernels for 12%

profile of v1, /device:TPU:0, one launch (start us, length us, event | category | flops | bytes accessed | tf_op | source)
XLA Modules:
  0.0 969.2 jit_solution(7769596849490085256)
XLA Ops:
  29.8 36.8 %collective-permute-done.2 = bf16[256,1536]{1,0:T(8,128)(2,1)S(1)} collective-permute-done((bf16[256,1536]{1,0:T(8,128)(2,1)S(1)}, bf16[256,1536]{1,0:T(8,128)(2,1)S(1)}, u32[]{:S(2)}, u32[]{:S(2)}) %collective-permute-start.2) | collective-permute-done | bytes 786464 | tf_op jit(solution)/shard_map/ppermute | solution.py:436
  67.8 19.9 %all-gather.4.cloned.1.call-done.refs_0_ = bf16[2368,384]{1,0:T(8,128)(2,1)} async-done(((bf16[592,384]{1,0:T(8,128)(2,1)}), bf16[2368,384]{1,0:T(8,128)(2,1)}) %all-gather.4.cloned.1.call-update) | async-done | bytes 1818640 | tf_op jit(solution)/shard_map/all_gather | solution.py:471
  101.1 7.4 collective-permute-start.28
  112.5 14.4 %collective-permute-done.5.refs_1_ = bf16[2368,384]{1,0:T(8,128)(2,1)} collective-permute-done((bf16[2368,384]{1,0:T(8,128)(2,1)}, bf16[2368,384]{1,0:T(8,128)(2,1)}, u32[]{:S(2)}, u32[]{:S(2)}) %collective-permute-start.5) | collective-permute-done | bytes 1818656 | tf_op jit(solution)/shard_map/ppermute | solution.py:409
  136.8 11.9 %collective-permute-done.7 = bf16[1184,384]{1,0:T(8,128)(2,1)S(1)} collective-permute-done((bf16[1184,384]{1,0:T(8,128)(2,1)S(1)}, bf16[1184,384]{1,0:T(8,128)(2,1)S(1)}, u32[]{:S(2)}, u32[]{:S(2)}) %collective-permute-start.7) | collective-permute-done | bytes 909344 | tf_op jit(solution)/shard_map/ppermute | solution.py:409
  153.0 16.2 %project.1 = (bf16[1024,768]{1,0:T(8,128)(2,1)}, bf16[1024,768]{1,0:T(8,128)(2,1)}, bf16[1024,768]{1,0:T(8,128)(2,1)}, f32[2,1024,32]{2,1,0:T(8,128)}) custom-call(bf16[1024,1536]{1,0:T(8,128)(2,1)} %pad_maximum_fusion.x_ref, bf16[2368,384]{1,0:T(8,128)(2,1)} %all-gather.4.cloned.1.call-done.refs_0_, bf16[2368,384]{1,0:T(8,128)(2,1)} %collective-permute-done.5.refs_1_, ...), custom_call_target="tpu_custom_call" | custom-call | flops 7449083904 | bytes 15138816 | tf_op jit(solution)/shard_map/project/pallas_call | solution.py:217
  170.7 23.1 %all-gather.6.cloned.1.call-done = bf16[4864,384]{1,0:T(8,128)(2,1)} async-done(((bf16[1216,384]{1,0:T(8,128)(2,1)}), bf16[4864,384]{1,0:T(8,128)(2,1)}) %all-gather.6.cloned.1.call-update) | async-done | bytes 3735568 | tf_op jit(solution)/shard_map/all_gather | solution.py:471
  213.1 25.0 %shard_map.246 = (bf16[1024,768]{1,0:T(8,128)(2,1)}, f32[1024,768]{1,0:T(8,128)}) custom-call(s32[1]{0:T(128)} %bitcast.9.len_ref, bf16[1024,768]{1,0:T(8,128)(2,1)} %get-tuple-element.35.q_ref, bf16[1024,768]{1,0:T(8,128)(2,1)} %get-tuple-element.36.k_ref, bf16[1024,768]{1,0:T(8,128)(2,1)} %get-tuple-element.37.v_ref, f32[6,1024,2]{2,1,0:T(8,128)} %bitcast.169), custom_call_target="tpu_custom_call" | custom-call | flops 6442450944 | bytes 9437184 | tf_op jit(solution)/shard_map/pallas_call | solution.py:97
  239.0 7.9 combine.3
  263.3 92.6 %collective-permute-done.21.refs_1_ = bf16[2048,384]{1,0:T(8,128)(2,1)} collective-permute-done((bf16[2048,384]{1,0:T(8,128)(2,1)}, bf16[2048,384]{1,0:T(8,128)(2,1)}, u32[]{:S(2)}, u32[]{:S(2)}) %collective-permute-start.21) | collective-permute-done | bytes 1572896 | tf_op jit(solution)/shard_map/ppermute | solution.py:409
  385.1 25.9 %collective-permute-done.18 = bf16[2048,384]{1,0:T(8,128)(2,1)S(1)} collective-permute-done((bf16[2048,384]{1,0:T(8,128)(2,1)S(1)}, bf16[2048,384]{1,0:T(8,128)(2,1)S(1)}, u32[]{:S(2)}, u32[]{:S(2)}) %collective-permute-start.18) | collective-permute-done | bytes 1572896 | tf_op jit(solution)/shard_map/ppermute | solution.py:409
  413.8 20.5 %inner_units.1 = (f32[1024,2048]{1,0:T(8,128)}, f32[1024,2048]{1,0:T(8,128)}, bf16[1024,2048]{1,0:T(8,128)(2,1)}) custom-call(bf16[1024,1536]{1,0:T(8,128)(2,1)} %pad_maximum_fusion.1.x_ref, bf16[4096,384]{1,0:T(8,128)(2,1)} %bitcast.31.refs_0_.refs_4_, bf16[4096,384]{1,0:T(8,128)(2,1)} %collective-permute-done.16.refs_1_.refs_5_, ...), custom_call_target="tpu_custom_call" | custom-call | flops 12884901888 | bytes 36700160 | tf_op jit(solution)/shard_map/inner_units/pallas_call | solution.py:317
  440.5 57.8 %inner_back.1 = (bf16[1024,4096]{1,0:T(8,128)(2,1)}, bf16[512,1536]{1,0:T(8,128)(2,1)}, f32[512,1536]{1,0:T(8,128)}) custom-call(s32[1]{0:T(128)} %bitcast.8.core_ref, bf16[1024,1536]{1,0:T(8,128)(2,1)} %pad_maximum_fusion.2.x_ref, f32[1024,2048]{1,0:T(8,128)} %get-tuple-element.45.gate_ref, f32[1024,2048]{1,0:T(8,128)} %get-tuple-element.46.up_ref, ...), custom_call_target="tpu_custom_call" | custom-call | flops 19327352832 | bytes 51904512 | tf_op jit(solution)/shard_map/inner_back/pallas_call | solution.py:372
  510.2 14.4 %combine.4 = (bf16[512,1536]{1,0:T(8,128)(2,1)}, f32[512,1536]{1,0:T(8,128)}) custom-call(s32[1]{0:T(128)} %bitcast.8.core_ref, bf16[1024,2048]{1,0:T(8,128)(2,1)} %get-tuple-element.42.left_ref, bf16[2048,384]{1,0:T(8,128)(2,1)} %all-gather.8.cloned.1.call-done.refs_0_, bf16[2048,384]{1,0:T(8,128)(2,1)} %collective-permute-done.21.refs_1_, ...), custom_call_target="tpu_custom_call" | custom-call | flops 6442450944 | bytes 15204352 | tf_op jit(solution)/shard_map/combine/pallas_call | solution.py:257
  564.3 61.3 %collective-permute-done.46 = bf16[384,384]{1,0:T(8,128)(2,1)S(1)} collective-permute-done((bf16[384,384]{1,0:T(8,128)(2,1)S(1)}, bf16[384,384]{1,0:T(8,128)(2,1)S(1)}, u32[]{:S(2)}, u32[]{:S(2)}) %collective-permute-start.46) | collective-permute-done | bytes 294944 | tf_op jit(solution)/shard_map/ppermute | solution.py:409
  640.6 7.5 collective-permute-done.47
  672.6 32.8 %shard_map.247 = (bf16[1024,768]{1,0:T(8,128)(2,1)}, bf16[1024,768]{1,0:T(8,128)(2,1)}, bf16[1024,768]{1,0:T(8,128)(2,1)}, f32[1024,768]{1,0:T(8,128)}) custom-call(s32[1]{0:T(128)} %bitcast.9.len_ref, bf16[1024,768]{1,0:T(8,128)(2,1)} %get-tuple-element.35.q_ref, bf16[1024,768]{1,0:T(8,128)(2,1)} %get-tuple-element.36.k_ref, ...), custom_call_target="tpu_custom_call" | custom-call | flops 16106127360 | bytes 18874368 | tf_op jit(solution)/shard_map/pallas_call | solution.py:169
  728.6 13.1 %collective-permute-done.41 = bf16[1184,384]{1,0:T(8,128)(2,1)S(1)} collective-permute-done((bf16[1184,384]{1,0:T(8,128)(2,1)S(1)}, bf16[1184,384]{1,0:T(8,128)(2,1)S(1)}, u32[]{:S(2)}, u32[]{:S(2)}) %collective-permute-start.41) | collective-permute-done | bytes 909344 | tf_op jit(solution)/shard_map/ppermute | solution.py:409
  757.4 25.7 %collective-permute-done.42 = bf16[2368,384]{1,0:T(8,128)(2,1)S(1)} collective-permute-done((bf16[2368,384]{1,0:T(8,128)(2,1)S(1)}, bf16[2368,384]{1,0:T(8,128)(2,1)S(1)}, u32[]{:S(2)}, u32[]{:S(2)}) %collective-permute-start.42) | collective-permute-done | bytes 1818656 | tf_op jit(solution)/shard_map/ppermute | solution.py:409
  796.7 7.4 copy.150.left_ref
  804.1 16.6 %combine.5 = (bf16[512,1536]{1,0:T(8,128)(2,1)}, f32[512,1536]{1,0:T(8,128)}) custom-call(s32[1]{0:T(128)} %bitcast.8.core_ref, bf16[1024,2368]{1,0:T(8,128)(2,1)} %copy.150.left_ref, bf16[2368,384]{1,0:T(8,128)(2,1)} %all-gather.4.cloned.1.call-done.refs_0_, bf16[2368,384]{1,0:T(8,128)(2,1)} %collective-permute-done.5.refs_1_, ...), custom_call_target="tpu_custom_call" | custom-call | flops 7449083904 | bytes 16842752 | tf_op jit(solution)/shard_map/combine/pallas_call | solution.py:257
  820.9 31.1 %collective-permute-done.54 = bf16[4096,384]{1,0:T(8,128)(2,1)} collective-permute-done((bf16[4096,384]{1,0:T(8,128)(2,1)}, bf16[4096,384]{1,0:T(8,128)(2,1)}, u32[]{:S(2)}, u32[]{:S(2)}) %collective-permute-start.54) | collective-permute-done | bytes 3145760 | tf_op jit(solution)/shard_map/ppermute | solution.py:409
  852.0 11.8 %add_convert_fusion = bf16[4096,384]{1,0:T(8,128)(2,1)} fusion(bf16[4096,384]{1,0:T(8,128)(2,1)} %collective-permute-done.54, bf16[4096,384]{1,0:T(8,128)(2,1)} %collective-permute-done.52, bf16[1024,4096]{1,0:T(8,128)(2,1)} %get-tuple-element.56, bf16[512,1536]{1,0:T(8,128)(2,1)S(1)} %copy-done.31, bf16[512,1536]{1,0:T(8,128)(2,1)} %copy-done.32), kind=kOutput, calls=%fused_computation.8 | convolution fusion | flops 3230662656 | bytes 20971520 | tf_op jit(solution)/shard_map/dot_general | solution.py:30
  884.6 58.3 %collective-permute-done.40 = f32[3096]{0:T(1024)S(1)} collective-permute-done((f32[3096]{0:T(1024)S(1)}, f32[3096]{0:T(1024)S(1)}, u32[]{:S(2)}, u32[]{:S(2)}) %collective-permute-start.40) | collective-permute-done | bytes 12416 | tf_op jit(solution)/shard_map/ppermute | solution.py:536
  (499 shorter events, 313.6 us)
Async XLA Ops:
  7.2 80.5 %all-gather.4.cloned.1.call-start = ((), (), s32[]{:S(2)}) async-start(), calls=%async_computation.4 | async-start | bytes 2273280 | tf_op jit(solution)/shard_map/all_gather | solution.py:471
  14.1 179.8 %all-gather.6.cloned.1.call-start = ((), (), s32[]{:S(2)}) async-start(), calls=%async_computation.5 | async-start | bytes 4669440 | tf_op jit(solution)/shard_map/all_gather | solution.py:471
  22.9 231.7 %all-gather.8.cloned.1.call-start = ((), (), s32[]{:S(2)}) async-start(), calls=%async_computation.6 | async-start | bytes 1966080 | tf_op jit(solution)/shard_map/all_gather | solution.py:471
  101.1 152.0 %collective-permute-start.28 = (bf16[256,1536]{1,0:T(8,128)(2,1)}, bf16[256,1536]{1,0:T(8,128)(2,1)}, u32[]{:S(2)}, u32[]{:S(2)}) collective-permute-start(bf16[256,1536]{1,0:T(8,128)(2,1)} %pad_maximum_fusion.20), channel_id=1, source_target_pairs={{0,0},{1,2},{2,4},{3,6},{4,1},{5,3},{6,5},{7,7},{8,8},{9,10},{10,1... | collective-permute-start | bytes 2359304 | tf_op jit(solution)/shard_map/ppermute | solution.py:436
  111.2 141.9 %collective-permute-start.29 = (bf16[256,1536]{1,0:T(8,128)(2,1)}, bf16[256,1536]{1,0:T(8,128)(2,1)}, u32[]{:S(2)}, u32[]{:S(2)}) collective-permute-start(bf16[256,1536]{1,0:T(8,128)(2,1)} %pad_maximum_fusion.21), channel_id=1, source_target_pairs={{0,2},{1,0},{2,6},{3,4},{4,3},{5,1},{6,7},{7,5},{8,10},{9,8},{10,1... | collective-permute-start | bytes 2359304 | tf_op jit(solution)/shard_map/ppermute | solution.py:436
  112.2 830.7 %reduce-scatter.7.cloned.1.call-start = ((), (), s32[]{:S(2)}) async-start(), calls=%async_computation.8 | async-start | bytes 737280 | tf_op jit(solution)/shard_map/reduce_scatter | solution.py:522
  251.5 110.9 %collective-permute-start.16 = (bf16[4096,384]{1,0:T(8,128)(2,1)}, bf16[4096,384]{1,0:T(8,128)(2,1)}, u32[]{:S(2)}, u32[]{:S(2)}) collective-permute-start(bf16[4096,384]{1,0:T(8,128)(2,1)} %bitcast.31.refs_0_.refs_4_), channel_id=1, source_target_pairs={{0,8},{4,12},{8,0},{12,4},{16,24},{20,28},{24,16},{28,20},{1,9},{5... | collective-permute-start | bytes 9437192 | tf_op jit(solution)/shard_map/ppermute | solution.py:409
  252.0 114.0 %collective-permute-start.17 = (bf16[4096,384]{1,0:T(8,128)(2,1)}, bf16[4096,384]{1,0:T(8,128)(2,1)}, u32[]{:S(2)}, u32[]{:S(2)}) collective-permute-start(bf16[4096,384]{1,0:T(8,128)(2,1)} %bitcast.31.refs_0_.refs_4_), channel_id=1, source_target_pairs={{0,16},{4,20},{8,24},{12,28},{16,0},{20,4},{24,8},{28,12},{1,17},{... | collective-permute-start | bytes 9437192 | tf_op jit(solution)/shard_map/ppermute | solution.py:409
  254.7 101.3 %collective-permute-start.21 = (bf16[2048,384]{1,0:T(8,128)(2,1)}, bf16[2048,384]{1,0:T(8,128)(2,1)}, u32[]{:S(2)}, u32[]{:S(2)}) collective-permute-start(bf16[2048,384]{1,0:T(8,128)(2,1)} %all-gather.8.cloned.1.call-done.refs_0_), channel_id=1, source_target_pairs={{0,8},{4,12},{8,0},{12,4},{16,24},{20,28},{24,16},{28,20},{1,9},{5... | collective-permute-start | bytes 4718600 | tf_op jit(solution)/shard_map/ppermute | solution.py:409
  257.2 101.9 %collective-permute-start.30 = (bf16[512,1536]{1,0:T(8,128)(2,1)}, bf16[512,1536]{1,0:T(8,128)(2,1)}, u32[]{:S(2)}, u32[]{:S(2)}) collective-permute-start(bf16[512,1536]{1,0:T(8,128)(2,1)} %fusion.26), channel_id=1, source_target_pairs={{0,4},{4,0},{8,12},{12,8},{16,20},{20,16},{24,28},{28,24},{1,5},{5... | collective-permute-start | bytes 4718600 | tf_op jit(solution)/shard_map/ppermute | solution.py:405
  257.2 100.0 %collective-permute-start.22 = (bf16[2048,384]{1,0:T(8,128)(2,1)}, bf16[2048,384]{1,0:T(8,128)(2,1)}, u32[]{:S(2)}, u32[]{:S(2)}) collective-permute-start(bf16[2048,384]{1,0:T(8,128)(2,1)} %all-gather.8.cloned.1.call-done.refs_0_), channel_id=1, source_target_pairs={{0,16},{4,20},{8,24},{12,28},{16,0},{20,4},{24,8},{28,12},{1,17},{... | collective-permute-start | bytes 4718600 | tf_op jit(solution)/shard_map/ppermute | solution.py:409
  548.8 87.5 %collective-permute-start.51 = (bf16[2048,384]{1,0:T(8,128)(2,1)S(1)}, bf16[2048,384]{1,0:T(8,128)(2,1)S(1)}, u32[]{:S(2)}, u32[]{:S(2)}) collective-permute-start(bf16[2048,384]{1,0:T(8,128)(2,1)S(1)} %copy-done.69), channel_id=1, source_target_pairs={{0,16},{4,20},{8,24},{12,28},{16,0},{20,4},{24,8},{28,12},{1,17},{... | collective-permute-start | bytes 4718600 | tf_op jit(solution)/shard_map/ppermute | solution.py:409
  549.9 198.1 %collective-permute-start.53 = (bf16[2048,384]{1,0:T(8,128)(2,1)}, bf16[2048,384]{1,0:T(8,128)(2,1)}, u32[]{:S(2)}, u32[]{:S(2)}) collective-permute-start(bf16[2048,384]{1,0:T(8,128)(2,1)} %fusion.42), channel_id=1, source_target_pairs={{0,8},{4,12},{8,0},{12,4},{16,24},{20,28},{24,16},{28,20},{1,9},{5... | collective-permute-start | bytes 4718600 | tf_op jit(solution)/shard_map/ppermute | solution.py:409
  554.6 102.1 %collective-permute-start.57 = (bf16[2048,384]{1,0:T(8,128)(2,1)}, bf16[2048,384]{1,0:T(8,128)(2,1)}, u32[]{:S(2)}, u32[]{:S(2)}) collective-permute-start(bf16[2048,384]{1,0:T(8,128)(2,1)} %pad_maximum_fusion.12), channel_id=1, source_target_pairs={{0,8},{4,12},{8,0},{12,4},{16,24},{20,28},{24,16},{28,20},{1,9},{5... | collective-permute-start | bytes 4718600 | tf_op jit(solution)/shard_map/ppermute | solution.py:409
  559.5 97.2 %collective-permute-start.59 = (bf16[2048,384]{1,0:T(8,128)(2,1)}, bf16[2048,384]{1,0:T(8,128)(2,1)}, u32[]{:S(2)}, u32[]{:S(2)}) collective-permute-start(bf16[2048,384]{1,0:T(8,128)(2,1)} %pad_maximum_fusion.13), channel_id=1, source_target_pairs={{0,16},{4,20},{8,24},{12,28},{16,0},{20,4},{24,8},{28,12},{1,17},{... | collective-permute-start | bytes 4718600 | tf_op jit(solution)/shard_map/ppermute | solution.py:409
  561.5 64.1 %collective-permute-start.46 = (bf16[384,384]{1,0:T(8,128)(2,1)S(1)}, bf16[384,384]{1,0:T(8,128)(2,1)S(1)}, u32[]{:S(2)}, u32[]{:S(2)}) collective-permute-start(bf16[384,384]{1,0:T(8,128)(2,1)S(1)} %convolution_convert_fusion.7), channel_id=1, source_target_pairs={{0,16},{4,20},{8,24},{12,28},{16,0},{20,4},{24,8},{28,12},{1,17},{... | collective-permute-start | bytes 884744 | tf_op jit(solution)/shard_map/ppermute | solution.py:409
  651.9 295.4 %reduce-scatter.11.cloned.1.call-start = ((), (), s32[]{:S(2)}) async-start(), calls=%async_computation.10 | async-start | bytes 1966080 | tf_op jit(solution)/shard_map/reduce_scatter | solution.py:522
  656.1 164.8 %collective-permute-start.52 = (bf16[4096,384]{1,0:T(8,128)(2,1)}, bf16[4096,384]{1,0:T(8,128)(2,1)}, u32[]{:S(2)}, u32[]{:S(2)}) collective-permute-start(bf16[4096,384]{1,0:T(8,128)(2,1)} %pad_maximum_fusion.4), channel_id=1, source_target_pairs={{0,8},{4,12},{8,0},{12,4},{16,24},{20,28},{24,16},{28,20},{1,9},{5... | collective-permute-start | bytes 9437192 | tf_op jit(solution)/shard_map/ppermute | solution.py:409
  663.6 287.1 %reduce-scatter.5.cloned.1.call-start = ((), (), s32[]{:S(2)}) async-start(), calls=%async_computation.7 | async-start | bytes 2273280 | tf_op jit(solution)/shard_map/reduce_scatter | solution.py:522
  754.7 97.4 %collective-permute-start.54 = (bf16[4096,384]{1,0:T(8,128)(2,1)}, bf16[4096,384]{1,0:T(8,128)(2,1)}, u32[]{:S(2)}, u32[]{:S(2)}) collective-permute-start(bf16[4096,384]{1,0:T(8,128)(2,1)} %pad_maximum_fusion.5), channel_id=1, source_target_pairs={{0,16},{4,20},{8,24},{12,28},{16,0},{20,4},{24,8},{28,12},{1,17},{... | collective-permute-start | bytes 9437192 | tf_op jit(solution)/shard_map/ppermute | solution.py:409
  793.8 160.5 %reduce-scatter.9.cloned.1.call-start = ((), (), s32[]{:S(2)}) async-start(), calls=%async_computation.9 | async-start | bytes 3932160 | tf_op jit(solution)/shard_map/reduce_scatter | solution.py:522
  877.9 70.9 %collective-permute-start.35 = (bf16[256,1536]{1,0:T(8,128)(2,1)S(1)}, bf16[256,1536]{1,0:T(8,128)(2,1)S(1)}, u32[]{:S(2)}, u32[]{:S(2)}) collective-permute-start(bf16[256,1536]{1,0:T(8,128)(2,1)S(1)} %pad_maximum_fusion.23), channel_id=1, source_target_pairs={{2,0},{0,1},{6,2},{4,3},{3,4},{1,5},{7,6},{5,7},{10,8},{8,9},{14,1... | collective-permute-start | bytes 2359304 | tf_op jit(solution)/shard_map/ppermute | solution.py:449
  883.6 59.3 %collective-permute-start.40 = (f32[3096]{0:T(1024)S(1)}, f32[3096]{0:T(1024)S(1)}, u32[]{:S(2)}, u32[]{:S(2)}) collective-permute-start(f32[3096]{0:T(1024)S(1)} %add.400), channel_id=1, source_target_pairs={{0,2},{1,3},{2,0},{3,1},{4,6},{5,7},{6,4},{7,5},{8,10},{9,11},{10,... | collective-permute-start | bytes 37160 | tf_op jit(solution)/shard_map/ppermute | solution.py:536
  883.7 65.2 %collective-permute-start.34 = (bf16[256,1536]{1,0:T(8,128)(2,1)S(1)}, bf16[256,1536]{1,0:T(8,128)(2,1)S(1)}, u32[]{:S(2)}, u32[]{:S(2)}) collective-permute-start(bf16[256,1536]{1,0:T(8,128)(2,1)S(1)} %pad_maximum_fusion.22), channel_id=1, source_target_pairs={{0,0},{2,1},{4,2},{6,3},{1,4},{3,5},{5,6},{7,7},{8,8},{10,9},{12,1... | collective-permute-start | bytes 2359304 | tf_op jit(solution)/shard_map/ppermute | solution.py:449
  (122 other events, 1711.2 us)
Sparse Core Ops, SparseCore 0:
  14.2 73.4 all-gather.3
  89.2 104.5 all-gather.5
  195.4 35.4 all-gather.7
  652.1 19.6 reduce-scatter.6
  673.9 33.6 reduce-scatter.10
  793.9 38.1 reduce-scatter.4
  864.0 83.2 reduce-scatter.8

commit v2 on v1

--- a/solution.py
+++ b/solution.py
@@ -483,44 +483,11 @@
             parts = parts + [self.swap_chip(p, bit) for p in parts]
         return [jnp.concatenate(parts, axis=1)]
 
-    def reduce_weight(self, left, right):
-        wide = right.shape[1] // self.chips
-        rows = left.shape[1]
-        half = rows // 2
-
-        def term(r, lo=0, hi=rows):
-            return dot_first(left[:, lo:hi], right[:, r * wide : (r + 1) * wide])
-
-        if self.bits == 2:
-            far_top = self.swap_chip(term(3, 0, half).astype(BF16), 1)
-            far_low = self.swap_chip(term(3, half, rows).astype(BF16), 0)
-            send_x = jnp.concatenate(
-                [
-                    (term(1, 0, half) + far_top.astype(F32)).astype(BF16),
-                    term(1, half, rows).astype(BF16),
-                ],
-                axis=0,
-            )
-            send_y = jnp.concatenate(
-                [
-                    term(2, 0, half).astype(BF16),
-                    (term(2, half, rows) + far_low.astype(F32)).astype(BF16),
-                ],
-                axis=0,
-            )
-            by_x = self.swap_chip(send_x, 0)
-            by_y = self.swap_chip(send_y, 1)
-            total = term(0) + by_x.astype(F32) + by_y.astype(F32)
-        else:
-            parts = [term(r) for r in range(self.chips)]
-            for bit in reversed(range(self.bits)):
-                keep, give = parts[: 1 << bit], parts[1 << bit :]
-                parts = [
-                    k + self.swap_chip(g.astype(BF16), bit).astype(F32) for k, g in zip(keep, give)
-                ]
-            total = parts[0]
-        pair = lax.psum_scatter(total.astype(BF16), "tensor", scatter_dimension=0, tiled=True)
-        narrow = wide // 2
+    def scatter(self, total):
+        return lax.psum_scatter(total, "tensor", scatter_dimension=0, tiled=True)
+
+    def share(self, pair):
+        narrow = pair.shape[1] // 2
         mine = lax.dynamic_slice_in_dim(pair, self.core * narrow, narrow, axis=1)
         theirs = lax.dynamic_slice_in_dim(pair, (1 - self.core) * narrow, narrow, axis=1)
         other = self.swap_core(theirs)
@@ -535,6 +502,79 @@
             perm = [(z, z ^ (1 << bit)) for z in range(4)]
             vector = vector + lax.ppermute(vector, "tensor", perm)
         return vector
+
+
+class Reduction:
+    def __init__(self, plan, left, right):
+        self.plan, self.left, self.right = plan, left, right
+        self.wide = right.shape[1] // plan.chips
+        self.rows = left.shape[1]
+        self.half = self.rows // 2
+        self.staged = plan.bits == 2
+        if self.staged:
+            self.first = [
+                self.top(3).astype(BF16),
+                self.low(3).astype(BF16),
+                self.low(1).astype(BF16),
+                self.top(2).astype(BF16),
+            ]
+        else:
+            self.first = [self.term(r, 0, self.rows) for r in range(plan.chips)]
+
+    def term(self, r, lo, hi):
+        return dot_first(self.left[:, lo:hi], self.right[:, r * self.wide : (r + 1) * self.wide])
+
+    def top(self, r):
+        return self.term(r, 0, self.half)
+
+    def low(self, r):
+        return self.term(r, self.half, self.rows)
+
+    def send_first(self):
+        if self.staged:
+            a, b, c, d = self.first
+            swap = self.plan.swap_chip
+            self.got = [swap(a, 1), swap(b, 0), swap(c, 0), swap(d, 1)]
+        else:
+            self.got = list(self.first)
+
+    def prepare_second(self):
+        if self.staged:
+            far_top, far_low = self.got[:2]
+            self.second = [
+                (self.top(1) + far_top.astype(F32)).astype(BF16),
+                (self.low(2) + far_low.astype(F32)).astype(BF16),
+            ]
+        else:
+            self.second = []
+
+    def send_second(self):
+        if self.staged:
+            self.last = [self.plan.swap_chip(self.second[0], 0), self.plan.swap_chip(self.second[1], 1)]
+        else:
+            self.last = []
+
+    def finish(self):
+        if self.staged:
+            x_top, y_low = self.last
+            x_low, y_top = self.got[2:]
+            top = self.top(0) + x_top.astype(F32) + y_top.astype(F32)
+            low = self.low(0) + x_low.astype(F32) + y_low.astype(F32)
+            total = jnp.concatenate([top, low], axis=0)
+        else:
+            parts = self.got
+            for bit in reversed(range(self.plan.bits)):
+                keep, give = parts[: 1 << bit], parts[1 << bit :]
+                parts = [
+                    k + self.plan.swap_chip(g.astype(BF16), bit).astype(F32)
+                    for k, g in zip(keep, give)
+                ]
+            total = parts[0]
+        return total.astype(BF16)
+
+
+def together(*groups):
+    return lax.optimization_barrier(groups)
 
 
 def split_columns(matrix):
@@ -584,21 +624,18 @@
             axis=1,
         )
     )
+    inputs, line_one = together(inputs, line_one)
     full_one = plan.chip_gather(line_one)
     rows_in = plan.to_chip(inputs).astype(F32)
-    two_part = jnp.concatenate([by_block(w_gate), by_block(w_up)], axis=2)
     line_mid = plan.line_gather(
-        jnp.concatenate(
-            [split_rows(w_out), two_part.reshape(2, -1, two_part.shape[-1])], axis=1
-        )
+        jnp.concatenate([split_rows(w_out), split_rows(w_down)], axis=1)
     )
     line_mid = line_mid.reshape(4, -1, line_mid.shape[-1])
     full_out = plan.chip_gather(line_mid[:, :shard_cols].reshape(4 * shard_cols, -1))
-    full_two = plan.chip_gather(
-        line_mid[:, shard_cols:].reshape(-1, line_mid.shape[-1])
-    )
-    full_down = plan.chip_gather(plan.line_gather(split_rows(w_down)))
-    cotangent = plan.to_chip(out_grad).astype(F32)
+    full_down = plan.chip_gather(line_mid[:, shard_cols:].reshape(-1, line_mid.shape[-1]))
+    two_part = jnp.concatenate([by_block(w_gate), by_block(w_up)], axis=2)
+    line_two = plan.line_gather(two_part.reshape(2, -1, two_part.shape[-1]))
+    full_two = plan.chip_gather(line_two)
 
     other_assign = plan.swap_core(seq_assign)
     assign_both = jnp.where(
@@ -624,20 +661,30 @@
     cumul_gate = jnp.cumsum(jax.nn.log_sigmoid(forget_logit), axis=0)
     gate_pairs = cumul_gate.reshape(seq_rows, heads_here // 2, 2).transpose(1, 0, 2)
     mixed_low, log_total = attn_fwd(count, queries, key_rows, value_rows, gate_pairs)
+    mixed_low, out_grad = together(mixed_low, out_grad)
+    cotangent = plan.to_chip(out_grad).astype(F32)
     hidden_in = rows_in + plan.sum_rows(*combine(core, mixed_low, full_out))
 
     scale_two = row_scale(hidden_in)
     normed_two = plan.both_rows((hidden_in * scale_two * gain_two).astype(BF16))
     gate_pre, up_pre, inner_low = inner_units(normed_two, full_two)
     grad_ffn = plan.both_rows((valid_here * cotangent).astype(BF16))
-    down_shard = plan.reduce_weight(inner_low, grad_ffn)
+    down_sum = Reduction(plan, inner_low, grad_ffn)
+    down_sum.first, gate_pre = together(down_sum.first, gate_pre)
+    down_sum.send_first()
     ffn_rows = plan.sum_rows(*combine(core, inner_low, full_down))
     outputs = plan.from_chip((valid_here * (hidden_in + ffn_rows)).astype(BF16))
 
     grad_pre, give_two, keep_two = inner_back(
         core, grad_ffn, gate_pre, up_pre, full_down, full_two
     )
-    two_shard = plan.reduce_weight(grad_pre, normed_two)
+    down_sum.got, grad_pre = together(down_sum.got, grad_pre)
+    down_sum.prepare_second()
+    two_sum = Reduction(plan, grad_pre, normed_two)
+    two_sum.first, down_sum.second = together(two_sum.first, down_sum.second)
+    down_sum.send_second()
+    two_sum.send_first()
+    down_pair = plan.scatter(down_sum.finish())
     grad_normed_two = plan.sum_rows(give_two, keep_two)
     gain_two_term = jnp.sum(grad_normed_two * hidden_in * scale_two, axis=0)
     grad_hidden = valid_here * cotangent + norm_back(
@@ -645,11 +692,16 @@
     )
 
     grad_attn = plan.both_rows(grad_hidden.astype(BF16))
-    out_shard = plan.reduce_weight(mixed_low, grad_attn)
     grad_mixed = spread(count, grad_attn, full_out)
     query_low, key_low, value_low, grad_cumul = attn_bwd(
         count, queries, key_rows, value_rows, gate_pairs, log_total, mixed_low, grad_mixed
     )
+    two_sum.got, query_low = together(two_sum.got, query_low)
+    two_sum.prepare_second()
+    two_sum.second, query_low, key_low, value_low, grad_cumul = together(
+        two_sum.second, query_low, key_low, value_low, grad_cumul
+    )
+    two_sum.send_second()
     grad_logf = jnp.flip(jnp.cumsum(jnp.flip(grad_cumul, 0), axis=0), 0)
     grad_logit = grad_logf * jax.nn.sigmoid(-forget_logit)
     bias_term = jnp.sum(grad_logit, axis=0)
@@ -665,7 +717,30 @@
         ],
         axis=2,
     ).reshape(seq_rows, -1)
-    one_shard = plan.reduce_weight(grad_one, normed_one)
+    grad_attn, grad_one = together(grad_attn, grad_one)
+    out_sum = Reduction(plan, mixed_low, grad_attn)
+    one_sum = Reduction(plan, grad_one, normed_one)
+    out_sum.first, one_sum.first, two_sum.last = together(
+        out_sum.first, one_sum.first, two_sum.last
+    )
+    out_sum.send_first()
+    one_sum.send_first()
+    two_total, down_pair = together(two_sum.finish(), down_pair)
+    two_pair = plan.scatter(two_total)
+    out_sum.got, one_sum.got, two_total, grad_one = together(
+        out_sum.got, one_sum.got, two_total, grad_one
+    )
+    out_sum.prepare_second()
+    one_sum.prepare_second()
+    out_sum.second, one_sum.second = together(out_sum.second, one_sum.second)
+    out_sum.send_second()
+    one_sum.send_second()
+    out_total, two_pair = together(out_sum.finish(), two_pair)
+    out_pair = plan.scatter(out_total)
+    one_total, out_pair = together(one_sum.finish(), out_pair)
+    one_pair = plan.scatter(one_total)
+    down_shard, two_shard = plan.share(down_pair), plan.share(two_pair)
+    out_shard, one_shard = plan.share(out_pair), plan.share(one_pair)
     grad_normed_one = plan.sum_rows(*combine(core, grad_one, full_one))
     gain_one_term = jnp.sum(grad_normed_one * rows_in * scale_one, axis=0)
     input_grad = plan.from_chip(

time: 984 us -> 1020 us (1.037)
  starting transfers between devices: 63.5 us -> 131 us
  waiting for transfers between devices: 464 us -> 401 us
  matrix products: 79.9 us -> 99.3 us
  other arithmetic: 72.2 us -> 85.3 us
    ppermute x34 -> x42, waiting for transfers between devices: 318 us -> 269 us  [swap_chip(): return lax.ppermute(array, 'dp', perm)]
    ppermute x17, starting transfers between devices: 7.53 us -> 47.2 us  [swap_core(): return lax.ppermute(array, 'dp', self.core_perm)]
    ppermute x2, waiting for transfers between devices: 61.9 us -> 39.3 us  [sum_all(): vector = vector + lax.ppermute(vector, 'tensor', perm)]
    dot_general x28 -> x32, matrix products: 79.9 us -> 99.3 us  [dot_first(): lax.dot_general(left, right, (((0,), (0,)), ((), ())), preferred_element_...]
    ppermute x2, starting transfers between devices: 0.01 us -> 18 us  [sum_all(): vector = vector + lax.ppermute(vector, 'tensor', perm)]
    reduce_scatter x4, waiting for transfers between devices: 0.03 us -> 16.1 us  [scatter(): return lax.psum_scatter(total, 'tensor', scatter_dimension=0, tiled=True)]
    optimization_barrier x0 -> x4, local copies, waits for them, and re-layouts: none -> 13.1 us  [together(): return lax.optimization_barrier(groups)]
    ppermute x34 -> x42, starting transfers between devices: 38 us -> 47 us  [swap_chip(): return lax.ppermute(array, 'dp', perm)]
  transfers between devices with their start and end apart: 68 -> 76, of which waited for: 30 -> 28; matrix products, arithmetic and copies ran while one was open for 20% -> 23% of each run, Pallas kernels for 12% -> 18%
where the time goes in v2:
time: 1020 us; the launch traced here: 1010 us
  waiting for transfers between devices  401 us (39%)
  Pallas kernels  199 us (20%)
  starting transfers between devices  131 us (13%)
  matrix products  99.3 us (10%)
  other arithmetic  85.3 us (8%)
  local copies, waits for them, and re-layouts  77.3 us (8%)
  between operations  16 us (2%)
    ppermute x42, waiting for transfers between devices, swap_chip(): return lax.ppermute(array, 'dp', perm)  269 us
    dot_general x32, matrix products, dot_first(): lax.dot_general(left, right, (((0,), (0,)), ((), ())), preferred_element_...  99.3 us
    pallas_call x1, Pallas kernels, inner_back(): pl.pallas_call(inner_back_kernel, grid=(total // UNIT_BLOCK,), in_specs=[...  57.8 us
    ppermute x17, starting transfers between devices, swap_core(): return lax.ppermute(array, 'dp', self.core_perm)  47.2 us
    ppermute x42, starting transfers between devices, swap_chip(): return lax.ppermute(array, 'dp', perm)  47 us
    all_gather x3, waiting for transfers between devices, line_gather(): return lax.all_gather(pair, 'tensor', axis=0, tiled=True)  40.4 us
    ppermute x2, waiting for transfers between devices, sum_all(): vector = vector + lax.ppermute(vector, 'tensor', perm)  39.3 us
    pallas_call x3, Pallas kernels, combine(): pl.pallas_call(combine_kernel, grid_spec=pltpu.PrefetchScalarGridSpec(num...  38.7 us
  transfers between devices with their start and end apart: 76, of which 28 were waited for; matrix products, arithmetic and copies ran while one was open for 23% of the time, Pallas kernels for 18%

profile of v2, /device:TPU:0, one launch (start us, length us, event | category | flops | bytes accessed | tf_op | source)
XLA Modules:
  0.0 1008.2 jit_solution(5809622439405244417)
XLA Ops:
  20.2 37.6 %all-gather.4.cloned.1.call-done.refs_0_ = bf16[2368,384]{1,0:T(8,128)(2,1)} async-done(((bf16[592,384]{1,0:T(8,128)(2,1)}), bf16[2368,384]{1,0:T(8,128)(2,1)}) %all-gather.4.cloned.1.call-update) | async-done | bytes 1818640 | tf_op jit(solution)/shard_map/all_gather | solution.py:471
  66.0 28.5 %collective-permute-done.3 = bf16[256,1536]{1,0:T(8,128)(2,1)S(1)} collective-permute-done((bf16[256,1536]{1,0:T(8,128)(2,1)S(1)}, bf16[256,1536]{1,0:T(8,128)(2,1)S(1)}, u32[]{:S(2)}, u32[]{:S(2)}) %collective-permute-start.3) | collective-permute-done | bytes 786464 | tf_op jit(solution)/shard_map/ppermute | solution.py:436
  96.2 32.3 %collective-permute-start.4 = (bf16[512,1536]{1,0:T(8,128)(2,1)S(1)}, bf16[512,1536]{1,0:T(8,128)(2,1)}, u32[]{:S(2)}, u32[]{:S(2)}) collective-permute-start(bf16[512,1536]{1,0:T(8,128)(2,1)S(1)} %fusion.4), channel_id=1, source_target_pairs={{0,4},{4,0},{8,12},{12,8},{16,20},{20,16},{24,28},{28,24},{1,5},{5... | collective-permute-start | bytes 4718600 | tf_op jit(solution)/shard_map/ppermute | solution.py:405
  138.0 10.8 %collective-permute-done.10.refs_1_ = bf16[768,384]{1,0:T(8,128)(2,1)} collective-permute-done((bf16[768,384]{1,0:T(8,128)(2,1)}, bf16[768,384]{1,0:T(8,128)(2,1)}, u32[]{:S(2)}, u32[]{:S(2)}) %collective-permute-start.10) | collective-permute-done | bytes 589856 | tf_op jit(solution)/shard_map/ppermute | solution.py:409
  183.0 40.9 %collective-permute-done.7 = bf16[1184,384]{1,0:T(8,128)(2,1)S(1)} collective-permute-done((bf16[1184,384]{1,0:T(8,128)(2,1)S(1)}, bf16[1184,384]{1,0:T(8,128)(2,1)S(1)}, u32[]{:S(2)}, u32[]{:S(2)}) %collective-permute-start.7) | collective-permute-done | bytes 909344 | tf_op jit(solution)/shard_map/ppermute | solution.py:409
  225.4 16.1 %project.1 = (bf16[1024,768]{1,0:T(8,128)(2,1)}, bf16[1024,768]{1,0:T(8,128)(2,1)}, bf16[1024,768]{1,0:T(8,128)(2,1)}, f32[2,1024,32]{2,1,0:T(8,128)}) custom-call(bf16[1024,1536]{1,0:T(8,128)(2,1)} %pad_maximum_fusion.x_ref, bf16[2368,384]{1,0:T(8,128)(2,1)} %all-gather.4.cloned.1.call-done.refs_0_, bf16[2368,384]{1,0:T(8,128)(2,1)} %collective-permute-done.5.refs_1_, ...), custom_call_target="tpu_custom_call" | custom-call | flops 7449083904 | bytes 15138816 | tf_op jit(solution)/shard_map/project/pallas_call | solution.py:217
  249.4 25.2 %shard_map.246 = (bf16[1024,768]{1,0:T(8,128)(2,1)}, f32[1024,768]{1,0:T(8,128)}) custom-call(s32[1]{0:T(128)} %bitcast.18.len_ref, bf16[1024,768]{1,0:T(8,128)(2,1)} %get-tuple-element.99.q_ref, bf16[1024,768]{1,0:T(8,128)(2,1)} %get-tuple-element.100.k_ref, bf16[1024,768]{1,0:T(8,128)(2,1)} %get-tuple-element.101.v_ref, f32[6,1024,2]{2,1,0:T(8,128)} %bitcast.168), custom_call_target="tpu_custom_call" | custom-call | flops 6442450944 | bytes 9437184 | tf_op jit(solution)/shard_map/pallas_call | solution.py:97
  324.3 57.9 %collective-permute-done.24 = bf16[1024,384]{1,0:T(8,128)(2,1)} collective-permute-done((bf16[1024,384]{1,0:T(8,128)(2,1)}, bf16[1024,384]{1,0:T(8,128)(2,1)}, u32[]{:S(2)}, u32[]{:S(2)}) %collective-permute-start.24) | collective-permute-done | bytes 786464 | tf_op jit(solution)/shard_map/ppermute | solution.py:409
  400.7 21.4 %collective-permute-done.19 = bf16[2048,384]{1,0:T(8,128)(2,1)S(1)} collective-permute-done((bf16[2048,384]{1,0:T(8,128)(2,1)S(1)}, bf16[2048,384]{1,0:T(8,128)(2,1)S(1)}, u32[]{:S(2)}, u32[]{:S(2)}) %collective-permute-start.19) | collective-permute-done | bytes 1572896 | tf_op jit(solution)/shard_map/ppermute | solution.py:409
  429.4 20.7 %inner_units.1 = (f32[1024,2048]{1,0:T(8,128)}, f32[1024,2048]{1,0:T(8,128)}, bf16[1024,2048]{1,0:T(8,128)(2,1)}) custom-call(bf16[1024,1536]{1,0:T(8,128)(2,1)} %pad_maximum_fusion.1.x_ref, bf16[4096,384]{1,0:T(8,128)(2,1)} %all-gather.8.cloned.1.call-done.refs_0_.refs_4_, bf16[4096,384]{1,0:T(8,128)(2,1)} %collective-permute-done.17.refs_1_.refs_5_, ...), custom_call_target="tpu_custom_call" | custom-call | flops 12884901888 | bytes 36700160 | tf_op jit(solution)/shard_map/inner_units/pallas_call | solution.py:317
  464.8 57.8 %inner_back.1 = (bf16[1024,4096]{1,0:T(8,128)(2,1)}, bf16[512,1536]{1,0:T(8,128)(2,1)}, f32[512,1536]{1,0:T(8,128)}) custom-call(s32[1]{0:T(128)} %bitcast.17.core_ref, bf16[1024,1536]{1,0:T(8,128)(2,1)} %pad_maximum_fusion.2.x_ref, f32[1024,2048]{1,0:T(8,128)} %get-tuple-element.112.gate_ref, f32[1024,2048]{1,0:T(8,128)} %get-tuple-element.113.up_ref, ...), custom_call_target="tpu_custom_call" | custom-call | flops 19327352832 | bytes 51904512 | tf_op jit(solution)/shard_map/inner_back/pallas_call | solution.py:372
  526.8 14.6 %combine.4 = (bf16[512,1536]{1,0:T(8,128)(2,1)}, f32[512,1536]{1,0:T(8,128)}) custom-call(s32[1]{0:T(128)} %bitcast.17.core_ref, bf16[1024,2048]{1,0:T(8,128)(2,1)} %get-tuple-element.107.left_ref, bf16[2048,384]{1,0:T(8,128)(2,1)} %bitcast.177, bf16[2048,384]{1,0:T(8,128)(2,1)} %collective-permute-done.21.refs_1_, ...), custom_call_target="tpu_custom_call" | custom-call | flops 6442450944 | bytes 15204352 | tf_op jit(solution)/shard_map/combine/pallas_call | solution.py:257
  591.9 25.3 %collective-permute-done.52 = bf16[1024,384]{1,0:T(8,128)(2,1)S(1)} collective-permute-done((bf16[1024,384]{1,0:T(8,128)(2,1)S(1)}, bf16[1024,384]{1,0:T(8,128)(2,1)S(1)}, u32[]{:S(2)}, u32[]{:S(2)}) %collective-permute-start.52) | collective-permute-done | bytes 786464 | tf_op jit(solution)/shard_map/ppermute | solution.py:409
  639.7 33.2 %shard_map.247 = (bf16[1024,768]{1,0:T(8,128)(2,1)}, bf16[1024,768]{1,0:T(8,128)(2,1)}, bf16[1024,768]{1,0:T(8,128)(2,1)}, f32[1024,768]{1,0:T(8,128)}) custom-call(s32[1]{0:T(128)} %bitcast.18.len_ref, bf16[1024,768]{1,0:T(8,128)(2,1)} %get-tuple-element.99.q_ref, bf16[1024,768]{1,0:T(8,128)(2,1)} %get-tuple-element.100.k_ref, ...), custom_call_target="tpu_custom_call" | custom-call | flops 16106127360 | bytes 18874368 | tf_op jit(solution)/shard_map/pallas_call | solution.py:169
  673.0 13.7 %collective-permute-done.39 = bf16[2048,384]{1,0:T(8,128)(2,1)} collective-permute-done((bf16[2048,384]{1,0:T(8,128)(2,1)}, bf16[2048,384]{1,0:T(8,128)(2,1)}, u32[]{:S(2)}, u32[]{:S(2)}) %collective-permute-start.39) | collective-permute-done | bytes 1572896 | tf_op jit(solution)/shard_map/ppermute | solution.py:409
  733.8 22.8 %collective-permute-done.41 = bf16[2048,384]{1,0:T(8,128)(2,1)S(1)} collective-permute-done((bf16[2048,384]{1,0:T(8,128)(2,1)S(1)}, bf16[2048,384]{1,0:T(8,128)(2,1)S(1)}, u32[]{:S(2)}, u32[]{:S(2)}) %collective-permute-start.41) | collective-permute-done | bytes 1572896 | tf_op jit(solution)/shard_map/ppermute | solution.py:409
  777.1 32.9 %collective-permute-done.45 = bf16[384,384]{1,0:T(8,128)(2,1)} collective-permute-done((bf16[384,384]{1,0:T(8,128)(2,1)}, bf16[384,384]{1,0:T(8,128)(2,1)}, u32[]{:S(2)}, u32[]{:S(2)}) %collective-permute-start.45) | collective-permute-done | bytes 294944 | tf_op jit(solution)/shard_map/ppermute | solution.py:409
  838.2 16.6 %combine.5 = (bf16[512,1536]{1,0:T(8,128)(2,1)}, f32[512,1536]{1,0:T(8,128)}) custom-call(s32[1]{0:T(128)} %bitcast.17.core_ref, bf16[1024,2368]{1,0:T(8,128)(2,1)} %copy.107.left_ref, bf16[2368,384]{1,0:T(8,128)(2,1)} %all-gather.4.cloned.1.call-done.refs_0_, bf16[2368,384]{1,0:T(8,128)(2,1)} %collective-permute-done.5.refs_1_, ...), custom_call_target="tpu_custom_call" | custom-call | flops 7449083904 | bytes 16842752 | tf_op jit(solution)/shard_map/combine/pallas_call | solution.py:257
  854.9 9.8 collective-permute-done.64
  872.5 14.3 %collective-permute-done.61 = bf16[1184,384]{1,0:T(8,128)(2,1)} collective-permute-done((bf16[1184,384]{1,0:T(8,128)(2,1)}, bf16[1184,384]{1,0:T(8,128)(2,1)}, u32[]{:S(2)}, u32[]{:S(2)}) %collective-permute-start.61) | collective-permute-done | bytes 909344 | tf_op jit(solution)/shard_map/ppermute | solution.py:409
  900.0 16.1 %reduce-scatter.9.cloned.1.call-done = bf16[192,384]{1,0:T(8,128)(2,1)} async-done(((bf16[768,384]{1,0:T(8,128)(2,1)}), bf16[192,384]{1,0:T(8,128)(2,1)}) %reduce-scatter.9.cloned.1.call-update) | async-done | bytes 147472 | tf_op jit(solution)/shard_map/reduce_scatter | solution.py:487
  926.9 29.5 %collective-permute-done.59 = f32[3096]{0:T(1024)S(1)} collective-permute-done((f32[3096]{0:T(1024)S(1)}, f32[3096]{0:T(1024)S(1)}, u32[]{:S(2)}, u32[]{:S(2)}) %collective-permute-start.59) | collective-permute-done | bytes 12416 | tf_op jit(solution)/shard_map/ppermute | solution.py:503
  956.3 18.0 %collective-permute-start.60 = (f32[3096]{0:T(1024)S(1)}, f32[3096]{0:T(1024)S(1)}, u32[]{:S(2)}, u32[]{:S(2)}) collective-permute-start(f32[3096]{0:T(1024)S(1)} %add.436), channel_id=1, source_target_pairs={{0,2},{1,3},{2,0},{3,1},{4,6},{5,7},{6,4},{7,5},{8,10},{9,11},{10,... | collective-permute-start | bytes 37160 | tf_op jit(solution)/shard_map/ppermute | solution.py:503
  975.7 9.9 collective-permute-done.60
  (536 shorter events, 386.5 us)
Async XLA Ops:
  14.1 117.2 %all-gather.6.cloned.1.call-start = ((), (), s32[]{:S(2)}) async-start(), calls=%async_computation.5 | async-start | bytes 2703360 | tf_op jit(solution)/shard_map/all_gather | solution.py:471
  20.1 274.4 %all-gather.8.cloned.1.call-start = ((), (), s32[]{:S(2)}) async-start(), calls=%async_computation.6 | async-start | bytes 3932160 | tf_op jit(solution)/shard_map/all_gather | solution.py:471
  63.0 110.0 %collective-permute-start.5 = (bf16[2368,384]{1,0:T(8,128)(2,1)}, bf16[2368,384]{1,0:T(8,128)(2,1)}, u32[]{:S(2)}, u32[]{:S(2)}) collective-permute-start(bf16[2368,384]{1,0:T(8,128)(2,1)} %all-gather.4.cloned.1.call-done.refs_0_), channel_id=1, source_target_pairs={{0,8},{4,12},{8,0},{12,4},{16,24},{20,28},{24,16},{28,20},{1,9},{5... | collective-permute-start | bytes 5455880 | tf_op jit(solution)/shard_map/ppermute | solution.py:409
  64.5 111.3 %collective-permute-start.6 = (bf16[2368,384]{1,0:T(8,128)(2,1)}, bf16[2368,384]{1,0:T(8,128)(2,1)}, u32[]{:S(2)}, u32[]{:S(2)}) collective-permute-start(bf16[2368,384]{1,0:T(8,128)(2,1)} %all-gather.4.cloned.1.call-done.refs_0_), channel_id=1, source_target_pairs={{0,16},{4,20},{8,24},{12,28},{16,0},{20,4},{24,8},{28,12},{1,17},{... | collective-permute-start | bytes 5455880 | tf_op jit(solution)/shard_map/ppermute | solution.py:409
  96.2 81.4 %collective-permute-start.4 = (bf16[512,1536]{1,0:T(8,128)(2,1)S(1)}, bf16[512,1536]{1,0:T(8,128)(2,1)}, u32[]{:S(2)}, u32[]{:S(2)}) collective-permute-start(bf16[512,1536]{1,0:T(8,128)(2,1)S(1)} %fusion.4), channel_id=1, source_target_pairs={{0,4},{4,0},{8,12},{12,8},{16,20},{20,16},{24,28},{28,24},{1,5},{5... | collective-permute-start | bytes 4718600 | tf_op jit(solution)/shard_map/ppermute | solution.py:405
  157.0 611.7 %reduce-scatter.5.cloned.1.call-start = ((), (), s32[]{:S(2)}) async-start(), calls=%async_computation.7 | async-start | bytes 1966080 | tf_op jit(solution)/shard_map/reduce_scatter | solution.py:487
  165.3 129.1 %collective-permute-start.21 = (bf16[2048,384]{1,0:T(8,128)(2,1)S(1)}, bf16[2048,384]{1,0:T(8,128)(2,1)}, u32[]{:S(2)}, u32[]{:S(2)}) collective-permute-start(bf16[2048,384]{1,0:T(8,128)(2,1)S(1)} %bitcast.174), channel_id=1, source_target_pairs={{0,8},{4,12},{8,0},{12,4},{16,24},{20,28},{24,16},{28,20},{1,9},{5... | collective-permute-start | bytes 4718600 | tf_op jit(solution)/shard_map/ppermute | solution.py:409
  169.8 128.1 %collective-permute-start.22 = (bf16[2048,384]{1,0:T(8,128)(2,1)S(1)}, bf16[2048,384]{1,0:T(8,128)(2,1)}, u32[]{:S(2)}, u32[]{:S(2)}) collective-permute-start(bf16[2048,384]{1,0:T(8,128)(2,1)S(1)} %bitcast.175), channel_id=1, source_target_pairs={{0,16},{4,20},{8,24},{12,28},{16,0},{20,4},{24,8},{28,12},{1,17},{... | collective-permute-start | bytes 4718600 | tf_op jit(solution)/shard_map/ppermute | solution.py:409
  173.0 112.1 %collective-permute-start.13 = (bf16[384,384]{1,0:T(8,128)(2,1)S(1)}, bf16[384,384]{1,0:T(8,128)(2,1)}, u32[]{:S(2)}, u32[]{:S(2)}) collective-permute-start(bf16[384,384]{1,0:T(8,128)(2,1)S(1)} %slice.247), channel_id=1, source_target_pairs={{0,8},{4,12},{8,0},{12,4},{16,24},{20,28},{24,16},{28,20},{1,9},{5... | collective-permute-start | bytes 884744 | tf_op jit(solution)/shard_map/ppermute | solution.py:409
  294.5 90.1 %collective-permute-start.17 = (bf16[4096,384]{1,0:T(8,128)(2,1)}, bf16[4096,384]{1,0:T(8,128)(2,1)}, u32[]{:S(2)}, u32[]{:S(2)}) collective-permute-start(bf16[4096,384]{1,0:T(8,128)(2,1)} %all-gather.8.cloned.1.call-done.refs_0_.refs_4_), channel_id=1, source_target_pairs={{0,8},{4,12},{8,0},{12,4},{16,24},{20,28},{24,16},{28,20},{1,9},{5... | collective-permute-start | bytes 9437192 | tf_op jit(solution)/shard_map/ppermute | solution.py:409
  301.5 80.6 %collective-permute-start.24 = (bf16[1024,384]{1,0:T(8,128)(2,1)}, bf16[1024,384]{1,0:T(8,128)(2,1)}, u32[]{:S(2)}, u32[]{:S(2)}) collective-permute-start(bf16[1024,384]{1,0:T(8,128)(2,1)} %slice.252), channel_id=1, source_target_pairs={{0,8},{4,12},{8,0},{12,4},{16,24},{20,28},{24,16},{28,20},{1,9},{5... | collective-permute-start | bytes 2359304 | tf_op jit(solution)/shard_map/ppermute | solution.py:409
  303.4 86.4 %collective-permute-start.18 = (bf16[4096,384]{1,0:T(8,128)(2,1)}, bf16[4096,384]{1,0:T(8,128)(2,1)}, u32[]{:S(2)}, u32[]{:S(2)}) collective-permute-start(bf16[4096,384]{1,0:T(8,128)(2,1)} %all-gather.8.cloned.1.call-done.refs_0_.refs_4_), channel_id=1, source_target_pairs={{0,16},{4,20},{8,24},{12,28},{16,0},{20,4},{24,8},{28,12},{1,17},{... | collective-permute-start | bytes 9437192 | tf_op jit(solution)/shard_map/ppermute | solution.py:409
  308.2 79.5 %collective-permute-start.30 = (bf16[512,1536]{1,0:T(8,128)(2,1)}, bf16[512,1536]{1,0:T(8,128)(2,1)}, u32[]{:S(2)}, u32[]{:S(2)}) collective-permute-start(bf16[512,1536]{1,0:T(8,128)(2,1)} %fusion.12), channel_id=1, source_target_pairs={{0,4},{4,0},{8,12},{12,8},{16,20},{20,16},{24,28},{28,24},{1,5},{5... | collective-permute-start | bytes 4718600 | tf_op jit(solution)/shard_map/ppermute | solution.py:405
  321.4 74.5 %collective-permute-start.15 = (bf16[512,1536]{1,0:T(8,128)(2,1)}, bf16[512,1536]{1,0:T(8,128)(2,1)}, u32[]{:S(2)}, u32[]{:S(2)}) collective-permute-start(bf16[512,1536]{1,0:T(8,128)(2,1)} %multiply_convert_fusion.1), channel_id=1, source_target_pairs={{0,4},{4,0},{8,12},{12,8},{16,20},{20,16},{24,28},{28,24},{1,5},{5... | collective-permute-start | bytes 4718600 | tf_op jit(solution)/shard_map/ppermute | solution.py:405
  460.8 80.6 %collective-permute-start.33 = (bf16[1024,384]{1,0:T(8,128)(2,1)}, bf16[1024,384]{1,0:T(8,128)(2,1)}, u32[]{:S(2)}, u32[]{:S(2)}) collective-permute-start(bf16[1024,384]{1,0:T(8,128)(2,1)} %convolution_convert_fusion.11), channel_id=1, source_target_pairs={{0,16},{4,20},{8,24},{12,28},{16,0},{20,4},{24,8},{28,12},{1,17},{... | collective-permute-start | bytes 2359304 | tf_op jit(solution)/shard_map/ppermute | solution.py:409
  461.3 80.6 %collective-permute-start.34 = (bf16[1024,384]{1,0:T(8,128)(2,1)}, bf16[1024,384]{1,0:T(8,128)(2,1)}, u32[]{:S(2)}, u32[]{:S(2)}) collective-permute-start(bf16[1024,384]{1,0:T(8,128)(2,1)} %convolution_convert_fusion.10), channel_id=1, source_target_pairs={{0,8},{4,12},{8,0},{12,4},{16,24},{20,28},{24,16},{28,20},{1,9},{5... | collective-permute-start | bytes 2359304 | tf_op jit(solution)/shard_map/ppermute | solution.py:409
  462.8 79.1 %collective-permute-start.35 = (bf16[1024,384]{1,0:T(8,128)(2,1)}, bf16[1024,384]{1,0:T(8,128)(2,1)}, u32[]{:S(2)}, u32[]{:S(2)}) collective-permute-start(bf16[1024,384]{1,0:T(8,128)(2,1)} %convolution_convert_fusion.9), channel_id=1, source_target_pairs={{0,8},{4,12},{8,0},{12,4},{16,24},{20,28},{24,16},{28,20},{1,9},{5... | collective-permute-start | bytes 2359304 | tf_op jit(solution)/shard_map/ppermute | solution.py:409
  463.4 78.6 %collective-permute-start.36 = (bf16[1024,384]{1,0:T(8,128)(2,1)}, bf16[1024,384]{1,0:T(8,128)(2,1)}, u32[]{:S(2)}, u32[]{:S(2)}) collective-permute-start(bf16[1024,384]{1,0:T(8,128)(2,1)} %convolution_convert_fusion.8), channel_id=1, source_target_pairs={{0,16},{4,20},{8,24},{12,28},{16,0},{20,4},{24,8},{28,12},{1,17},{... | collective-permute-start | bytes 2359304 | tf_op jit(solution)/shard_map/ppermute | solution.py:409
  563.7 109.2 %collective-permute-start.37 = (bf16[2048,384]{1,0:T(8,128)(2,1)}, bf16[2048,384]{1,0:T(8,128)(2,1)}, u32[]{:S(2)}, u32[]{:S(2)}) collective-permute-start(bf16[2048,384]{1,0:T(8,128)(2,1)} %convolution_convert_fusion.7), channel_id=1, source_target_pairs={{0,16},{4,20},{8,24},{12,28},{16,0},{20,4},{24,8},{28,12},{1,17},{... | collective-permute-start | bytes 4718600 | tf_op jit(solution)/shard_map/ppermute | solution.py:409
  622.5 272.8 %reduce-scatter.7.cloned.1.call-start = ((), (), s32[]{:S(2)}) async-start(), calls=%async_computation.8 | async-start | bytes 3932160 | tf_op jit(solution)/shard_map/reduce_scatter | solution.py:487
  768.7 147.3 %reduce-scatter.9.cloned.1.call-start = ((), (), s32[]{:S(2)}) async-start(), calls=%async_computation.9 | async-start | bytes 737280 | tf_op jit(solution)/shard_map/reduce_scatter | solution.py:487
  816.9 107.6 %collective-permute-start.68 = (bf16[512,192]{1,0:T(8,128)(2,1)}, bf16[512,192]{1,0:T(8,128)(2,1)}, u32[]{:S(2)}, u32[]{:S(2)}) collective-permute-start(bf16[512,192]{1,0:T(8,128)(2,1)} %constant_dynamic-slice_fusion), channel_id=1, source_target_pairs={{0,4},{4,0},{8,12},{12,8},{16,20},{20,16},{24,28},{28,24},{1,5},{5... | collective-permute-start | bytes 589832 | tf_op jit(solution)/shard_map/ppermute | solution.py:405
  895.3 99.2 %reduce-scatter.11.cloned.1.call-start = ((), (), s32[]{:S(2)}) async-start(), calls=%async_computation.10 | async-start | bytes 2273280 | tf_op jit(solution)/shard_map/reduce_scatter | solution.py:487
  917.5 69.5 %collective-permute-start.54 = (bf16[256,1536]{1,0:T(8,128)(2,1)S(1)}, bf16[256,1536]{1,0:T(8,128)(2,1)}, u32[]{:S(2)}, u32[]{:S(2)}) collective-permute-start(bf16[256,1536]{1,0:T(8,128)(2,1)S(1)} %pad_maximum_fusion.19), channel_id=1, source_target_pairs={{0,0},{2,1},{4,2},{6,3},{1,4},{3,5},{5,6},{7,7},{8,8},{10,9},{12,1... | collective-permute-start | bytes 2359304 | tf_op jit(solution)/shard_map/ppermute | solution.py:449
  (138 other events, 2547.2 us)
Sparse Core Ops, SparseCore 0:
  14.2 43.6 all-gather.3
  60.0 71.1 all-gather.5
  157.1 64.3 all-gather.7
  622.6 33.2 reduce-scatter.4
  768.8 59.1 reduce-scatter.6
  895.4 20.6 reduce-scatter.8
  918.4 58.5 reduce-scatter.10

commit v3 on v2

--- a/solution.py
+++ b/solution.py
@@ -90,20 +90,25 @@
         o_ref[lo:hi, :] = jnp.where(pos < length, o, 0.0).astype(BF16)
         l_ref[lo:hi, :] = jnp.where(lane_b < hd, got[0][1], got[1][1])
 
-def attn_fwd(length, q, k, v, c, blk=256):
-    rows, cols = q.shape
+def third(rows, pairs, n):
+    return pl.BlockSpec((rows, 128), lambda p: (0, n * pairs + p))
+
+
+def attn_fwd(length, qkv, c, blk=256):
+    rows, cols = qkv.shape[0], qkv.shape[1] // 3
     pairs = cols // 128
     spec = pl.BlockSpec((rows, 128), lambda p: (0, p))
     return pl.pallas_call(
         functools.partial(attn_fwd_kernel, blk=blk),
         grid=(pairs,),
-        in_specs=[pl.BlockSpec(memory_space=pltpu.SMEM), spec, spec, spec,
-                  pl.BlockSpec((1, rows, 2), lambda p: (p, 0, 0))],
+        in_specs=[pl.BlockSpec(memory_space=pltpu.SMEM)]
+        + [third(rows, pairs, n) for n in range(3)]
+        + [pl.BlockSpec((1, rows, 2), lambda p: (p, 0, 0))],
         out_specs=[spec, spec],
         out_shape=[jax.ShapeDtypeStruct((rows, cols), BF16), jax.ShapeDtypeStruct((rows, cols), F32)],
         compiler_params=pltpu.CompilerParams(vmem_limit_bytes=VMEM_BYTES),
         cost_estimate=pl.CostEstimate(flops=rows*rows*128*4*pairs*2, bytes_accessed=rows*cols*12, transcendentals=rows*rows*pairs),
-    )(length, q, k, v, c)
+    )(length, qkv, qkv, qkv, c)
 
 def attn_bwd_kernel(len_ref, q_ref, k_ref, v_ref, c_ref, l_ref, o_ref, g_ref, dq_ref, dk_ref, dv_ref, dc_ref, acc_k, acc_v, *, blk):
     rows, wide = q_ref.shape
@@ -161,22 +166,23 @@
     dv_ref[...] = jnp.where(first, res[0][2], res[1][2]).astype(BF16)
     dc_ref[...] = jnp.where(first, res[1][3], res[0][3])
 
-def attn_bwd(length, q, k, v, c, l, o, g, blk=256):
-    rows, cols = q.shape
+def attn_bwd(length, qkv, c, l, o, g, blk=256):
+    rows, cols = o.shape
     pairs = cols // 128
     spec = pl.BlockSpec((rows, 128), lambda p: (0, p))
     low = jax.ShapeDtypeStruct((rows, cols), BF16)
     dq, dk, dv, dc = pl.pallas_call(
         functools.partial(attn_bwd_kernel, blk=blk),
         grid=(pairs,),
-        in_specs=[pl.BlockSpec(memory_space=pltpu.SMEM), spec, spec, spec,
-                  pl.BlockSpec((1, rows, 2), lambda p: (p, 0, 0)), spec, spec, spec],
+        in_specs=[pl.BlockSpec(memory_space=pltpu.SMEM)]
+        + [third(rows, pairs, n) for n in range(3)]
+        + [pl.BlockSpec((1, rows, 2), lambda p: (p, 0, 0)), spec, spec, spec],
         out_specs=[spec]*4,
         out_shape=[low, low, low, jax.ShapeDtypeStruct((rows, cols), F32)],
         scratch_shapes=[pltpu.VMEM((rows, 128), F32)]*2,
         compiler_params=pltpu.CompilerParams(vmem_limit_bytes=VMEM_BYTES),
         cost_estimate=pl.CostEstimate(flops=rows*rows*128*10*pairs*2, bytes_accessed=rows*cols*24, transcendentals=rows*rows*pairs),
-    )(length, q, k, v, c, l, o, g)
+    )(length, qkv, qkv, qkv, c, l, o, g)
     d3 = dc.reshape(rows, pairs, 128)
     grad_cumul = jnp.stack([d3[:, :, 67], d3[:, :, 3]], axis=2).reshape(rows, 2 * pairs)
     return dq, dk, dv, grad_cumul
@@ -197,40 +203,43 @@
     return jnp.concatenate([r[lo:hi, :] for r in refs], axis=1)
 
 
-def project_kernel(x_ref, *refs, shard):
-    w_refs, (q_ref, k_ref, v_ref, f_ref) = refs[:-4], refs[-4:]
-    step = w_refs[0].shape[0] // 2
-    x = x_ref[...]
-    for kind, out in enumerate((q_ref, k_ref, v_ref)):
-        rows = [joined(w_refs, t * step + kind * shard, t * step + (kind + 1) * shard) for t in range(2)]
-        out[...] = nt(x, jnp.concatenate(rows, axis=0)).astype(BF16)
-    rows = [joined(w_refs, t * step + 3 * shard, (t + 1) * step) for t in range(2)]
-    f_ref[0] = nt(x, jnp.concatenate(rows, axis=0))
-
-
-def project(x, weights, shard, few):
+def project_kernel(x_ref, *refs):
+    pieces_here = (len(refs) - 2) // 2
+    w_refs, f_refs, (out_ref, f_ref) = refs[:pieces_here], refs[pieces_here:-2], refs[-2:]
+    out_ref[...] = nt(x_ref[...], joined(w_refs)).astype(BF16)
+
+    @pl.when(pl.program_id(0) == 0)
+    def _():
+        f_ref[...] = nt(x_ref[...], joined(f_refs))
+
+
+def project(x, weights, few):
     rows = x.shape[0]
-    step = weights[0].shape[0] // 2
-    low = jax.ShapeDtypeStruct((rows, 4 * shard), BF16)
-    spec = pl.BlockSpec((rows, 2 * shard), lambda i: (0, i))
-    pad = step // 2 - 3 * shard
-    q, k, v, f = pl.pallas_call(
-        functools.partial(project_kernel, shard=shard),
-        grid=(2,),
+    extra = 4 * FORGET_PAD
+    cols = (weights[0].shape[0] - extra) // 3
+    outs = [
+        jax.ShapeDtypeStruct((rows, 3 * cols), BF16),
+        jax.ShapeDtypeStruct((rows, extra), F32),
+    ]
+    last = 3 * cols // extra
+    qkv, f = pl.pallas_call(
+        project_kernel,
+        grid=(3,),
         in_specs=[whole(x)]
-        + [pl.BlockSpec((step, w.shape[1]), lambda i: (i, 0)) for w in weights],
-        out_specs=[spec, spec, spec, pl.BlockSpec((1, rows, 2 * pad), lambda i: (i, 0, 0))],
-        out_shape=[low, low, low, jax.ShapeDtypeStruct((2, rows, 2 * pad), F32)],
+        + [pl.BlockSpec((cols, w.shape[1]), lambda i: (i, 0)) for w in weights]
+        + [pl.BlockSpec((extra, w.shape[1]), lambda i: (last, 0)) for w in weights],
+        out_specs=[pl.BlockSpec((rows, cols), lambda i: (0, i)), whole(outs[1])],
+        out_shape=outs,
         compiler_params=pltpu.CompilerParams(vmem_limit_bytes=VMEM_BYTES),
-        cost_estimate=cost(2 * rows * x.shape[1] * 4 * step // 2, [x, *weights, low, low, low]),
+        cost_estimate=cost(2 * rows * x.shape[1] * 3 * cols, [x, *weights, *outs]),
         name="project",
-    )(x, *weights)
-    logits = f.reshape(2, rows, 2, pad)[..., :few].transpose(1, 0, 2, 3).reshape(rows, 4 * few)
-    return q, k, v, logits
-
-
-def combine_kernel(core_ref, left_ref, *refs):
-    w_refs, (give_ref, keep_ref) = refs[:-2], refs[-2:]
+    )(x, *weights, *weights)
+    logits = f.reshape(rows, 4, FORGET_PAD)[..., :few].reshape(rows, 4 * few)
+    return qkv, logits
+
+
+def combine_kernel(core_ref, *refs, lefts):
+    left_refs, w_refs, (give_ref, keep_ref) = refs[:lefts], refs[lefts:-2], refs[-2:]
     step = pl.program_id(0)
     wide = w_refs[0].shape[1]
     for out, cond in ((give_ref, step < 2), (keep_ref, step >= 2)):
@@ -238,11 +247,17 @@
         @pl.when(cond)
         def _():
             for n, w in enumerate(w_refs):
-                out[:, n * wide : (n + 1) * wide] = nn(left_ref[...], w[...]).astype(out.dtype)
-
-
-def combine(core, left, weights):
-    rows = left.shape[0]
+                got, at = None, 0
+                for left in left_refs:
+                    deep = left.shape[1]
+                    part = nn(left[...], w[at : at + deep, :])
+                    got = part if got is None else got + part
+                    at += deep
+                out[:, n * wide : (n + 1) * wide] = got.astype(out.dtype)
+
+
+def combine(core, lefts, weights):
+    rows = lefts[0].shape[0]
     wide = weights[0].shape[1] * len(weights)
     block = rows // 4
 
@@ -255,11 +270,12 @@
         jax.ShapeDtypeStruct((rows // 2, wide), F32),
     ]
     return pl.pallas_call(
-        combine_kernel,
+        functools.partial(combine_kernel, lefts=len(lefts)),
         grid_spec=pltpu.PrefetchScalarGridSpec(
             num_scalar_prefetch=1,
             grid=(4,),
-            in_specs=[pl.BlockSpec((block, left.shape[1]), place)] + [whole(w) for w in weights],
+            in_specs=[pl.BlockSpec((block, left.shape[1]), place) for left in lefts]
+            + [whole(w) for w in weights],
             out_specs=[
                 pl.BlockSpec((block, wide), lambda i, c: (jnp.minimum(i, 1), 0)),
                 pl.BlockSpec((block, wide), lambda i, c: (jnp.maximum(i - 2, 0), 0)),
@@ -267,9 +283,11 @@
         ),
         out_shape=outs,
         compiler_params=pltpu.CompilerParams(vmem_limit_bytes=VMEM_BYTES),
-        cost_estimate=cost(2 * rows * left.shape[1] * wide, [left, *weights, *outs]),
+        cost_estimate=cost(
+            2 * rows * weights[0].shape[0] * wide, [*lefts, *weights, *outs]
+        ),
         name="combine",
-    )(core.reshape(1), left, *weights)
+    )(core.reshape(1), *lefts, *weights)
 
 
 def spread_kernel(len_ref, x_ref, *refs):
@@ -327,65 +345,31 @@
     )(x, *weights)
 
 
-def inner_back_kernel(core_ref, x_ref, gate_ref, up_ref, *refs):
-    pieces_here = (len(refs) - 4) // 2
-    down_refs, two_refs = refs[:pieces_here], refs[pieces_here : 2 * pieces_here]
-    pre_ref, give_ref, keep_ref, total = refs[2 * pieces_here :]
-    step = pl.program_id(0)
+def inner_grads_kernel(x_ref, gate_ref, up_ref, *refs):
+    down_refs, pre_ref = refs[:-1], refs[-1]
     grad = nt(x_ref[...], joined(down_refs))
     gate, up = gate_ref[...], up_ref[...]
     sig = jax.nn.sigmoid(gate)
-    grad_gate = (grad * up * (sig * (1.0 + gate * (1.0 - sig)))).astype(BF16)
-    grad_up = (grad * (gate * sig)).astype(BF16)
-    pre = jnp.concatenate([grad_gate, grad_up], axis=1)
-    pre_ref[...] = pre
-    wide = two_refs[0].shape[1]
-    for n, w in enumerate(two_refs):
-        cols = slice(n * wide, (n + 1) * wide)
-        part = nn(pre, w[...])
-
-        @pl.when(step == 0)
-        def _():
-            total[:, cols] = part
-
-        @pl.when(step > 0)
-        def _():
-            total[:, cols] += part
-
-    @pl.when(step == pl.num_programs(0) - 1)
-    def _():
-        half = give_ref.shape[0]
-        core = core_ref[0]
-        give_ref[...] = total[pl.ds(pl.multiple_of((1 - core) * half, half), half), :].astype(BF16)
-        keep_ref[...] = total[pl.ds(pl.multiple_of(core * half, half), half), :]
-
-
-def inner_back(core, x, gate, up, down, two):
+    pre_ref[:, :UNIT_BLOCK] = (grad * up * (sig * (1.0 + gate * (1.0 - sig)))).astype(BF16)
+    pre_ref[:, UNIT_BLOCK:] = (grad * (gate * sig)).astype(BF16)
+
+
+def inner_grads(x, gate, up, down):
     rows, cols = x.shape
     total = gate.shape[1]
     spec = pl.BlockSpec((rows, UNIT_BLOCK), lambda i: (0, i))
-    outs = [
-        jax.ShapeDtypeStruct((rows, 2 * total), BF16),
-        jax.ShapeDtypeStruct((rows // 2, cols), BF16),
-        jax.ShapeDtypeStruct((rows // 2, cols), F32),
-    ]
+    out = jax.ShapeDtypeStruct((rows, 2 * total), BF16)
     return pl.pallas_call(
-        inner_back_kernel,
+        inner_grads_kernel,
         grid=(total // UNIT_BLOCK,),
-        in_specs=[pl.BlockSpec(memory_space=pltpu.SMEM), whole(x), spec, spec]
-        + [pl.BlockSpec((UNIT_BLOCK, w.shape[1]), lambda i: (i, 0)) for w in down]
-        + [pl.BlockSpec((2 * UNIT_BLOCK, w.shape[1]), lambda i: (i, 0)) for w in two],
-        out_specs=[
-            pl.BlockSpec((rows, 2 * UNIT_BLOCK), lambda i: (0, i)),
-            whole(outs[1]),
-            whole(outs[2]),
-        ],
-        out_shape=outs,
-        scratch_shapes=[pltpu.VMEM((rows, cols), F32)],
+        in_specs=[whole(x), spec, spec]
+        + [pl.BlockSpec((UNIT_BLOCK, w.shape[1]), lambda i: (i, 0)) for w in down],
+        out_specs=pl.BlockSpec((rows, 2 * UNIT_BLOCK), lambda i: (0, i)),
+        out_shape=out,
         compiler_params=pltpu.CompilerParams(vmem_limit_bytes=VMEM_BYTES),
-        cost_estimate=cost(6 * rows * cols * total, [x, gate, up, *down, *two, *outs]),
-        name="inner_back",
-    )(core.reshape(1), x, gate, up, *down, *two)
+        cost_estimate=cost(2 * rows * cols * total, [x, gate, up, *down, out]),
+        name="inner_grads",
+    )(x, gate, up, *down)
 
 
 class Plan:
@@ -470,18 +454,22 @@
         )
         return lax.all_gather(pair, "tensor", axis=0, tiled=True)
 
-    def chip_gather(self, own):
-        half = own.shape[0] // 2
+    def near_gather(self, own):
         if self.bits == 2:
-            by_x = self.swap_chip(own, 0)
-            by_y = self.swap_chip(own, 1)
-            far_top = self.swap_chip(by_x[:half], 1)
-            far_low = self.swap_chip(by_y[half:], 0)
-            return [own, by_x, by_y, jnp.concatenate([far_top, far_low], axis=0)]
+            return [own, self.swap_chip(own, 0), self.swap_chip(own, 1)]
         parts = [own]
         for bit in range(self.bits):
             parts = parts + [self.swap_chip(p, bit) for p in parts]
         return [jnp.concatenate(parts, axis=1)]
+
+    def far_gather(self, near):
+        if self.bits != 2:
+            return near
+        own, by_x, by_y = near
+        half = own.shape[0] // 2
+        far_top = self.swap_chip(by_x[:half], 1)
+        far_low = self.swap_chip(by_y[half:], 0)
+        return [own, by_x, by_y, jnp.concatenate([far_top, far_low], axis=0)]
 
     def scatter(self, total):
         return lax.psum_scatter(total, "tensor", scatter_dimension=0, tiled=True)
@@ -505,11 +493,9 @@
 
 
 class Reduction:
-    def __init__(self, plan, left, right):
-        self.plan, self.left, self.right = plan, left, right
+    def __init__(self, plan, lefts, right):
+        self.plan, self.lefts, self.right = plan, lefts, right
         self.wide = right.shape[1] // plan.chips
-        self.rows = left.shape[1]
-        self.half = self.rows // 2
         self.staged = plan.bits == 2
         if self.staged:
             self.first = [
@@ -519,16 +505,34 @@
                 self.top(2).astype(BF16),
             ]
         else:
-            self.first = [self.term(r, 0, self.rows) for r in range(plan.chips)]
-
-    def term(self, r, lo, hi):
-        return dot_first(self.left[:, lo:hi], self.right[:, r * self.wide : (r + 1) * self.wide])
+            self.first = [
+                jnp.concatenate([self.top(r), self.low(r)], axis=0) for r in range(plan.chips)
+            ]
+
+    def term(self, r, side):
+        right = self.right[:, r * self.wide : (r + 1) * self.wide]
+        parts = []
+        for left in self.lefts:
+            half = left.shape[1] // 2
+            parts.append(dot_first(left[:, side * half : (side + 1) * half], right))
+        return parts[0] if len(parts) == 1 else jnp.concatenate(parts, axis=0)
 
     def top(self, r):
-        return self.term(r, 0, self.half)
+        return self.term(r, 0)
 
     def low(self, r):
-        return self.term(r, self.half, self.rows)
+        return self.term(r, 1)
+
+    def by_place(self, half):
+        if len(self.lefts) == 1:
+            return half
+        parts, at = [], 0
+        for left in self.lefts:
+            parts.append((at, left.shape[1] // 4))
+            at += left.shape[1] // 2
+        return jnp.concatenate(
+            [half[at + n * few : at + (n + 1) * few] for n in range(2) for at, few in parts], axis=0
+        )
 
     def send_first(self):
         if self.staged:
@@ -560,7 +564,7 @@
             x_low, y_top = self.got[2:]
             top = self.top(0) + x_top.astype(F32) + y_top.astype(F32)
             low = self.low(0) + x_low.astype(F32) + y_low.astype(F32)
-            total = jnp.concatenate([top, low], axis=0)
+            total = jnp.concatenate([self.by_place(top.astype(BF16)), self.by_place(low.astype(BF16))], axis=0)
         else:
             parts = self.got
             for bit in reversed(range(self.plan.bits)):
@@ -569,7 +573,10 @@
                     k + self.plan.swap_chip(g.astype(BF16), bit).astype(F32)
                     for k, g in zip(keep, give)
                 ]
-            total = parts[0]
+            half = parts[0].shape[0] // 2
+            total = jnp.concatenate(
+                [self.by_place(parts[0][:half]), self.by_place(parts[0][half:])], axis=0
+            )
         return total.astype(BF16)
 
 
@@ -625,17 +632,25 @@
         )
     )
     inputs, line_one = together(inputs, line_one)
-    full_one = plan.chip_gather(line_one)
+    rows_one = line_one.shape[0] // 4
+
+    def by_kind(piece):
+        piece = piece.reshape(4, rows_one, -1)
+        edges = [0, shard_cols, 2 * shard_cols, 3 * shard_cols, rows_one]
+        parts = [piece[:, a:b].reshape(-1, piece.shape[-1]) for a, b in zip(edges, edges[1:])]
+        return jnp.concatenate(parts, axis=0)
+
+    full_one = [by_kind(piece) for piece in plan.far_gather(plan.near_gather(line_one))]
     rows_in = plan.to_chip(inputs).astype(F32)
     line_mid = plan.line_gather(
         jnp.concatenate([split_rows(w_out), split_rows(w_down)], axis=1)
     )
+    line_mid, full_one = together(line_mid, full_one)
     line_mid = line_mid.reshape(4, -1, line_mid.shape[-1])
-    full_out = plan.chip_gather(line_mid[:, :shard_cols].reshape(4 * shard_cols, -1))
-    full_down = plan.chip_gather(line_mid[:, shard_cols:].reshape(-1, line_mid.shape[-1]))
+    near_out = plan.near_gather(line_mid[:, :shard_cols].reshape(4 * shard_cols, -1))
+    near_down = plan.near_gather(line_mid[:, shard_cols:].reshape(-1, line_mid.shape[-1]))
     two_part = jnp.concatenate([by_block(w_gate), by_block(w_up)], axis=2)
     line_two = plan.line_gather(two_part.reshape(2, -1, two_part.shape[-1]))
-    full_two = plan.chip_gather(line_two)
 
     other_assign = plan.swap_core(seq_assign)
     assign_both = jnp.where(
@@ -656,35 +671,39 @@
 
     scale_one = row_scale(rows_in)
     normed_one = plan.both_rows((rows_in * scale_one * gain_one).astype(BF16))
-    queries, key_rows, value_rows, logits = project(normed_one, full_one, shard_cols, heads_shard)
+    qkv, logits = project(normed_one, full_one, heads_shard)
     forget_logit = logits + bias_here
     cumul_gate = jnp.cumsum(jax.nn.log_sigmoid(forget_logit), axis=0)
     gate_pairs = cumul_gate.reshape(seq_rows, heads_here // 2, 2).transpose(1, 0, 2)
-    mixed_low, log_total = attn_fwd(count, queries, key_rows, value_rows, gate_pairs)
-    mixed_low, out_grad = together(mixed_low, out_grad)
+    near_out, gate_pairs = together(near_out, gate_pairs)
+    full_out = plan.far_gather(near_out)
+    mixed_low, log_total = attn_fwd(count, qkv, gate_pairs)
+    mixed_low, out_grad, near_down, full_out = together(mixed_low, out_grad, near_down, full_out)
+    full_down = plan.far_gather(near_down)
+    full_two = plan.far_gather(plan.near_gather(line_two))
     cotangent = plan.to_chip(out_grad).astype(F32)
-    hidden_in = rows_in + plan.sum_rows(*combine(core, mixed_low, full_out))
+    hidden_in = rows_in + plan.sum_rows(*combine(core, [mixed_low], full_out))
 
     scale_two = row_scale(hidden_in)
     normed_two = plan.both_rows((hidden_in * scale_two * gain_two).astype(BF16))
+    normed_two, full_down = together(normed_two, full_down)
     gate_pre, up_pre, inner_low = inner_units(normed_two, full_two)
     grad_ffn = plan.both_rows((valid_here * cotangent).astype(BF16))
-    down_sum = Reduction(plan, inner_low, grad_ffn)
+    down_sum = Reduction(plan, [inner_low], grad_ffn)
     down_sum.first, gate_pre = together(down_sum.first, gate_pre)
     down_sum.send_first()
-    ffn_rows = plan.sum_rows(*combine(core, inner_low, full_down))
-    outputs = plan.from_chip((valid_here * (hidden_in + ffn_rows)).astype(BF16))
-
-    grad_pre, give_two, keep_two = inner_back(
-        core, grad_ffn, gate_pre, up_pre, full_down, full_two
-    )
-    down_sum.got, grad_pre = together(down_sum.got, grad_pre)
+
+    grad_pre = inner_grads(grad_ffn, gate_pre, up_pre, full_down)
+    down_far, grad_pre = together(down_sum.got[:2], grad_pre)
+    down_sum.got = [*down_far, *down_sum.got[2:]]
+    two_sum = Reduction(plan, [grad_pre], normed_two)
+    two_sum.first, down_sum.got, grad_pre = together(two_sum.first, down_sum.got, grad_pre)
+    two_sum.send_first()
     down_sum.prepare_second()
-    two_sum = Reduction(plan, grad_pre, normed_two)
-    two_sum.first, down_sum.second = together(two_sum.first, down_sum.second)
+    give_two, keep_two = combine(core, [grad_pre], full_two)
+    two_far, down_sum.second, give_two = together(two_sum.got[:2], down_sum.second, give_two)
+    two_sum.got = [*two_far, *two_sum.got[2:]]
     down_sum.send_second()
-    two_sum.send_first()
-    down_pair = plan.scatter(down_sum.finish())
     grad_normed_two = plan.sum_rows(give_two, keep_two)
     gain_two_term = jnp.sum(grad_normed_two * hidden_in * scale_two, axis=0)
     grad_hidden = valid_here * cotangent + norm_back(
@@ -692,48 +711,44 @@
     )
 
     grad_attn = plan.both_rows(grad_hidden.astype(BF16))
+    out_sum = Reduction(plan, [mixed_low], grad_attn)
+    out_sum.first, down_sum.last, grad_attn = together(out_sum.first, down_sum.last, grad_attn)
+    out_sum.send_first()
     grad_mixed = spread(count, grad_attn, full_out)
     query_low, key_low, value_low, grad_cumul = attn_bwd(
-        count, queries, key_rows, value_rows, gate_pairs, log_total, mixed_low, grad_mixed
-    )
-    two_sum.got, query_low = together(two_sum.got, query_low)
+        count, qkv, gate_pairs, log_total, mixed_low, grad_mixed
+    )
+    two_sum.got, out_sum.got, query_low = together(two_sum.got, out_sum.got, query_low)
     two_sum.prepare_second()
-    two_sum.second, query_low, key_low, value_low, grad_cumul = together(
-        two_sum.second, query_low, key_low, value_low, grad_cumul
+    out_sum.prepare_second()
+    two_sum.second, out_sum.second, query_low, key_low, value_low, grad_cumul = together(
+        two_sum.second, out_sum.second, query_low, key_low, value_low, grad_cumul
     )
     two_sum.send_second()
+    out_sum.send_second()
+    down_pair = plan.scatter(down_sum.finish())
     grad_logf = jnp.flip(jnp.cumsum(jnp.flip(grad_cumul, 0), axis=0), 0)
     grad_logit = grad_logf * jax.nn.sigmoid(-forget_logit)
     bias_term = jnp.sum(grad_logit, axis=0)
-    grad_one = jnp.concatenate(
-        [
-            query_low.reshape(seq_rows, 4, shard_cols),
-            key_low.reshape(seq_rows, 4, shard_cols),
-            value_low.reshape(seq_rows, 4, shard_cols),
-            jnp.pad(
-                grad_logit.astype(BF16).reshape(seq_rows, 4, heads_shard),
-                ((0, 0), (0, 0), (0, FORGET_PAD - heads_shard)),
-            ),
-        ],
-        axis=2,
+    logit_low = jnp.pad(
+        grad_logit.astype(BF16).reshape(seq_rows, 4, heads_shard),
+        ((0, 0), (0, 0), (0, FORGET_PAD - heads_shard)),
     ).reshape(seq_rows, -1)
-    grad_attn, grad_one = together(grad_attn, grad_one)
-    out_sum = Reduction(plan, mixed_low, grad_attn)
+    grad_one = [query_low, key_low, value_low, logit_low]
+    grad_one, two_sum.last, out_sum.last = together(grad_one, two_sum.last, out_sum.last)
     one_sum = Reduction(plan, grad_one, normed_one)
-    out_sum.first, one_sum.first, two_sum.last = together(
-        out_sum.first, one_sum.first, two_sum.last
-    )
-    out_sum.send_first()
     one_sum.send_first()
+    one_far, two_sum.last, out_sum.last, inner_low = together(
+        one_sum.got[:2], two_sum.last, out_sum.last, inner_low
+    )
+    ffn_rows = plan.sum_rows(*combine(core, [inner_low], full_down))
+    outputs = plan.from_chip((valid_here * (hidden_in + ffn_rows)).astype(BF16))
+    one_sum.got = [*one_far, *one_sum.got[2:]]
     two_total, down_pair = together(two_sum.finish(), down_pair)
     two_pair = plan.scatter(two_total)
-    out_sum.got, one_sum.got, two_total, grad_one = together(
-        out_sum.got, one_sum.got, two_total, grad_one
-    )
-    out_sum.prepare_second()
+    one_sum.got, two_total = together(one_sum.got, two_total)
     one_sum.prepare_second()
-    out_sum.second, one_sum.second = together(out_sum.second, one_sum.second)
-    out_sum.send_second()
+    one_sum.second, grad_one = together(one_sum.second, grad_one)
     one_sum.send_second()
     out_total, two_pair = together(out_sum.finish(), two_pair)
     out_pair = plan.scatter(out_total)

time: 1020 us -> 971 us (0.952)
  waiting for transfers between devices: 401 us -> 334 us
  other arithmetic: 85.3 us -> 128 us
  Pallas kernels: 199 us -> 182 us
    ppermute x42, waiting for transfers between devices: 269 us -> 179 us  [swap_chip(): return lax.ppermute(array, 'dp', perm)]
    concatenate x5 -> x12, other arithmetic: 7.42 us -> 30.4 us  [the longest x2 18.3 us: by_kind(): return jnp.concatenate(parts, axis=0)]
    ppermute x2, waiting for transfers between devices: 39.3 us -> 59.3 us  [sum_all(): vector = vector + lax.ppermute(vector, 'tensor', perm)]
    convert_element_type x0 -> x7, other arithmetic: none -> 17.5 us  [the longest x3 7.4 us: finish(): top.astype(BF16)]
    pallas_call x5 -> x6, Pallas kernels: 113 us -> 95.5 us  [the longest x4 64.8 us: combine(): pl.pallas_call(functools.partial(combine_kernel, lefts=len(lefts)), grid_...]
    optimization_barrier x4 -> x1, local copies, waits for them, and re-layouts: 13.1 us -> 0.84 us  [together(): return lax.optimization_barrier(groups)]
    unnamed x193 -> x219, local copies, waits for them, and re-layouts: 15.2 us -> 21 us
    dot_general x32 -> x56, matrix products: 99.3 us -> 103 us  [dot_first(): lax.dot_general(left, right, (((0,), (0,)), ((), ())), preferred_element_...]
  transfers between devices with their start and end apart: 76 -> 76, of which waited for: 28 -> 29; matrix products, arithmetic and copies ran while one was open for 23% -> 26% of each run, Pallas kernels for 18% -> 17%
where the time goes in v3:
time: 971 us; the launch traced here: 962 us
  waiting for transfers between devices  334 us (34%)
  Pallas kernels  182 us (19%)
  other arithmetic  128 us (13%)
  starting transfers between devices  124 us (13%)
  matrix products  103 us (11%)
  local copies, waits for them, and re-layouts  74.4 us (8%)
  between operations  16.3 us (2%)
    ppermute x42, waiting for transfers between devices, swap_chip(): return lax.ppermute(array, 'dp', perm)  179 us
    dot_general x56, matrix products, dot_first(): lax.dot_general(left, right, (((0,), (0,)), ((), ())), preferred_element_...  103 us
    pallas_call x4, Pallas kernels, combine(): pl.pallas_call(functools.partial(combine_kernel, lefts=len(lefts)), grid_...  64.8 us
    ppermute x2, waiting for transfers between devices, sum_all(): vector = vector + lax.ppermute(vector, 'tensor', perm)  59.3 us
    ppermute x42, starting transfers between devices, swap_chip(): return lax.ppermute(array, 'dp', perm)  45.5 us
    ppermute x17, starting transfers between devices, swap_core(): return lax.ppermute(array, 'dp', self.core_perm)  45.5 us
    all_gather x3, waiting for transfers between devices, line_gather(): return lax.all_gather(pair, 'tensor', axis=0, tiled=True)  37.6 us
    ppermute x4, waiting for transfers between devices, to_chip(): lax.ppermute(self.by_chip(part), ('dp', 'tensor'), self.route(turn))  34.6 us
  transfers between devices with their start and end apart: 76, of which 29 were waited for; matrix products, arithmetic and copies ran while one was open for 26% of the time, Pallas kernels for 17%

profile of v3, /device:TPU:0, one launch (start us, length us, event | category | flops | bytes accessed | tf_op | source)
XLA Modules:
  0.0 961.5 jit_solution(5718885762301337064)
XLA Ops:
  20.2 37.6 %all-gather.4.cloned.1.call-done = bf16[2368,384]{1,0:T(8,128)(2,1)} async-done(((bf16[592,384]{1,0:T(8,128)(2,1)}), bf16[2368,384]{1,0:T(8,128)(2,1)}) %all-gather.4.cloned.1.call-update) | async-done | bytes 1818640 | tf_op jit(solution)/shard_map/all_gather | solution.py:455
  70.7 27.2 %collective-permute-done.3 = bf16[256,1536]{1,0:T(8,128)(2,1)} collective-permute-done((bf16[256,1536]{1,0:T(8,128)(2,1)}, bf16[256,1536]{1,0:T(8,128)(2,1)}, u32[]{:S(2)}, u32[]{:S(2)}) %collective-permute-start.3) | collective-permute-done | bytes 786464 | tf_op jit(solution)/shard_map/ppermute | solution.py:420
  101.0 27.5 %collective-permute-start.4 = (bf16[512,1536]{1,0:T(8,128)(2,1)S(1)}, bf16[512,1536]{1,0:T(8,128)(2,1)}, u32[]{:S(2)}, u32[]{:S(2)}) collective-permute-start(bf16[512,1536]{1,0:T(8,128)(2,1)S(1)} %fusion.2), channel_id=1, source_target_pairs={{0,4},{4,0},{8,12},{12,8},{16,20},{20,16},{24,28},{28,24},{1,5},{5... | collective-permute-start | bytes 4718600 | tf_op jit(solution)/shard_map/ppermute | solution.py:389
  142.2 9.3 pad_maximum_fusion.5
  176.3 13.0 %project.1 = (bf16[1024,2304]{1,0:T(8,128)(2,1)}, f32[1024,64]{1,0:T(8,128)}) custom-call(bf16[1024,1536]{1,0:T(8,128)(2,1)} %pad_maximum_fusion.x_ref, bf16[2368,384]{1,0:T(8,128)(2,1)} %get-tuple-element.136.refs_0_.refs_4_, bf16[2368,384]{1,0:T(8,128)(2,1)} %get-tuple-element.137.refs_1_.refs_5_, bf16[2368,384]{1,0:T(8,128)(2,1)} %get-tuple-element.138.refs_2_.refs_6_, ...), custom_call_target="tpu_custom_call" | custom-call | flops 7247757312 | bytes 15400960 | tf_op jit(solution)/shard_map/project/pallas_call | solution.py:225
  190.7 15.9 %reduce-window.14 = f32[12,8,128]{2,1,0:T(8,128)S(1)} reduce-window(f32[12,8,128]{2,1,0:T(8,128)S(1)} %slice.487, f32[]{:T(128)} %constant.558.clone.1), window={size=1x1x128 pad=0_0x0_0x127_0}, to_apply=%region_3.4 | reduce-window | flops 1560576 | bytes 98308 | tf_op jit(solution)/shard_map/reduce-window
  218.0 9.1 collective-permute-done.15
  228.6 25.1 %shard_map.246 = (bf16[1024,768]{1,0:T(8,128)(2,1)}, f32[1024,768]{1,0:T(8,128)}) custom-call(s32[1]{0:T(128)} %bitcast.18.len_ref, bf16[1024,2304]{1,0:T(8,128)(2,1)} %get-tuple-element.140.q_ref.k_ref.v_ref, bf16[1024,2304]{1,0:T(8,128)(2,1)} %get-tuple-element.140.q_ref.k_ref.v_ref, bf16[1024,2304]{1,0:T(8,128)(2,1)} %get-tuple-element.140.q_ref.k_ref.v_ref, ...), custom_call_target="tpu_custom_call" | custom-call | flops 6442450944 | bytes 9437184 | tf_op jit(solution)/shard_map/pallas_call | solution.py:101
  253.7 39.1 %collective-permute-done.14 = bf16[384,384]{1,0:T(8,128)(2,1)S(1)} collective-permute-done((bf16[384,384]{1,0:T(8,128)(2,1)S(1)}, bf16[384,384]{1,0:T(8,128)(2,1)S(1)}, u32[]{:S(2)}, u32[]{:S(2)}) %collective-permute-start.14) | collective-permute-done | bytes 294944 | tf_op jit(solution)/shard_map/ppermute | solution.py:393
  328.3 13.7 %collective-permute-start.27 = (bf16[512,1536]{1,0:T(8,128)(2,1)S(1)}, bf16[512,1536]{1,0:T(8,128)(2,1)S(1)}, u32[]{:S(2)}, u32[]{:S(2)}) collective-permute-start(bf16[512,1536]{1,0:T(8,128)(2,1)S(1)} %fusion.10), channel_id=1, source_target_pairs={{0,4},{4,0},{8,12},{12,8},{16,20},{20,16},{24,28},{28,24},{1,5},{5... | collective-permute-start | bytes 4718600 | tf_op jit(solution)/shard_map/ppermute | solution.py:389
  353.6 27.5 %collective-permute-done.23 = bf16[2048,384]{1,0:T(8,128)(2,1)S(1)} collective-permute-done((bf16[2048,384]{1,0:T(8,128)(2,1)S(1)}, bf16[2048,384]{1,0:T(8,128)(2,1)S(1)}, u32[]{:S(2)}, u32[]{:S(2)}) %collective-permute-start.23) | collective-permute-done | bytes 1572896 | tf_op jit(solution)/shard_map/ppermute | solution.py:393
  387.8 20.5 %inner_units.1 = (f32[1024,2048]{1,0:T(8,128)}, f32[1024,2048]{1,0:T(8,128)}, bf16[1024,2048]{1,0:T(8,128)(2,1)}) custom-call(bf16[1024,1536]{1,0:T(8,128)(2,1)} %pad_maximum_fusion.3.x_ref, bf16[4096,384]{1,0:T(8,128)(2,1)} %all-gather.8.cloned.1.call-done.refs_0_.refs_1_, bf16[4096,384]{1,0:T(8,128)(2,1)} %collective-permute-done.21.refs_1_.refs_2_, ...), custom_call_target="tpu_custom_call" | custom-call | flops 12884901888 | bytes 36700160 | tf_op jit(solution)/shard_map/inner_units/pallas_call | solution.py:335
  424.9 17.8 %inner_grads.1.refs_0_ = bf16[1024,4096]{1,0:T(8,128)(2,1)} custom-call(bf16[1024,1536]{1,0:T(8,128)(2,1)} %pad_maximum_fusion.1.x_ref, f32[1024,2048]{1,0:T(8,128)} %get-tuple-element.164.gate_ref, f32[1024,2048]{1,0:T(8,128)} %get-tuple-element.165.up_ref, bf16[2048,384]{1,0:T(8,128)(2,1)} %bitcast.200, bf16[2048,384]{1,0:T(8,128)(2,1)} %copy-done.31, ...), custom_call_target="tpu_custom_call" | custom-call | flops 6442450944 | bytes 34603008 | tf_op jit(solution)/shard_map/inner_grads/pallas_call | solution.py:362
  468.5 25.2 %combine.5 = (bf16[512,1536]{1,0:T(8,128)(2,1)}, f32[512,1536]{1,0:T(8,128)}) custom-call(s32[1]{0:T(128)} %bitcast.17.core_ref, bf16[1024,4096]{1,0:T(8,128)(2,1)} %inner_grads.1.refs_0_, bf16[4096,384]{1,0:T(8,128)(2,1)} %all-gather.8.cloned.1.call-done.refs_0_.refs_1_, bf16[4096,384]{1,0:T(8,128)(2,1)} %collective-permute-done.21.refs_1_.refs_2_, ...), custom_call_target="tpu_custom_call" | custom-call | flops 12884901888 | bytes 25690112 | tf_op jit(solution)/shard_map/combine/pallas_call | solution.py:272
  534.2 33.9 %collective-permute-done.38 = bf16[1024,384]{1,0:T(8,128)(2,1)} collective-permute-done((bf16[1024,384]{1,0:T(8,128)(2,1)S(1)}, bf16[1024,384]{1,0:T(8,128)(2,1)}, u32[]{:S(2)}, u32[]{:S(2)}) %collective-permute-start.38) | collective-permute-done | bytes 786464 | tf_op jit(solution)/shard_map/ppermute | solution.py:393
  578.9 33.4 %shard_map.247 = (bf16[1024,768]{1,0:T(8,128)(2,1)}, bf16[1024,768]{1,0:T(8,128)(2,1)}, bf16[1024,768]{1,0:T(8,128)(2,1)}, f32[1024,768]{1,0:T(8,128)}) custom-call(s32[1]{0:T(128)} %bitcast.18.len_ref, bf16[1024,2304]{1,0:T(8,128)(2,1)} %get-tuple-element.140.q_ref.k_ref.v_ref, bf16[1024,2304]{1,0:T(8,128)(2,1)} %get-tuple-element.140.q_ref.k_ref.v_ref, ...), custom_call_target="tpu_custom_call" | custom-call | flops 16106127360 | bytes 18874368 | tf_op jit(solution)/shard_map/pallas_call | solution.py:174
  656.0 25.1 %collective-permute-done.46 = bf16[384,384]{1,0:T(8,128)(2,1)} collective-permute-done((bf16[384,384]{1,0:T(8,128)(2,1)}, bf16[384,384]{1,0:T(8,128)(2,1)}, u32[]{:S(2)}, u32[]{:S(2)}) %collective-permute-start.46) | collective-permute-done | bytes 294944 | tf_op jit(solution)/shard_map/ppermute | solution.py:393
  720.4 13.8 %collective-permute-done.48 = bf16[1184,384]{1,0:T(8,128)(2,1)} collective-permute-done((bf16[1184,384]{1,0:T(8,128)(2,1)S(1)}, bf16[1184,384]{1,0:T(8,128)(2,1)}, u32[]{:S(2)}, u32[]{:S(2)}) %collective-permute-start.48) | collective-permute-done | bytes 909344 | tf_op jit(solution)/shard_map/ppermute | solution.py:393
  735.8 14.4 %combine.6 = (bf16[512,1536]{1,0:T(8,128)(2,1)}, f32[512,1536]{1,0:T(8,128)}) custom-call(s32[1]{0:T(128)} %bitcast.17.core_ref, bf16[1024,2048]{1,0:T(8,128)(2,1)} %get-tuple-element.220.refs_0_, bf16[2048,384]{1,0:T(8,128)(2,1)} %bitcast.201, bf16[2048,384]{1,0:T(8,128)(2,1)} %copy-done.31, bf16[2048,384]{1,0:T(8,128)(2,1)} %collective-permute-done.13.refs_2_.refs_3_, ...), custom_call_target="tpu_custom_call" | custom-call | flops 6442450944 | bytes 15204352 | tf_op jit(solution)/shard_map/combine/pallas_call | solution.py:272
  772.8 17.7 %combine.7 = (bf16[512,1536]{1,0:T(8,128)(2,1)}, f32[512,1536]{1,0:T(8,128)}) custom-call(s32[1]{0:T(128)} %bitcast.17.core_ref, bf16[1024,768]{1,0:T(8,128)(2,1)} %get-tuple-element.236.refs_0_, bf16[1024,768]{1,0:T(8,128)(2,1)} %get-tuple-element.237.refs_1_, bf16[1024,768]{1,0:T(8,128)(2,1)} %get-tuple-element.238.refs_2_, ...), custom_call_target="tpu_custom_call" | custom-call | flops 7449083904 | bytes 16842752 | tf_op jit(solution)/shard_map/combine/pallas_call | solution.py:272
  800.9 12.3 %collective-permute-done.64 = bf16[1184,384]{1,0:T(8,128)(2,1)} collective-permute-done((bf16[1184,384]{1,0:T(8,128)(2,1)S(1)}, bf16[1184,384]{1,0:T(8,128)(2,1)}, u32[]{:S(2)}, u32[]{:S(2)}) %collective-permute-start.64) | collective-permute-done | bytes 909344 | tf_op jit(solution)/shard_map/ppermute | solution.py:393
  846.9 13.7 %reduce-scatter.9.cloned.1.call-done = bf16[192,384]{1,0:T(8,128)(2,1)} async-done(((bf16[768,384]{1,0:T(8,128)(2,1)}), bf16[192,384]{1,0:T(8,128)(2,1)}) %reduce-scatter.9.cloned.1.call-update) | async-done | bytes 147472 | tf_op jit(solution)/shard_map/reduce_scatter | solution.py:475
  861.5 11.6 %collective-permute-start.62 = (f32[3096]{0:T(1024)S(1)}, f32[3096]{0:T(1024)S(1)}, u32[]{:S(2)}, u32[]{:S(2)}) collective-permute-start(f32[3096]{0:T(1024)S(1)} %add.440), channel_id=1, source_target_pairs={{0,2},{1,3},{2,0},{3,1},{4,6},{5,7},{6,4},{7,5},{8,10},{9,11},{10,... | collective-permute-start | bytes 37160 | tf_op jit(solution)/shard_map/ppermute | solution.py:491
  874.3 59.3 %collective-permute-done.62 = f32[3096]{0:T(1024)S(1)} collective-permute-done((f32[3096]{0:T(1024)S(1)}, f32[3096]{0:T(1024)S(1)}, u32[]{:S(2)}, u32[]{:S(2)}) %collective-permute-start.62) | collective-permute-done | bytes 12416 | tf_op jit(solution)/shard_map/ppermute | solution.py:491
  (600 shorter events, 401.4 us)
Async XLA Ops:
  7.2 50.7 %all-gather.4.cloned.1.call-start = ((), (), s32[]{:S(2)}) async-start(), calls=%async_computation.4 | async-start | bytes 2273280 | tf_op jit(solution)/shard_map/all_gather | solution.py:455
  14.1 154.6 %all-gather.6.cloned.1.call-start = ((), (), s32[]{:S(2)}) async-start(), calls=%async_computation.5 | async-start | bytes 2703360 | tf_op jit(solution)/shard_map/all_gather | solution.py:455
  20.1 194.0 %all-gather.8.cloned.1.call-start = ((), (), s32[]{:S(2)}) async-start(), calls=%async_computation.6 | async-start | bytes 3932160 | tf_op jit(solution)/shard_map/all_gather | solution.py:455
  67.3 61.2 %collective-permute-start.20 = (bf16[1024,192]{1,0:T(8,128)(2,1)}, bf16[1024,192]{1,0:T(8,128)(2,1)}, u32[]{:S(2)}, u32[]{:S(2)}) collective-permute-start(bf16[1024,192]{1,0:T(8,128)(2,1)} %dynamic-slice_bitcast_fusion), channel_id=1, source_target_pairs={{0,4},{4,0},{8,12},{12,8},{16,20},{20,16},{24,28},{28,24},{1,5},{5... | collective-permute-start | bytes 1179656 | tf_op jit(solution)/shard_map/ppermute | solution.py:389
  67.7 64.0 %collective-permute-start.6 = (bf16[2368,384]{1,0:T(8,128)(2,1)}, bf16[2368,384]{1,0:T(8,128)(2,1)}, u32[]{:S(2)}, u32[]{:S(2)}) collective-permute-start(bf16[2368,384]{1,0:T(8,128)(2,1)} %all-gather.4.cloned.1.call-done), channel_id=1, source_target_pairs={{0,8},{4,12},{8,0},{12,4},{16,24},{20,28},{24,16},{28,20},{1,9},{5... | collective-permute-start | bytes 5455880 | tf_op jit(solution)/shard_map/ppermute | solution.py:393
  69.2 63.3 %collective-permute-start.7 = (bf16[2368,384]{1,0:T(8,128)(2,1)}, bf16[2368,384]{1,0:T(8,128)(2,1)}, u32[]{:S(2)}, u32[]{:S(2)}) collective-permute-start(bf16[2368,384]{1,0:T(8,128)(2,1)} %all-gather.4.cloned.1.call-done), channel_id=1, source_target_pairs={{0,16},{4,20},{8,24},{12,28},{16,0},{20,4},{24,8},{28,12},{1,17},{... | collective-permute-start | bytes 5455880 | tf_op jit(solution)/shard_map/ppermute | solution.py:393
  130.8 635.3 %reduce-scatter.5.cloned.1.call-start = ((), (), s32[]{:S(2)}) async-start(), calls=%async_computation.7 | async-start | bytes 1966080 | tf_op jit(solution)/shard_map/reduce_scatter | solution.py:475
  174.2 120.5 %collective-permute-start.12 = (bf16[2048,384]{1,0:T(8,128)(2,1)S(1)}, bf16[2048,384]{1,0:T(8,128)(2,1)S(1)}, u32[]{:S(2)}, u32[]{:S(2)}) collective-permute-start(bf16[2048,384]{1,0:T(8,128)(2,1)S(1)} %bitcast.198), channel_id=1, source_target_pairs={{0,8},{4,12},{8,0},{12,4},{16,24},{20,28},{24,16},{28,20},{1,9},{5... | collective-permute-start | bytes 4718600 | tf_op jit(solution)/shard_map/ppermute | solution.py:393
  175.7 118.9 %collective-permute-start.13 = (bf16[2048,384]{1,0:T(8,128)(2,1)S(1)}, bf16[2048,384]{1,0:T(8,128)(2,1)}, u32[]{:S(2)}, u32[]{:S(2)}) collective-permute-start(bf16[2048,384]{1,0:T(8,128)(2,1)S(1)} %bitcast.199), channel_id=1, source_target_pairs={{0,16},{4,20},{8,24},{12,28},{16,0},{20,4},{24,8},{28,12},{1,17},{... | collective-permute-start | bytes 4718600 | tf_op jit(solution)/shard_map/ppermute | solution.py:393
  214.1 114.2 %collective-permute-start.21 = (bf16[4096,384]{1,0:T(8,128)(2,1)}, bf16[4096,384]{1,0:T(8,128)(2,1)}, u32[]{:S(2)}, u32[]{:S(2)}) collective-permute-start(bf16[4096,384]{1,0:T(8,128)(2,1)} %all-gather.8.cloned.1.call-done.refs_0_.refs_1_), channel_id=1, source_target_pairs={{0,8},{4,12},{8,0},{12,4},{16,24},{20,28},{24,16},{28,20},{1,9},{5... | collective-permute-start | bytes 9437192 | tf_op jit(solution)/shard_map/ppermute | solution.py:393
  215.6 128.2 %collective-permute-start.22 = (bf16[4096,384]{1,0:T(8,128)(2,1)}, bf16[4096,384]{1,0:T(8,128)(2,1)}, u32[]{:S(2)}, u32[]{:S(2)}) collective-permute-start(bf16[4096,384]{1,0:T(8,128)(2,1)} %all-gather.8.cloned.1.call-done.refs_0_.refs_1_), channel_id=1, source_target_pairs={{0,16},{4,20},{8,24},{12,28},{16,0},{20,4},{24,8},{28,12},{1,17},{... | collective-permute-start | bytes 9437192 | tf_op jit(solution)/shard_map/ppermute | solution.py:393
  227.1 65.7 %collective-permute-start.14 = (bf16[384,384]{1,0:T(8,128)(2,1)S(1)}, bf16[384,384]{1,0:T(8,128)(2,1)S(1)}, u32[]{:S(2)}, u32[]{:S(2)}) collective-permute-start(bf16[384,384]{1,0:T(8,128)(2,1)S(1)} %slice.345), channel_id=1, source_target_pairs={{0,16},{4,20},{8,24},{12,28},{16,0},{20,4},{24,8},{28,12},{1,17},{... | collective-permute-start | bytes 884744 | tf_op jit(solution)/shard_map/ppermute | solution.py:393
  514.7 101.2 %collective-permute-start.34 = (bf16[2048,384]{1,0:T(8,128)(2,1)}, bf16[2048,384]{1,0:T(8,128)(2,1)}, u32[]{:S(2)}, u32[]{:S(2)}) collective-permute-start(bf16[2048,384]{1,0:T(8,128)(2,1)} %convolution_convert_fusion.1), channel_id=1, source_target_pairs={{0,8},{4,12},{8,0},{12,4},{16,24},{20,28},{24,16},{28,20},{1,9},{5... | collective-permute-start | bytes 4718600 | tf_op jit(solution)/shard_map/ppermute | solution.py:393
  516.0 102.5 %collective-permute-start.35 = (bf16[2048,384]{1,0:T(8,128)(2,1)}, bf16[2048,384]{1,0:T(8,128)(2,1)}, u32[]{:S(2)}, u32[]{:S(2)}) collective-permute-start(bf16[2048,384]{1,0:T(8,128)(2,1)} %convolution_convert_fusion), channel_id=1, source_target_pairs={{0,16},{4,20},{8,24},{12,28},{16,0},{20,4},{24,8},{28,12},{1,17},{... | collective-permute-start | bytes 4718600 | tf_op jit(solution)/shard_map/ppermute | solution.py:393
  647.8 187.8 %reduce-scatter.7.cloned.1.call-start = ((), (), s32[]{:S(2)}) async-start(), calls=%async_computation.8 | async-start | bytes 3932160 | tf_op jit(solution)/shard_map/reduce_scatter | solution.py:475
  715.2 51.1 %collective-permute-start.53 = (bf16[1184,384]{1,0:T(8,128)(2,1)}, bf16[1184,384]{1,0:T(8,128)(2,1)}, u32[]{:S(2)}, u32[]{:S(2)}) collective-permute-start(bf16[1184,384]{1,0:T(8,128)(2,1)} %pad_maximum_fusion.18), channel_id=1, source_target_pairs={{0,8},{4,12},{8,0},{12,4},{16,24},{20,28},{24,16},{28,20},{1,9},{5... | collective-permute-start | bytes 2727944 | tf_op jit(solution)/shard_map/ppermute | solution.py:393
  750.2 70.2 %collective-permute-start.50 = (bf16[512,1536]{1,0:T(8,128)(2,1)}, bf16[512,1536]{1,0:T(8,128)(2,1)}, u32[]{:S(2)}, u32[]{:S(2)}) collective-permute-start(bf16[512,1536]{1,0:T(8,128)(2,1)} %get-tuple-element.222), channel_id=1, source_target_pairs={{0,4},{4,0},{8,12},{12,8},{16,20},{20,16},{24,28},{28,24},{1,5},{5... | collective-permute-start | bytes 4718600 | tf_op jit(solution)/shard_map/ppermute | solution.py:389
  766.2 94.4 %reduce-scatter.9.cloned.1.call-start = ((), (), s32[]{:S(2)}) async-start(), calls=%async_computation.9 | async-start | bytes 737280 | tf_op jit(solution)/shard_map/reduce_scatter | solution.py:475
  824.8 110.0 %collective-permute-start.51 = (bf16[256,1536]{1,0:T(8,128)(2,1)S(1)}, bf16[256,1536]{1,0:T(8,128)(2,1)}, u32[]{:S(2)}, u32[]{:S(2)}) collective-permute-start(bf16[256,1536]{1,0:T(8,128)(2,1)S(1)} %pad_maximum_fusion.26), channel_id=1, source_target_pairs={{0,0},{2,1},{4,2},{6,3},{1,4},{3,5},{5,6},{7,7},{8,8},{10,9},{12,1... | collective-permute-start | bytes 2359304 | tf_op jit(solution)/shard_map/ppermute | solution.py:433
  826.5 108.3 %collective-permute-start.52 = (bf16[256,1536]{1,0:T(8,128)(2,1)S(1)}, bf16[256,1536]{1,0:T(8,128)(2,1)}, u32[]{:S(2)}, u32[]{:S(2)}) collective-permute-start(bf16[256,1536]{1,0:T(8,128)(2,1)S(1)} %pad_maximum_fusion.27), channel_id=1, source_target_pairs={{2,0},{0,1},{6,2},{4,3},{3,4},{1,5},{7,6},{5,7},{10,8},{8,9},{14,1... | collective-permute-start | bytes 2359304 | tf_op jit(solution)/shard_map/ppermute | solution.py:433
  835.6 112.1 %reduce-scatter.11.cloned.1.call-start = ((), (), s32[]{:S(2)}) async-start(), calls=%async_computation.10 | async-start | bytes 2273280 | tf_op jit(solution)/shard_map/reduce_scatter | solution.py:475
  860.7 77.2 %collective-permute-start.56 = (bf16[256,1536]{1,0:T(8,128)(2,1)S(1)}, bf16[256,1536]{1,0:T(8,128)(2,1)S(1)}, u32[]{:S(2)}, u32[]{:S(2)}) collective-permute-start(bf16[256,1536]{1,0:T(8,128)(2,1)S(1)} %pad_maximum_fusion.28), channel_id=1, source_target_pairs={{0,0},{2,1},{4,2},{6,3},{1,4},{3,5},{5,6},{7,7},{8,8},{10,9},{12,1... | collective-permute-start | bytes 2359304 | tf_op jit(solution)/shard_map/ppermute | solution.py:433
  861.5 72.2 %collective-permute-start.62 = (f32[3096]{0:T(1024)S(1)}, f32[3096]{0:T(1024)S(1)}, u32[]{:S(2)}, u32[]{:S(2)}) collective-permute-start(f32[3096]{0:T(1024)S(1)} %add.440), channel_id=1, source_target_pairs={{0,2},{1,3},{2,0},{3,1},{4,6},{5,7},{6,4},{7,5},{8,10},{9,11},{10,... | collective-permute-start | bytes 37160 | tf_op jit(solution)/shard_map/ppermute | solution.py:491
  873.2 68.9 %collective-permute-start.57 = (bf16[256,1536]{1,0:T(8,128)(2,1)S(1)}, bf16[256,1536]{1,0:T(8,128)(2,1)S(1)}, u32[]{:S(2)}, u32[]{:S(2)}) collective-permute-start(bf16[256,1536]{1,0:T(8,128)(2,1)S(1)} %pad_maximum_fusion.29), channel_id=1, source_target_pairs={{2,0},{0,1},{6,2},{4,3},{3,4},{1,5},{7,6},{5,7},{10,8},{8,9},{14,1... | collective-permute-start | bytes 2359304 | tf_op jit(solution)/shard_map/ppermute | solution.py:433
  (145 other events, 2398.3 us)
Sparse Core Ops, SparseCore 0:
  14.2 43.6 all-gather.3
  60.0 71.2 all-gather.5
  133.5 64.3 all-gather.7
  647.9 37.9 reduce-scatter.4
  766.3 62.9 reduce-scatter.6
  835.8 24.8 reduce-scatter.8
  862.9 67.0 reduce-scatter.10

commit v4 on v3

--- a/solution.py
+++ b/solution.py
@@ -90,25 +90,20 @@
         o_ref[lo:hi, :] = jnp.where(pos < length, o, 0.0).astype(BF16)
         l_ref[lo:hi, :] = jnp.where(lane_b < hd, got[0][1], got[1][1])
 
-def third(rows, pairs, n):
-    return pl.BlockSpec((rows, 128), lambda p: (0, n * pairs + p))
-
-
-def attn_fwd(length, qkv, c, blk=256):
-    rows, cols = qkv.shape[0], qkv.shape[1] // 3
+def attn_fwd(length, q, k, v, c, blk=256):
+    rows, cols = q.shape
     pairs = cols // 128
     spec = pl.BlockSpec((rows, 128), lambda p: (0, p))
     return pl.pallas_call(
         functools.partial(attn_fwd_kernel, blk=blk),
         grid=(pairs,),
-        in_specs=[pl.BlockSpec(memory_space=pltpu.SMEM)]
-        + [third(rows, pairs, n) for n in range(3)]
-        + [pl.BlockSpec((1, rows, 2), lambda p: (p, 0, 0))],
+        in_specs=[pl.BlockSpec(memory_space=pltpu.SMEM), spec, spec, spec,
+                  pl.BlockSpec((1, rows, 2), lambda p: (p, 0, 0))],
         out_specs=[spec, spec],
         out_shape=[jax.ShapeDtypeStruct((rows, cols), BF16), jax.ShapeDtypeStruct((rows, cols), F32)],
         compiler_params=pltpu.CompilerParams(vmem_limit_bytes=VMEM_BYTES),
         cost_estimate=pl.CostEstimate(flops=rows*rows*128*4*pairs*2, bytes_accessed=rows*cols*12, transcendentals=rows*rows*pairs),
-    )(length, qkv, qkv, qkv, c)
+    )(length, q, k, v, c)
 
 def attn_bwd_kernel(len_ref, q_ref, k_ref, v_ref, c_ref, l_ref, o_ref, g_ref, dq_ref, dk_ref, dv_ref, dc_ref, acc_k, acc_v, *, blk):
     rows, wide = q_ref.shape
@@ -166,23 +161,22 @@
     dv_ref[...] = jnp.where(first, res[0][2], res[1][2]).astype(BF16)
     dc_ref[...] = jnp.where(first, res[1][3], res[0][3])
 
-def attn_bwd(length, qkv, c, l, o, g, blk=256):
-    rows, cols = o.shape
+def attn_bwd(length, q, k, v, c, l, o, g, blk=256):
+    rows, cols = q.shape
     pairs = cols // 128
     spec = pl.BlockSpec((rows, 128), lambda p: (0, p))
     low = jax.ShapeDtypeStruct((rows, cols), BF16)
     dq, dk, dv, dc = pl.pallas_call(
         functools.partial(attn_bwd_kernel, blk=blk),
         grid=(pairs,),
-        in_specs=[pl.BlockSpec(memory_space=pltpu.SMEM)]
-        + [third(rows, pairs, n) for n in range(3)]
-        + [pl.BlockSpec((1, rows, 2), lambda p: (p, 0, 0)), spec, spec, spec],
+        in_specs=[pl.BlockSpec(memory_space=pltpu.SMEM), spec, spec, spec,
+                  pl.BlockSpec((1, rows, 2), lambda p: (p, 0, 0)), spec, spec, spec],
         out_specs=[spec]*4,
         out_shape=[low, low, low, jax.ShapeDtypeStruct((rows, cols), F32)],
         scratch_shapes=[pltpu.VMEM((rows, 128), F32)]*2,
         compiler_params=pltpu.CompilerParams(vmem_limit_bytes=VMEM_BYTES),
         cost_estimate=pl.CostEstimate(flops=rows*rows*128*10*pairs*2, bytes_accessed=rows*cols*24, transcendentals=rows*rows*pairs),
-    )(length, qkv, qkv, qkv, c, l, o, g)
+    )(length, q, k, v, c, l, o, g)
     d3 = dc.reshape(rows, pairs, 128)
     grad_cumul = jnp.stack([d3[:, :, 67], d3[:, :, 3]], axis=2).reshape(rows, 2 * pairs)
     return dq, dk, dv, grad_cumul
@@ -203,39 +197,36 @@
     return jnp.concatenate([r[lo:hi, :] for r in refs], axis=1)
 
 
-def project_kernel(x_ref, *refs):
-    pieces_here = (len(refs) - 2) // 2
-    w_refs, f_refs, (out_ref, f_ref) = refs[:pieces_here], refs[pieces_here:-2], refs[-2:]
-    out_ref[...] = nt(x_ref[...], joined(w_refs)).astype(BF16)
-
-    @pl.when(pl.program_id(0) == 0)
-    def _():
-        f_ref[...] = nt(x_ref[...], joined(f_refs))
-
-
-def project(x, weights, few):
+def project_kernel(x_ref, *refs, shard):
+    w_refs, (q_ref, k_ref, v_ref, f_ref) = refs[:-4], refs[-4:]
+    step = w_refs[0].shape[0] // 2
+    x = x_ref[...]
+    for kind, out in enumerate((q_ref, k_ref, v_ref)):
+        rows = [joined(w_refs, t * step + kind * shard, t * step + (kind + 1) * shard) for t in range(2)]
+        out[...] = nt(x, jnp.concatenate(rows, axis=0)).astype(BF16)
+    rows = [joined(w_refs, t * step + 3 * shard, (t + 1) * step) for t in range(2)]
+    f_ref[0] = nt(x, jnp.concatenate(rows, axis=0))
+
+
+def project(x, weights, shard, few):
     rows = x.shape[0]
-    extra = 4 * FORGET_PAD
-    cols = (weights[0].shape[0] - extra) // 3
-    outs = [
-        jax.ShapeDtypeStruct((rows, 3 * cols), BF16),
-        jax.ShapeDtypeStruct((rows, extra), F32),
-    ]
-    last = 3 * cols // extra
-    qkv, f = pl.pallas_call(
-        project_kernel,
-        grid=(3,),
+    step = weights[0].shape[0] // 2
+    low = jax.ShapeDtypeStruct((rows, 4 * shard), BF16)
+    spec = pl.BlockSpec((rows, 2 * shard), lambda i: (0, i))
+    pad = step // 2 - 3 * shard
+    q, k, v, f = pl.pallas_call(
+        functools.partial(project_kernel, shard=shard),
+        grid=(2,),
         in_specs=[whole(x)]
-        + [pl.BlockSpec((cols, w.shape[1]), lambda i: (i, 0)) for w in weights]
-        + [pl.BlockSpec((extra, w.shape[1]), lambda i: (last, 0)) for w in weights],
-        out_specs=[pl.BlockSpec((rows, cols), lambda i: (0, i)), whole(outs[1])],
-        out_shape=outs,
+        + [pl.BlockSpec((step, w.shape[1]), lambda i: (i, 0)) for w in weights],
+        out_specs=[spec, spec, spec, pl.BlockSpec((1, rows, 2 * pad), lambda i: (i, 0, 0))],
+        out_shape=[low, low, low, jax.ShapeDtypeStruct((2, rows, 2 * pad), F32)],
         compiler_params=pltpu.CompilerParams(vmem_limit_bytes=VMEM_BYTES),
-        cost_estimate=cost(2 * rows * x.shape[1] * 3 * cols, [x, *weights, *outs]),
+        cost_estimate=cost(2 * rows * x.shape[1] * 4 * step // 2, [x, *weights, low, low, low]),
         name="project",
-    )(x, *weights, *weights)
-    logits = f.reshape(rows, 4, FORGET_PAD)[..., :few].reshape(rows, 4 * few)
-    return qkv, logits
+    )(x, *weights)
+    logits = f.reshape(2, rows, 2, pad)[..., :few].transpose(1, 0, 2, 3).reshape(rows, 4 * few)
+    return q, k, v, logits
 
 
 def combine_kernel(core_ref, *refs, lefts):
@@ -640,8 +631,10 @@
         parts = [piece[:, a:b].reshape(-1, piece.shape[-1]) for a, b in zip(edges, edges[1:])]
         return jnp.concatenate(parts, axis=0)
 
-    full_one = [by_kind(piece) for piece in plan.far_gather(plan.near_gather(line_one))]
-    rows_in = plan.to_chip(inputs).astype(F32)
+    full_one = plan.far_gather(plan.near_gather(line_one))
+    rows_in = plan.to_chip(inputs)
+    rows_in, full_one = together(rows_in, full_one)
+    rows_in = rows_in.astype(F32)
     line_mid = plan.line_gather(
         jnp.concatenate([split_rows(w_out), split_rows(w_down)], axis=1)
     )
@@ -671,22 +664,26 @@
 
     scale_one = row_scale(rows_in)
     normed_one = plan.both_rows((rows_in * scale_one * gain_one).astype(BF16))
-    qkv, logits = project(normed_one, full_one, heads_shard)
+    queries, key_rows, value_rows, logits = project(
+        normed_one, full_one, shard_cols, heads_shard
+    )
     forget_logit = logits + bias_here
     cumul_gate = jnp.cumsum(jax.nn.log_sigmoid(forget_logit), axis=0)
     gate_pairs = cumul_gate.reshape(seq_rows, heads_here // 2, 2).transpose(1, 0, 2)
     near_out, gate_pairs = together(near_out, gate_pairs)
-    full_out = plan.far_gather(near_out)
-    mixed_low, log_total = attn_fwd(count, qkv, gate_pairs)
-    mixed_low, out_grad, near_down, full_out = together(mixed_low, out_grad, near_down, full_out)
+    full_out, line_two, gate_pairs = together(plan.far_gather(near_out), line_two, gate_pairs)
+    mixed_low, log_total = attn_fwd(count, queries, key_rows, value_rows, gate_pairs)
+    mixed_low, near_down, full_one = together(mixed_low, near_down, full_one)
+    kinds_one = [by_kind(piece) for piece in full_one]
     full_down = plan.far_gather(near_down)
-    full_two = plan.far_gather(plan.near_gather(line_two))
+    near_two, out_grad = together(plan.near_gather(line_two), out_grad)
+    full_two = plan.far_gather(near_two)
     cotangent = plan.to_chip(out_grad).astype(F32)
     hidden_in = rows_in + plan.sum_rows(*combine(core, [mixed_low], full_out))
 
     scale_two = row_scale(hidden_in)
     normed_two = plan.both_rows((hidden_in * scale_two * gain_two).astype(BF16))
-    normed_two, full_down = together(normed_two, full_down)
+    normed_two, full_down, kinds_one = together(normed_two, full_down, kinds_one)
     gate_pre, up_pre, inner_low = inner_units(normed_two, full_two)
     grad_ffn = plan.both_rows((valid_here * cotangent).astype(BF16))
     down_sum = Reduction(plan, [inner_low], grad_ffn)
@@ -701,9 +698,12 @@
     two_sum.send_first()
     down_sum.prepare_second()
     give_two, keep_two = combine(core, [grad_pre], full_two)
-    two_far, down_sum.second, give_two = together(two_sum.got[:2], down_sum.second, give_two)
+    give_ffn, keep_ffn = combine(core, [inner_low], full_down)
+    down_sum.send_second()
+    two_far, down_sum.last, give_two, give_ffn = together(
+        two_sum.got[:2], down_sum.last, give_two, give_ffn
+    )
     two_sum.got = [*two_far, *two_sum.got[2:]]
-    down_sum.send_second()
     grad_normed_two = plan.sum_rows(give_two, keep_two)
     gain_two_term = jnp.sum(grad_normed_two * hidden_in * scale_two, axis=0)
     grad_hidden = valid_here * cotangent + norm_back(
@@ -712,21 +712,25 @@
 
     grad_attn = plan.both_rows(grad_hidden.astype(BF16))
     out_sum = Reduction(plan, [mixed_low], grad_attn)
-    out_sum.first, down_sum.last, grad_attn = together(out_sum.first, down_sum.last, grad_attn)
+    two_sum.prepare_second()
+    out_sum.first, two_sum.second, grad_attn = together(
+        out_sum.first, two_sum.second, grad_attn
+    )
+    two_sum.send_second()
     out_sum.send_first()
+    ffn_rows = plan.sum_rows(give_ffn, keep_ffn)
+    outputs = (valid_here * (hidden_in + ffn_rows)).astype(BF16)
     grad_mixed = spread(count, grad_attn, full_out)
     query_low, key_low, value_low, grad_cumul = attn_bwd(
-        count, qkv, gate_pairs, log_total, mixed_low, grad_mixed
-    )
-    two_sum.got, out_sum.got, query_low = together(two_sum.got, out_sum.got, query_low)
-    two_sum.prepare_second()
+        count, queries, key_rows, value_rows, gate_pairs, log_total, mixed_low, grad_mixed
+    )
+    two_sum.got, two_sum.last, out_sum.got, query_low, key_low, value_low, grad_cumul = together(
+        two_sum.got, two_sum.last, out_sum.got, query_low, key_low, value_low, grad_cumul
+    )
     out_sum.prepare_second()
-    two_sum.second, out_sum.second, query_low, key_low, value_low, grad_cumul = together(
-        two_sum.second, out_sum.second, query_low, key_low, value_low, grad_cumul
-    )
-    two_sum.send_second()
+    out_sum.second, outputs, grad_cumul = together(out_sum.second, outputs, grad_cumul)
+    outputs = plan.from_chip(outputs)
     out_sum.send_second()
-    down_pair = plan.scatter(down_sum.finish())
     grad_logf = jnp.flip(jnp.cumsum(jnp.flip(grad_cumul, 0), axis=0), 0)
     grad_logit = grad_logf * jax.nn.sigmoid(-forget_logit)
     bias_term = jnp.sum(grad_logit, axis=0)
@@ -735,32 +739,21 @@
         ((0, 0), (0, 0), (0, FORGET_PAD - heads_shard)),
     ).reshape(seq_rows, -1)
     grad_one = [query_low, key_low, value_low, logit_low]
-    grad_one, two_sum.last, out_sum.last = together(grad_one, two_sum.last, out_sum.last)
     one_sum = Reduction(plan, grad_one, normed_one)
+    one_sum.first, out_sum.last = together(one_sum.first, out_sum.last)
     one_sum.send_first()
-    one_far, two_sum.last, out_sum.last, inner_low = together(
-        one_sum.got[:2], two_sum.last, out_sum.last, inner_low
-    )
-    ffn_rows = plan.sum_rows(*combine(core, [inner_low], full_down))
-    outputs = plan.from_chip((valid_here * (hidden_in + ffn_rows)).astype(BF16))
+    one_far, grad_one = together(one_sum.got[:2], grad_one)
     one_sum.got = [*one_far, *one_sum.got[2:]]
-    two_total, down_pair = together(two_sum.finish(), down_pair)
+    down_pair = plan.scatter(down_sum.finish())
+    two_total, down_pair, outputs = together(two_sum.finish(), down_pair, outputs)
     two_pair = plan.scatter(two_total)
-    one_sum.got, two_total = together(one_sum.got, two_total)
-    one_sum.prepare_second()
-    one_sum.second, grad_one = together(one_sum.second, grad_one)
-    one_sum.send_second()
-    out_total, two_pair = together(out_sum.finish(), two_pair)
-    out_pair = plan.scatter(out_total)
-    one_total, out_pair = together(one_sum.finish(), out_pair)
-    one_pair = plan.scatter(one_total)
-    down_shard, two_shard = plan.share(down_pair), plan.share(two_pair)
-    out_shard, one_shard = plan.share(out_pair), plan.share(one_pair)
-    grad_normed_one = plan.sum_rows(*combine(core, grad_one, full_one))
+    grad_normed_one = plan.sum_rows(*combine(core, grad_one, kinds_one))
     gain_one_term = jnp.sum(grad_normed_one * rows_in * scale_one, axis=0)
     input_grad = plan.from_chip(
         (grad_hidden + norm_back(rows_in, scale_one, gain_one, grad_normed_one)).astype(BF16)
     )
+    one_sum.prepare_second()
+    one_sum.send_second()
 
     bias_full = jnp.where(
         (jnp.arange(2) == core)[None, :, None], bias_term.reshape(4, 1, heads_shard), 0.0
@@ -769,6 +762,13 @@
     small = plan.sum_all(
         jnp.concatenate([plan.by_chip(gain_one_term), plan.by_chip(gain_two_term), bias_full])
     )
+
+    out_total, two_pair = together(out_sum.finish(), two_pair)
+    out_pair = plan.scatter(out_total)
+    one_total, out_pair, input_grad = together(one_sum.finish(), out_pair, input_grad)
+    one_pair = plan.scatter(one_total)
+    down_shard, two_shard = plan.share(down_pair), plan.share(two_pair)
+    out_shard, one_shard = plan.share(out_pair), plan.share(one_pair)
 
     two_shard = two_shard.reshape(2, blocks, 2, UNIT_BLOCK, -1)
 

time: 971 us -> 857 us (0.88)
  waiting for transfers between devices: 334 us -> 271 us
  other arithmetic: 128 us -> 95.1 us
  starting transfers between devices: 124 us -> 102 us
    ppermute x2, waiting for transfers between devices: 59.3 us -> 8.68 us  [sum_all(): vector = vector + lax.ppermute(vector, 'tensor', perm)]
    ppermute x42, waiting for transfers between devices: 179 us -> 132 us  [swap_chip(): return lax.ppermute(array, 'dp', perm)]
    ppermute x4, waiting for transfers between devices: 4.18 us -> 50.8 us  [from_chip(): got.append(lax.ppermute(self.by_chip(part), ('dp', 'tensor'), back))]
    ppermute x4, waiting for transfers between devices: 34.6 us -> 21.6 us  [to_chip(): lax.ppermute(self.by_chip(part), ('dp', 'tensor'), self.route(turn))]
    concatenate x2 -> x4, other arithmetic: 18.3 us -> 5.69 us  [by_kind(): return jnp.concatenate(parts, axis=0)]
    another operation x6, other arithmetic: 19.5 us -> 7 us
    ppermute x17, starting transfers between devices: 45.5 us -> 33.2 us  [swap_core(): return lax.ppermute(array, 'dp', self.core_perm)]
    ppermute x2, starting transfers between devices: 11.6 us -> 0.01 us  [sum_all(): vector = vector + lax.ppermute(vector, 'tensor', perm)]
  transfers between devices with their start and end apart: 76 -> 76, of which waited for: 29 -> 26; matrix products, arithmetic and copies ran while one was open for 26% -> 28% of each run, Pallas kernels for 17% -> 22%
where the time goes in v4:
time: 857 us; the launch traced here: 846 us
  waiting for transfers between devices  271 us (32%)
  Pallas kernels  185 us (22%)
  matrix products  105 us (12%)
  starting transfers between devices  102 us (12%)
  other arithmetic  95.1 us (11%)
  local copies, waits for them, and re-layouts  71.5 us (8%)
  between operations  16.5 us (2%)
    ppermute x42, waiting for transfers between devices, swap_chip(): return lax.ppermute(array, 'dp', perm)  132 us
    dot_general x56, matrix products, dot_first(): lax.dot_general(left, right, (((0,), (0,)), ((), ())), preferred_element_...  105 us
    pallas_call x4, Pallas kernels, combine(): pl.pallas_call(functools.partial(combine_kernel, lefts=len(lefts)), grid_...  64.7 us
    ppermute x4, waiting for transfers between devices, from_chip(): got.append(lax.ppermute(self.by_chip(part), ('dp', 'tensor'), back))  50.8 us
    ppermute x42, starting transfers between devices, swap_chip(): return lax.ppermute(array, 'dp', perm)  46.4 us
    all_gather x3, waiting for transfers between devices, line_gather(): return lax.all_gather(pair, 'tensor', axis=0, tiled=True)  37.7 us
    ppermute x17, starting transfers between devices, swap_core(): return lax.ppermute(array, 'dp', self.core_perm)  33.2 us
    pallas_call x1, Pallas kernels, attn_bwd(): pl.pallas_call(functools.partial(attn_bwd_kernel, blk=blk), grid=(pairs,)...  32.9 us
  transfers between devices with their start and end apart: 76, of which 26 were waited for; matrix products, arithmetic and copies ran while one was open for 28% of the time, Pallas kernels for 22%

profile of v4, /device:TPU:0, one launch (start us, length us, event | category | flops | bytes accessed | tf_op | source)
XLA Modules:
  0.0 845.9 jit_solution(8792084072133623892)
XLA Ops:
  20.2 37.7 %all-gather.4.cloned.1.call-done.refs_0_ = bf16[2368,384]{1,0:T(8,128)(2,1)} async-done(((bf16[592,384]{1,0:T(8,128)(2,1)}), bf16[2368,384]{1,0:T(8,128)(2,1)}) %all-gather.4.cloned.1.call-update) | async-done | bytes 1818640 | tf_op jit(solution)/shard_map/all_gather | solution.py:446
  69.4 7.4 collective-permute-start.1
  79.1 20.1 %collective-permute-done.4.refs_2_ = bf16[2368,384]{1,0:T(8,128)(2,1)S(1)} collective-permute-done((bf16[2368,384]{1,0:T(8,128)(2,1)}, bf16[2368,384]{1,0:T(8,128)(2,1)S(1)}, u32[]{:S(2)}, u32[]{:S(2)}) %collective-permute-start.4) | collective-permute-done | bytes 1818656 | tf_op jit(solution)/shard_map/ppermute | solution.py:384
  129.1 15.8 %collective-permute-start.8 = (bf16[512,1536]{1,0:T(8,128)(2,1)S(1)}, bf16[512,1536]{1,0:T(8,128)(2,1)}, u32[]{:S(2)}, u32[]{:S(2)}) collective-permute-start(bf16[512,1536]{1,0:T(8,128)(2,1)S(1)} %fusion.2), channel_id=1, source_target_pairs={{0,4},{4,0},{8,12},{12,8},{16,20},{20,16},{24,28},{28,24},{1,5},{5... | collective-permute-start | bytes 4718600 | tf_op jit(solution)/shard_map/ppermute | solution.py:380
  164.1 16.4 %project.1 = (bf16[1024,768]{1,0:T(8,128)(2,1)}, bf16[1024,768]{1,0:T(8,128)(2,1)}, bf16[1024,768]{1,0:T(8,128)(2,1)}, f32[2,1024,32]{2,1,0:T(8,128)}) custom-call(bf16[1024,1536]{1,0:T(8,128)(2,1)} %pad_maximum_fusion.x_ref, bf16[2368,384]{1,0:T(8,128)(2,1)} %all-gather.4.cloned.1.call-done.refs_0_, bf16[2368,384]{1,0:T(8,128)(2,1)} %collective-permute-done.3.refs_1_, ...), custom_call_target="tpu_custom_call" | custom-call | flops 7449083904 | bytes 15138816 | tf_op jit(solution)/shard_map/project/pallas_call | solution.py:217
  195.9 11.9 %collective-permute-done.13 = bf16[384,384]{1,0:T(8,128)(2,1)S(1)} collective-permute-done((bf16[384,384]{1,0:T(8,128)(2,1)S(1)}, bf16[384,384]{1,0:T(8,128)(2,1)S(1)}, u32[]{:S(2)}, u32[]{:S(2)}) %collective-permute-start.13) | collective-permute-done | bytes 294944 | tf_op jit(solution)/shard_map/ppermute | solution.py:384
  211.9 25.1 %shard_map.246 = (bf16[1024,768]{1,0:T(8,128)(2,1)}, f32[1024,768]{1,0:T(8,128)}) custom-call(s32[1]{0:T(128)} %bitcast.18.len_ref, bf16[1024,768]{1,0:T(8,128)(2,1)} %get-tuple-element.154.q_ref, bf16[1024,768]{1,0:T(8,128)(2,1)} %get-tuple-element.155.k_ref, bf16[1024,768]{1,0:T(8,128)(2,1)} %get-tuple-element.156.v_ref, f32[6,1024,2]{2,1,0:T(8,128)} %bitcast.216), custom_call_target="tpu_custom_call" | custom-call | flops 6442450944 | bytes 9437184 | tf_op jit(solution)/shard_map/pallas_call | solution.py:97
  237.1 8.0 combine.4
  261.6 34.7 %collective-permute-done.20 = bf16[1024,384]{1,0:T(8,128)(2,1)S(1)} collective-permute-done((bf16[1024,384]{1,0:T(8,128)(2,1)S(1)}, bf16[1024,384]{1,0:T(8,128)(2,1)S(1)}, u32[]{:S(2)}, u32[]{:S(2)}) %collective-permute-start.20) | collective-permute-done | bytes 786464 | tf_op jit(solution)/shard_map/ppermute | solution.py:384
  309.9 15.3 %collective-permute-done.26 = bf16[256,1536]{1,0:T(8,128)(2,1)S(1)} collective-permute-done((bf16[256,1536]{1,0:T(8,128)(2,1)S(1)}, bf16[256,1536]{1,0:T(8,128)(2,1)S(1)}, u32[]{:S(2)}, u32[]{:S(2)}) %collective-permute-start.26) | collective-permute-done | bytes 786464 | tf_op jit(solution)/shard_map/ppermute | solution.py:411
  326.8 14.9 %collective-permute-start.27 = (bf16[512,1536]{1,0:T(8,128)(2,1)}, bf16[512,1536]{1,0:T(8,128)(2,1)}, u32[]{:S(2)}, u32[]{:S(2)}) collective-permute-start(bf16[512,1536]{1,0:T(8,128)(2,1)} %fusion.10), channel_id=1, source_target_pairs={{0,4},{4,0},{8,12},{12,8},{16,20},{20,16},{24,28},{28,24},{1,5},{5... | collective-permute-start | bytes 4718600 | tf_op jit(solution)/shard_map/ppermute | solution.py:380
  344.3 20.6 %inner_units.1 = (f32[1024,2048]{1,0:T(8,128)}, f32[1024,2048]{1,0:T(8,128)}, bf16[1024,2048]{1,0:T(8,128)(2,1)}) custom-call(bf16[1024,1536]{1,0:T(8,128)(2,1)} %pad_maximum_fusion.3.x_ref, bf16[4096,384]{1,0:T(8,128)(2,1)} %all-gather.8.cloned.1.call-done.refs_0_.refs_1_, bf16[4096,384]{1,0:T(8,128)(2,1)} %collective-permute-done.21.refs_1_.refs_2_, ...), custom_call_target="tpu_custom_call" | custom-call | flops 12884901888 | bytes 36700160 | tf_op jit(solution)/shard_map/inner_units/pallas_call | solution.py:326
  364.9 14.1 %combine.6 = (bf16[512,1536]{1,0:T(8,128)(2,1)}, f32[512,1536]{1,0:T(8,128)}) custom-call(s32[1]{0:T(128)} %bitcast.17.core_ref, bf16[1024,2048]{1,0:T(8,128)(2,1)} %get-tuple-element.184.refs_0_, bf16[2048,384]{1,0:T(8,128)(2,1)} %bitcast.32.refs_0_.refs_1_, bf16[2048,384]{1,0:T(8,128)(2,1)} %collective-permute-done.15.refs_1_.refs_2_, ...), custom_call_target="tpu_custom_call" | custom-call | flops 6442450944 | bytes 15204352 | tf_op jit(solution)/shard_map/combine/pallas_call | solution.py:263
  399.4 17.6 %inner_grads.1.refs_0_ = bf16[1024,4096]{1,0:T(8,128)(2,1)} custom-call(bf16[1024,1536]{1,0:T(8,128)(2,1)} %pad_maximum_fusion.1.x_ref, f32[1024,2048]{1,0:T(8,128)} %get-tuple-element.189.gate_ref, f32[1024,2048]{1,0:T(8,128)} %get-tuple-element.190.up_ref, bf16[2048,384]{1,0:T(8,128)(2,1)} %bitcast.32.refs_0_.refs_1_, ...), custom_call_target="tpu_custom_call" | custom-call | flops 6442450944 | bytes 34603008 | tf_op jit(solution)/shard_map/inner_grads/pallas_call | solution.py:353
  444.6 25.6 %combine.5 = (bf16[512,1536]{1,0:T(8,128)(2,1)}, f32[512,1536]{1,0:T(8,128)}) custom-call(s32[1]{0:T(128)} %bitcast.17.core_ref, bf16[1024,4096]{1,0:T(8,128)(2,1)} %inner_grads.1.refs_0_, bf16[4096,384]{1,0:T(8,128)(2,1)} %all-gather.8.cloned.1.call-done.refs_0_.refs_1_, bf16[4096,384]{1,0:T(8,128)(2,1)} %collective-permute-done.21.refs_1_.refs_2_, ...), custom_call_target="tpu_custom_call" | custom-call | flops 12884901888 | bytes 25690112 | tf_op jit(solution)/shard_map/combine/pallas_call | solution.py:263
  470.2 16.5 %collective-permute-done.34 = bf16[1024,384]{1,0:T(8,128)(2,1)} collective-permute-done((bf16[1024,384]{1,0:T(8,128)(2,1)}, bf16[1024,384]{1,0:T(8,128)(2,1)}, u32[]{:S(2)}, u32[]{:S(2)}) %collective-permute-start.34) | collective-permute-done | bytes 786464 | tf_op jit(solution)/shard_map/ppermute | solution.py:384
  541.3 7.5 spread.1.g_ref
  548.8 32.9 %shard_map.247 = (bf16[1024,768]{1,0:T(8,128)(2,1)}, bf16[1024,768]{1,0:T(8,128)(2,1)}, bf16[1024,768]{1,0:T(8,128)(2,1)}, f32[1024,768]{1,0:T(8,128)}) custom-call(s32[1]{0:T(128)} %bitcast.18.len_ref, bf16[1024,768]{1,0:T(8,128)(2,1)} %get-tuple-element.154.q_ref, bf16[1024,768]{1,0:T(8,128)(2,1)} %get-tuple-element.155.k_ref, ...), custom_call_target="tpu_custom_call" | custom-call | flops 16106127360 | bytes 18874368 | tf_op jit(solution)/shard_map/pallas_call | solution.py:169
  644.6 7.5 collective-permute-start.47
  677.3 9.0 %collective-permute-done.48 = bf16[256,1536]{1,0:T(8,128)(2,1)} collective-permute-done((bf16[256,1536]{1,0:T(8,128)(2,1)}, bf16[256,1536]{1,0:T(8,128)(2,1)}, u32[]{:S(2)}, u32[]{:S(2)}) %collective-permute-start.48) | collective-permute-done | bytes 786464 | tf_op jit(solution)/shard_map/ppermute | solution.py:424
  689.4 20.7 %collective-permute-done.51 = bf16[1184,384]{1,0:T(8,128)(2,1)} collective-permute-done((bf16[1184,384]{1,0:T(8,128)(2,1)}, bf16[1184,384]{1,0:T(8,128)(2,1)}, u32[]{:S(2)}, u32[]{:S(2)}) %collective-permute-start.51) | collective-permute-done | bytes 909344 | tf_op jit(solution)/shard_map/ppermute | solution.py:384
  716.4 16.9 %combine.7 = (bf16[512,1536]{1,0:T(8,128)(2,1)}, f32[512,1536]{1,0:T(8,128)}) custom-call(s32[1]{0:T(128)} %bitcast.17.core_ref, bf16[1024,768]{1,0:T(8,128)(2,1)} %get-tuple-element.258.refs_0_, bf16[1024,768]{1,0:T(8,128)(2,1)} %get-tuple-element.259.refs_1_, bf16[1024,768]{1,0:T(8,128)(2,1)} %get-tuple-element.260.refs_2_, ...), custom_call_target="tpu_custom_call" | custom-call | flops 7449083904 | bytes 16842752 | tf_op jit(solution)/shard_map/combine/pallas_call | solution.py:263
  748.9 41.8 %collective-permute-done.59 = bf16[256,1536]{1,0:T(8,128)(2,1)} collective-permute-done((bf16[256,1536]{1,0:T(8,128)(2,1)}, bf16[256,1536]{1,0:T(8,128)(2,1)}, u32[]{:S(2)}, u32[]{:S(2)}) %collective-permute-start.59) | collective-permute-done | bytes 786464 | tf_op jit(solution)/shard_map/ppermute | solution.py:424
  819.4 12.6 %reduce-scatter.11.cloned.1.call-done = bf16[592,384]{1,0:T(8,128)(2,1)} async-done(((bf16[2368,384]{1,0:T(8,128)(2,1)}), bf16[592,384]{1,0:T(8,128)(2,1)}) %reduce-scatter.11.cloned.1.call-update) | async-done | bytes 454672 | tf_op jit(solution)/shard_map/reduce_scatter | solution.py:466
  (576 shorter events, 378.6 us)
Async XLA Ops:
  7.2 50.7 %all-gather.4.cloned.1.call-start = ((), (), s32[]{:S(2)}) async-start(), calls=%async_computation.4 | async-start | bytes 2273280 | tf_op jit(solution)/shard_map/all_gather | solution.py:446
  14.1 136.0 %all-gather.6.cloned.1.call-start = ((), (), s32[]{:S(2)}) async-start(), calls=%async_computation.5 | async-start | bytes 2703360 | tf_op jit(solution)/shard_map/all_gather | solution.py:446
  20.1 189.8 %all-gather.8.cloned.1.call-start = ((), (), s32[]{:S(2)}) async-start(), calls=%async_computation.6 | async-start | bytes 3932160 | tf_op jit(solution)/shard_map/all_gather | solution.py:446
  106.6 582.4 %reduce-scatter.5.cloned.1.call-start = ((), (), s32[]{:S(2)}) async-start(), calls=%async_computation.7 | async-start | bytes 1966080 | tf_op jit(solution)/shard_map/reduce_scatter | solution.py:466
  157.7 79.4 %collective-permute-start.15 = (bf16[2048,384]{1,0:T(8,128)(2,1)}, bf16[2048,384]{1,0:T(8,128)(2,1)}, u32[]{:S(2)}, u32[]{:S(2)}) collective-permute-start(bf16[2048,384]{1,0:T(8,128)(2,1)} %bitcast.32.refs_0_.refs_1_), channel_id=1, source_target_pairs={{0,8},{4,12},{8,0},{12,4},{16,24},{20,28},{24,16},{28,20},{1,9},{5... | collective-permute-start | bytes 4718600 | tf_op jit(solution)/shard_map/ppermute | solution.py:384
  158.3 78.8 %collective-permute-start.16 = (bf16[2048,384]{1,0:T(8,128)(2,1)}, bf16[2048,384]{1,0:T(8,128)(2,1)}, u32[]{:S(2)}, u32[]{:S(2)}) collective-permute-start(bf16[2048,384]{1,0:T(8,128)(2,1)} %bitcast.32.refs_0_.refs_1_), channel_id=1, source_target_pairs={{0,16},{4,20},{8,24},{12,28},{16,0},{20,4},{24,8},{28,12},{1,17},{... | collective-permute-start | bytes 4718600 | tf_op jit(solution)/shard_map/ppermute | solution.py:384
  209.9 87.9 %collective-permute-start.21 = (bf16[4096,384]{1,0:T(8,128)(2,1)}, bf16[4096,384]{1,0:T(8,128)(2,1)}, u32[]{:S(2)}, u32[]{:S(2)}) collective-permute-start(bf16[4096,384]{1,0:T(8,128)(2,1)} %all-gather.8.cloned.1.call-done.refs_0_.refs_1_), channel_id=1, source_target_pairs={{0,8},{4,12},{8,0},{12,4},{16,24},{20,28},{24,16},{28,20},{1,9},{5... | collective-permute-start | bytes 9437192 | tf_op jit(solution)/shard_map/ppermute | solution.py:384
  210.5 87.4 %collective-permute-start.22 = (bf16[4096,384]{1,0:T(8,128)(2,1)}, bf16[4096,384]{1,0:T(8,128)(2,1)}, u32[]{:S(2)}, u32[]{:S(2)}) collective-permute-start(bf16[4096,384]{1,0:T(8,128)(2,1)} %all-gather.8.cloned.1.call-done.refs_0_.refs_1_), channel_id=1, source_target_pairs={{0,16},{4,20},{8,24},{12,28},{16,0},{20,4},{24,8},{28,12},{1,17},{... | collective-permute-start | bytes 9437192 | tf_op jit(solution)/shard_map/ppermute | solution.py:384
  259.9 47.4 %collective-permute-start.18 = (bf16[512,1536]{1,0:T(8,128)(2,1)S(1)}, bf16[512,1536]{1,0:T(8,128)(2,1)S(1)}, u32[]{:S(2)}, u32[]{:S(2)}) collective-permute-start(bf16[512,1536]{1,0:T(8,128)(2,1)S(1)} %multiply_convert_fusion.1), channel_id=1, source_target_pairs={{0,4},{4,0},{8,12},{12,8},{16,20},{20,16},{24,28},{28,24},{1,5},{5... | collective-permute-start | bytes 4718600 | tf_op jit(solution)/shard_map/ppermute | solution.py:380
  326.8 52.3 %collective-permute-start.27 = (bf16[512,1536]{1,0:T(8,128)(2,1)}, bf16[512,1536]{1,0:T(8,128)(2,1)}, u32[]{:S(2)}, u32[]{:S(2)}) collective-permute-start(bf16[512,1536]{1,0:T(8,128)(2,1)} %fusion.10), channel_id=1, source_target_pairs={{0,4},{4,0},{8,12},{12,8},{16,20},{20,16},{24,28},{28,24},{1,5},{5... | collective-permute-start | bytes 4718600 | tf_op jit(solution)/shard_map/ppermute | solution.py:380
  433.9 52.9 %collective-permute-start.32 = (bf16[2048,384]{1,0:T(8,128)(2,1)}, bf16[2048,384]{1,0:T(8,128)(2,1)}, u32[]{:S(2)}, u32[]{:S(2)}) collective-permute-start(bf16[2048,384]{1,0:T(8,128)(2,1)} %convolution_convert_fusion.3), channel_id=1, source_target_pairs={{0,16},{4,20},{8,24},{12,28},{16,0},{20,4},{24,8},{28,12},{1,17},{... | collective-permute-start | bytes 4718600 | tf_op jit(solution)/shard_map/ppermute | solution.py:384
  434.7 52.1 %collective-permute-start.33 = (bf16[2048,384]{1,0:T(8,128)(2,1)}, bf16[2048,384]{1,0:T(8,128)(2,1)}, u32[]{:S(2)}, u32[]{:S(2)}) collective-permute-start(bf16[2048,384]{1,0:T(8,128)(2,1)} %convolution_convert_fusion.2), channel_id=1, source_target_pairs={{0,8},{4,12},{8,0},{12,4},{16,24},{20,28},{24,16},{28,20},{1,9},{5... | collective-permute-start | bytes 4718600 | tf_op jit(solution)/shard_map/ppermute | solution.py:384
  438.8 48.0 %collective-permute-start.34 = (bf16[1024,384]{1,0:T(8,128)(2,1)}, bf16[1024,384]{1,0:T(8,128)(2,1)}, u32[]{:S(2)}, u32[]{:S(2)}) collective-permute-start(bf16[1024,384]{1,0:T(8,128)(2,1)} %add_convert_fusion.7), channel_id=1, source_target_pairs={{0,8},{4,12},{8,0},{12,4},{16,24},{20,28},{24,16},{28,20},{1,9},{5... | collective-permute-start | bytes 2359304 | tf_op jit(solution)/shard_map/ppermute | solution.py:384
  490.1 95.3 %collective-permute-start.36 = (bf16[2048,384]{1,0:T(8,128)(2,1)}, bf16[2048,384]{1,0:T(8,128)(2,1)}, u32[]{:S(2)}, u32[]{:S(2)}) collective-permute-start(bf16[2048,384]{1,0:T(8,128)(2,1)} %convolution_convert_fusion.1), channel_id=1, source_target_pairs={{0,8},{4,12},{8,0},{12,4},{16,24},{20,28},{24,16},{28,20},{1,9},{5... | collective-permute-start | bytes 4718600 | tf_op jit(solution)/shard_map/ppermute | solution.py:384
  490.9 95.2 %collective-permute-start.37 = (bf16[2048,384]{1,0:T(8,128)(2,1)}, bf16[2048,384]{1,0:T(8,128)(2,1)}, u32[]{:S(2)}, u32[]{:S(2)}) collective-permute-start(bf16[2048,384]{1,0:T(8,128)(2,1)} %convolution_convert_fusion), channel_id=1, source_target_pairs={{0,16},{4,20},{8,24},{12,28},{16,0},{20,4},{24,8},{28,12},{1,17},{... | collective-permute-start | bytes 4718600 | tf_op jit(solution)/shard_map/ppermute | solution.py:384
  514.7 233.8 %reduce-scatter.7.cloned.1.call-start = ((), (), s32[]{:S(2)}) async-start(), calls=%async_computation.8 | async-start | bytes 3932160 | tf_op jit(solution)/shard_map/reduce_scatter | solution.py:466
  538.0 61.9 %collective-permute-start.40 = (bf16[2048,384]{1,0:T(8,128)(2,1)}, bf16[2048,384]{1,0:T(8,128)(2,1)}, u32[]{:S(2)}, u32[]{:S(2)}) collective-permute-start(bf16[2048,384]{1,0:T(8,128)(2,1)} %add_convert_fusion.3), channel_id=1, source_target_pairs={{0,8},{4,12},{8,0},{12,4},{16,24},{20,28},{24,16},{28,20},{1,9},{5... | collective-permute-start | bytes 4718600 | tf_op jit(solution)/shard_map/ppermute | solution.py:384
  539.3 60.7 %collective-permute-start.41 = (bf16[2048,384]{1,0:T(8,128)(2,1)}, bf16[2048,384]{1,0:T(8,128)(2,1)}, u32[]{:S(2)}, u32[]{:S(2)}) collective-permute-start(bf16[2048,384]{1,0:T(8,128)(2,1)} %add_convert_fusion.2), channel_id=1, source_target_pairs={{0,16},{4,20},{8,24},{12,28},{16,0},{20,4},{24,8},{28,12},{1,17},{... | collective-permute-start | bytes 4718600 | tf_op jit(solution)/shard_map/ppermute | solution.py:384
  540.0 47.3 %collective-permute-start.42 = (bf16[384,384]{1,0:T(8,128)(2,1)}, bf16[384,384]{1,0:T(8,128)(2,1)}, u32[]{:S(2)}, u32[]{:S(2)}) collective-permute-start(bf16[384,384]{1,0:T(8,128)(2,1)} %convolution_convert_fusion.23), channel_id=1, source_target_pairs={{0,16},{4,20},{8,24},{12,28},{16,0},{20,4},{24,8},{28,12},{1,17},{... | collective-permute-start | bytes 884744 | tf_op jit(solution)/shard_map/ppermute | solution.py:384
  669.0 64.3 %collective-permute-start.54 = (bf16[1184,384]{1,0:T(8,128)(2,1)}, bf16[1184,384]{1,0:T(8,128)(2,1)}, u32[]{:S(2)}, u32[]{:S(2)}) collective-permute-start(bf16[1184,384]{1,0:T(8,128)(2,1)} %pad_maximum_fusion.19), channel_id=1, source_target_pairs={{0,16},{4,20},{8,24},{12,28},{16,0},{20,4},{24,8},{28,12},{1,17},{... | collective-permute-start | bytes 2727944 | tf_op jit(solution)/shard_map/ppermute | solution.py:384
  676.4 59.0 %collective-permute-start.55 = (bf16[1184,384]{1,0:T(8,128)(2,1)}, bf16[1184,384]{1,0:T(8,128)(2,1)}, u32[]{:S(2)}, u32[]{:S(2)}) collective-permute-start(bf16[1184,384]{1,0:T(8,128)(2,1)} %pad_maximum_fusion.18), channel_id=1, source_target_pairs={{0,8},{4,12},{8,0},{12,4},{16,24},{20,28},{24,16},{28,20},{1,9},{5... | collective-permute-start | bytes 2727944 | tf_op jit(solution)/shard_map/ppermute | solution.py:384
  689.1 104.5 %reduce-scatter.9.cloned.1.call-start = ((), (), s32[]{:S(2)}) async-start(), calls=%async_computation.9 | async-start | bytes 737280 | tf_op jit(solution)/shard_map/reduce_scatter | solution.py:466
  746.0 44.8 %collective-permute-start.59 = (bf16[256,1536]{1,0:T(8,128)(2,1)}, bf16[256,1536]{1,0:T(8,128)(2,1)}, u32[]{:S(2)}, u32[]{:S(2)}) collective-permute-start(bf16[256,1536]{1,0:T(8,128)(2,1)} %pad_maximum_fusion.29), channel_id=1, source_target_pairs={{2,0},{0,1},{6,2},{4,3},{3,4},{1,5},{7,6},{5,7},{10,8},{8,9},{14,1... | collective-permute-start | bytes 2359304 | tf_op jit(solution)/shard_map/ppermute | solution.py:424
  748.6 83.4 %reduce-scatter.11.cloned.1.call-start = ((), (), s32[]{:S(2)}) async-start(), calls=%async_computation.10 | async-start | bytes 2273280 | tf_op jit(solution)/shard_map/reduce_scatter | solution.py:466
  (132 other events, 1893.3 us)
Sparse Core Ops, SparseCore 0:
  14.2 43.6 all-gather.3
  59.4 77.5 all-gather.5
  139.2 62.7 all-gather.7
  514.8 37.4 reduce-scatter.4
  689.2 57.1 reduce-scatter.6
  748.7 29.7 reduce-scatter.8
  793.7 38.2 reduce-scatter.10

commit v5 on v4

--- a/solution.py
+++ b/solution.py
@@ -233,18 +233,22 @@
     left_refs, w_refs, (give_ref, keep_ref) = refs[:lefts], refs[lefts:-2], refs[-2:]
     step = pl.program_id(0)
     wide = w_refs[0].shape[1]
-    for out, cond in ((give_ref, step < 2), (keep_ref, step >= 2)):
-
-        @pl.when(cond)
+    for n, w in enumerate(w_refs):
+        got, at = None, 0
+        for left in left_refs:
+            deep = left.shape[1]
+            part = nn(left[...], w[at : at + deep, :])
+            got = part if got is None else got + part
+            at += deep
+        cols = slice(n * wide, (n + 1) * wide)
+
+        @pl.when(step < 2)
         def _():
-            for n, w in enumerate(w_refs):
-                got, at = None, 0
-                for left in left_refs:
-                    deep = left.shape[1]
-                    part = nn(left[...], w[at : at + deep, :])
-                    got = part if got is None else got + part
-                    at += deep
-                out[:, n * wide : (n + 1) * wide] = got.astype(out.dtype)
+            give_ref[:, cols] = got.astype(BF16)
+
+        @pl.when(step >= 2)
+        def _():
+            keep_ref[:, cols] = got
 
 
 def combine(core, lefts, weights):
@@ -363,6 +367,119 @@
     )(x, gate, up, *down)
 
 
+def half_products(left_refs, right, side):
+    parts = []
+    for ref, narrow in left_refs:
+        got = dot_first(ref[...], right)
+        if narrow:
+            few = got.shape[0] // 2
+            got = jnp.where(side == 0, got[:few], got[few:])
+        parts.append(got)
+    return parts
+
+
+def term_kernel(*refs, narrow, side):
+    count = len(narrow)
+    right_ref, add_refs, out_ref = refs[count], refs[count + 1 : -1], refs[-1]
+    at = 0
+    for part in half_products(list(zip(refs[:count], narrow)), right_ref[...], side):
+        rows = slice(at, at + part.shape[0])
+        for add in add_refs:
+            part = part + add[rows, :].astype(F32)
+        out_ref[rows, :] = part.astype(BF16)
+        at += part.shape[0]
+
+
+def left_specs(lefts, steps, block):
+    specs, narrow = [], []
+    for left in lefts:
+        rows, cols = left.shape
+        wide = cols // (2 * steps)
+        narrow.append(wide % 128 != 0)
+        if wide % 128:
+            specs.append(pl.BlockSpec((rows, cols), lambda i: (0, 0)))
+        else:
+            specs.append(pl.BlockSpec((rows, wide), lambda i: (0, block(i))))
+    return specs, tuple(narrow)
+
+
+def chunks_of(lefts):
+    half = lefts[0].shape[1] // 2
+    return max(1, half // 512) if len(lefts) == 1 else 1
+
+
+def term_sum(lefts, right, side, r, wide, adds=()):
+    steps = chunks_of(lefts)
+    half = sum(left.shape[1] for left in lefts) // 2
+    specs, narrow = left_specs(lefts, steps, lambda i: side * steps + i)
+    part = pl.BlockSpec((half // steps, wide), lambda i: (i, 0))
+    out = jax.ShapeDtypeStruct((half, wide), BF16)
+    return pl.pallas_call(
+        functools.partial(term_kernel, narrow=narrow, side=side),
+        grid=(steps,),
+        in_specs=specs
+        + [pl.BlockSpec((right.shape[0], wide), lambda i: (0, r))]
+        + [part] * len(adds),
+        out_specs=part,
+        out_shape=out,
+        compiler_params=pltpu.CompilerParams(vmem_limit_bytes=VMEM_BYTES),
+        cost_estimate=cost(2 * right.shape[0] * half * wide, [*adds, out, out]),
+        name="term_sum",
+    )(*lefts, right, *adds)
+
+
+def total_kernel(*refs, narrow, steps):
+    count = len(narrow)
+    right_ref, tops, lows, out_ref = refs[count], refs[count + 1 : -3], refs[-3:-1], refs[-1]
+    step = pl.program_id(0)
+    side = step // steps
+    parts = half_products(list(zip(refs[:count], narrow)), right_ref[...], side)
+    if count == 1:
+        places = [parts]
+    else:
+        places = [
+            [part[n * (part.shape[0] // 2) : (n + 1) * (part.shape[0] // 2)] for part in parts]
+            for n in range(2)
+        ]
+    for this, adds in ((0, tops), (1, lows)):
+
+        @pl.when(side == this)
+        def _():
+            at = 0
+            for n, place in enumerate(places):
+                off = 0
+                for part, whole_part in zip(place, parts):
+                    few = part.shape[0]
+                    start = off + n * few if count > 1 else 0
+                    got = part
+                    for add in adds:
+                        got = got + add[start : start + few, :].astype(F32)
+                    out_ref[at : at + few, :] = got.astype(BF16)
+                    at += few
+                    off += whole_part.shape[0]
+
+
+def total_sum(lefts, right, tops, lows, wide):
+    steps = chunks_of(lefts)
+    full = sum(left.shape[1] for left in lefts)
+    block = full // (2 * steps)
+    specs, narrow = left_specs(lefts, steps, lambda i: i)
+    out = jax.ShapeDtypeStruct((full, wide), BF16)
+    return pl.pallas_call(
+        functools.partial(total_kernel, narrow=narrow, steps=steps),
+        grid=(2 * steps,),
+        in_specs=specs
+        + [pl.BlockSpec((right.shape[0], wide), lambda i: (0, 0))]
+        + [pl.BlockSpec((block, wide), lambda i: (jnp.minimum(i, steps - 1), 0))] * 2
+        + [pl.BlockSpec((block, wide), lambda i: (jnp.maximum(i - steps, 0), 0))] * 2,
+        out_specs=pl.BlockSpec((block, wide), lambda i: (i, 0)),
+        out_shape=out,
+        compiler_params=pltpu.CompilerParams(vmem_limit_bytes=VMEM_BYTES),
+        cost_estimate=cost(2 * right.shape[0] * full * wide, [out, out, out]),
+        name="total_sum",
+    )(*lefts, right, *tops, *lows)
+
+
 class Plan:
     def __init__(self, ways_dp, ways_tensor):
         self.ways_dp = ways_dp
@@ -489,12 +606,15 @@
         self.wide = right.shape[1] // plan.chips
         self.staged = plan.bits == 2
         if self.staged:
-            self.first = [
-                self.top(3).astype(BF16),
-                self.low(3).astype(BF16),
-                self.low(1).astype(BF16),
-                self.top(2).astype(BF16),
-            ]
+            if len(lefts) == 1:
+                self.first = [
+                    self.top(3).astype(BF16),
+                    self.low(3).astype(BF16),
+                    self.low(1).astype(BF16),
+                    self.top(2).astype(BF16),
+                ]
+            else:
+                self.first = [self.sent(0, 3), self.sent(1, 3), self.sent(1, 1), self.sent(0, 2)]
         else:
             self.first = [
                 jnp.concatenate([self.top(r), self.low(r)], axis=0) for r in range(plan.chips)
@@ -507,6 +627,9 @@
             half = left.shape[1] // 2
             parts.append(dot_first(left[:, side * half : (side + 1) * half], right))
         return parts[0] if len(parts) == 1 else jnp.concatenate(parts, axis=0)
+
+    def sent(self, side, r, *adds):
+        return term_sum(self.lefts, self.right, side, r, self.wide, adds)
 
     def top(self, r):
         return self.term(r, 0)
@@ -536,10 +659,7 @@
     def prepare_second(self):
         if self.staged:
             far_top, far_low = self.got[:2]
-            self.second = [
-                (self.top(1) + far_top.astype(F32)).astype(BF16),
-                (self.low(2) + far_low.astype(F32)).astype(BF16),
-            ]
+            self.second = [self.sent(0, 1, far_top), self.sent(1, 2, far_low)]
         else:
             self.second = []
 
@@ -553,9 +673,7 @@
         if self.staged:
             x_top, y_low = self.last
             x_low, y_top = self.got[2:]
-            top = self.top(0) + x_top.astype(F32) + y_top.astype(F32)
-            low = self.low(0) + x_low.astype(F32) + y_low.astype(F32)
-            total = jnp.concatenate([self.by_place(top.astype(BF16)), self.by_place(low.astype(BF16))], axis=0)
+            return total_sum(self.lefts, self.right, (x_top, y_top), (x_low, y_low), self.wide)
         else:
             parts = self.got
             for bit in reversed(range(self.plan.bits)):
@@ -694,7 +812,9 @@
     down_far, grad_pre = together(down_sum.got[:2], grad_pre)
     down_sum.got = [*down_far, *down_sum.got[2:]]
     two_sum = Reduction(plan, [grad_pre], normed_two)
-    two_sum.first, down_sum.got, grad_pre = together(two_sum.first, down_sum.got, grad_pre)
+    two_sum.first, down_sum.got, grad_pre, inner_low = together(
+        two_sum.first, down_sum.got, grad_pre, inner_low
+    )
     two_sum.send_first()
     down_sum.prepare_second()
     give_two, keep_two = combine(core, [grad_pre], full_two)
@@ -728,8 +848,7 @@
         two_sum.got, two_sum.last, out_sum.got, query_low, key_low, value_low, grad_cumul
     )
     out_sum.prepare_second()
-    out_sum.second, outputs, grad_cumul = together(out_sum.second, outputs, grad_cumul)
-    outputs = plan.from_chip(outputs)
+    out_sum.second, grad_cumul = together(out_sum.second, grad_cumul)
     out_sum.send_second()
     grad_logf = jnp.flip(jnp.cumsum(jnp.flip(grad_cumul, 0), axis=0), 0)
     grad_logit = grad_logf * jax.nn.sigmoid(-forget_logit)
@@ -742,18 +861,20 @@
     one_sum = Reduction(plan, grad_one, normed_one)
     one_sum.first, out_sum.last = together(one_sum.first, out_sum.last)
     one_sum.send_first()
-    one_far, grad_one = together(one_sum.got[:2], grad_one)
-    one_sum.got = [*one_far, *one_sum.got[2:]]
+    one_sum.prepare_second()
+    one_sum.second, grad_one, two_sum.last, outputs = together(
+        one_sum.second, grad_one, two_sum.last, outputs
+    )
+    one_sum.send_second()
+    outputs = plan.from_chip(outputs)
     down_pair = plan.scatter(down_sum.finish())
-    two_total, down_pair, outputs = together(two_sum.finish(), down_pair, outputs)
+    two_total, down_pair = together(two_sum.finish(), down_pair)
     two_pair = plan.scatter(two_total)
     grad_normed_one = plan.sum_rows(*combine(core, grad_one, kinds_one))
     gain_one_term = jnp.sum(grad_normed_one * rows_in * scale_one, axis=0)
     input_grad = plan.from_chip(
         (grad_hidden + norm_back(rows_in, scale_one, gain_one, grad_normed_one)).astype(BF16)
     )
-    one_sum.prepare_second()
-    one_sum.send_second()
 
     bias_full = jnp.where(
         (jnp.arange(2) == core)[None, :, None], bias_term.reshape(4, 1, heads_shard), 0.0
@@ -765,7 +886,7 @@
 
     out_total, two_pair = together(out_sum.finish(), two_pair)
     out_pair = plan.scatter(out_total)
-    one_total, out_pair, input_grad = together(one_sum.finish(), out_pair, input_grad)
+    one_total, out_pair = together(one_sum.finish(), out_pair)
     one_pair = plan.scatter(one_total)
     down_shard, two_shard = plan.share(down_pair), plan.share(two_pair)
     out_shard, one_shard = plan.share(out_pair), plan.share(one_pair)

time: 857 us -> 854 us (level)
  Pallas kernels: 185 us -> 278 us
  matrix products: 105 us -> 30.8 us
  other arithmetic: 95.1 us -> 75 us
    pallas_call x0 -> x16, Pallas kernels: none -> 84.1 us  [the longest x12 53 us: term_sum(): pl.pallas_call(functools.partial(term_kernel, narrow=narrow, side=side),...]
    dot_general x56 -> x12, matrix products: 105 us -> 30.8 us  [dot_first(): lax.dot_general(left, right, (((0,), (0,)), ((), ())), preferred_element_...]
    ppermute x4, waiting for transfers between devices: 50.8 us -> 0.01 us  [from_chip(): got.append(lax.ppermute(self.by_chip(part), ('dp', 'tensor'), back))]
    ppermute x2, waiting for transfers between devices: 8.68 us -> 58.4 us  [sum_all(): vector = vector + lax.ppermute(vector, 'tensor', perm)]
    reduce_scatter x4, waiting for transfers between devices: 12.6 us -> 30.9 us  [scatter(): return lax.psum_scatter(total, 'tensor', scatter_dimension=0, tiled=True)]
    convert_element_type x8 -> x0, other arithmetic: 15.2 us -> none  [the longest x3 6.56 us: finish(): low.astype(BF16)]
    pallas_call x4, Pallas kernels: 64.7 us -> 74.1 us  [combine(): pl.pallas_call(functools.partial(combine_kernel, lefts=len(lefts)), grid_...]
  transfers between devices with their start and end apart: 76 -> 76, of which waited for: 26 -> 28; matrix products, arithmetic and copies ran while one was open for 28% -> 16% of each run, Pallas kernels for 22% -> 32%
where the time goes in v5:
time: 854 us; the launch traced here: 844 us
  Pallas kernels  278 us (33%)
  waiting for transfers between devices  276 us (32%)
  starting transfers between devices  103 us (12%)
  other arithmetic  75 us (9%)
  local copies, waits for them, and re-layouts  64.4 us (8%)
  matrix products  30.8 us (4%)
  between operations  16 us (2%)
    ppermute x42, waiting for transfers between devices, swap_chip(): return lax.ppermute(array, 'dp', perm)  125 us
    pallas_call x4, Pallas kernels, combine(): pl.pallas_call(functools.partial(combine_kernel, lefts=len(lefts)), grid_...  74.1 us
    ppermute x2, waiting for transfers between devices, sum_all(): vector = vector + lax.ppermute(vector, 'tensor', perm)  58.4 us
    pallas_call x12, Pallas kernels, term_sum(): pl.pallas_call(functools.partial(term_kernel, narrow=narrow, side=side),...  53 us
    ppermute x42, starting transfers between devices, swap_chip(): return lax.ppermute(array, 'dp', perm)  48.3 us
    all_gather x3, waiting for transfers between devices, line_gather(): return lax.all_gather(pair, 'tensor', axis=0, tiled=True)  37.7 us
    pallas_call x1, Pallas kernels, attn_bwd(): pl.pallas_call(functools.partial(attn_bwd_kernel, blk=blk), grid=(pairs,)...  32.8 us
    ppermute x17, starting transfers between devices, swap_core(): return lax.ppermute(array, 'dp', self.core_perm)  32.8 us
  transfers between devices with their start and end apart: 76, of which 28 were waited for; matrix products, arithmetic and copies ran while one was open for 16% of the time, Pallas kernels for 32%

profile of v5, /device:TPU:0, one launch (start us, length us, event | category | flops | bytes accessed | tf_op | source)
XLA Modules:
  0.0 843.6 jit_solution(16889095300001330977)
XLA Ops:
  20.1 37.7 %all-gather.4.cloned.1.call-done.refs_0_ = bf16[2368,384]{1,0:T(8,128)(2,1)} async-done(((bf16[592,384]{1,0:T(8,128)(2,1)}), bf16[2368,384]{1,0:T(8,128)(2,1)}) %all-gather.4.cloned.1.call-update) | async-done | bytes 1818640 | tf_op jit(solution)/shard_map/all_gather | solution.py:563
  80.3 18.9 %collective-permute-done.3.refs_1_ = bf16[2368,384]{1,0:T(8,128)(2,1)S(1)} collective-permute-done((bf16[2368,384]{1,0:T(8,128)(2,1)}, bf16[2368,384]{1,0:T(8,128)(2,1)S(1)}, u32[]{:S(2)}, u32[]{:S(2)}) %collective-permute-start.3) | collective-permute-done | bytes 1818656 | tf_op jit(solution)/shard_map/ppermute | solution.py:501
  130.2 15.7 %collective-permute-start.8 = (bf16[512,1536]{1,0:T(8,128)(2,1)}, bf16[512,1536]{1,0:T(8,128)(2,1)}, u32[]{:S(2)}, u32[]{:S(2)}) collective-permute-start(bf16[512,1536]{1,0:T(8,128)(2,1)} %fusion.10), channel_id=1, source_target_pairs={{0,4},{4,0},{8,12},{12,8},{16,20},{20,16},{24,28},{28,24},{1,5},{5... | collective-permute-start | bytes 4718600 | tf_op jit(solution)/shard_map/ppermute | solution.py:497
  157.9 16.4 %project.1 = (bf16[1024,768]{1,0:T(8,128)(2,1)}, bf16[1024,768]{1,0:T(8,128)(2,1)}, bf16[1024,768]{1,0:T(8,128)(2,1)}, f32[2,1024,32]{2,1,0:T(8,128)}) custom-call(bf16[1024,1536]{1,0:T(8,128)(2,1)} %pad_maximum_fusion.2.x_ref.refs_4_, bf16[2368,384]{1,0:T(8,128)(2,1)} %all-gather.4.cloned.1.call-done.refs_0_, bf16[2368,384]{1,0:T(8,128)(2,1)} %copy-done.13, ...), custom_call_target="tpu_custom_call" | custom-call | flops 7449083904 | bytes 15138816 | tf_op jit(solution)/shard_map/project/pallas_call | solution.py:217
  189.8 15.4 %collective-permute-done.12 = bf16[384,384]{1,0:T(8,128)(2,1)S(1)} collective-permute-done((bf16[384,384]{1,0:T(8,128)(2,1)S(1)}, bf16[384,384]{1,0:T(8,128)(2,1)S(1)}, u32[]{:S(2)}, u32[]{:S(2)}) %collective-permute-start.12) | collective-permute-done | bytes 294944 | tf_op jit(solution)/shard_map/ppermute | solution.py:501
  208.2 25.1 %shard_map.246 = (bf16[1024,768]{1,0:T(8,128)(2,1)}, f32[1024,768]{1,0:T(8,128)}) custom-call(s32[1]{0:T(128)} %bitcast.18.len_ref, bf16[1024,768]{1,0:T(8,128)(2,1)} %get-tuple-element.155.q_ref, bf16[1024,768]{1,0:T(8,128)(2,1)} %get-tuple-element.156.k_ref, bf16[1024,768]{1,0:T(8,128)(2,1)} %get-tuple-element.157.v_ref, f32[6,1024,2]{2,1,0:T(8,128)} %bitcast.177), custom_call_target="tpu_custom_call" | custom-call | flops 6442450944 | bytes 9437184 | tf_op jit(solution)/shard_map/pallas_call | solution.py:97
  233.6 10.0 %combine.4 = (bf16[512,1536]{1,0:T(8,128)(2,1)}, f32[512,1536]{1,0:T(8,128)}) custom-call(s32[1]{0:T(128)} %bitcast.17.core_ref, bf16[1024,768]{1,0:T(8,128)(2,1)} %get-tuple-element.166.refs_0_.o_ref, bf16[768,384]{1,0:T(8,128)(2,1)} %bitcast.20.refs_1_.refs_0_, bf16[768,384]{1,0:T(8,128)(2,1)} %collective-permute-done.10.refs_2_.refs_1_, ...), custom_call_target="tpu_custom_call" | custom-call | flops 2415919104 | bytes 8650752 | tf_op jit(solution)/shard_map/combine/pallas_call | solution.py:267
  260.1 32.7 %collective-permute-done.19 = bf16[1024,384]{1,0:T(8,128)(2,1)S(1)} collective-permute-done((bf16[1024,384]{1,0:T(8,128)(2,1)S(1)}, bf16[1024,384]{1,0:T(8,128)(2,1)S(1)}, u32[]{:S(2)}, u32[]{:S(2)}) %collective-permute-start.19) | collective-permute-done | bytes 786464 | tf_op jit(solution)/shard_map/ppermute | solution.py:501
  304.7 11.9 %collective-permute-done.26 = bf16[256,1536]{1,0:T(8,128)(2,1)S(1)} collective-permute-done((bf16[256,1536]{1,0:T(8,128)(2,1)S(1)}, bf16[256,1536]{1,0:T(8,128)(2,1)S(1)}, u32[]{:S(2)}, u32[]{:S(2)}) %collective-permute-start.26) | collective-permute-done | bytes 786464 | tf_op jit(solution)/shard_map/ppermute | solution.py:528
  318.2 14.0 %collective-permute-start.27 = (bf16[512,1536]{1,0:T(8,128)(2,1)}, bf16[512,1536]{1,0:T(8,128)(2,1)}, u32[]{:S(2)}, u32[]{:S(2)}) collective-permute-start(bf16[512,1536]{1,0:T(8,128)(2,1)} %fusion.18), channel_id=1, source_target_pairs={{0,4},{4,0},{8,12},{12,8},{16,20},{20,16},{24,28},{28,24},{1,5},{5... | collective-permute-start | bytes 4718600 | tf_op jit(solution)/shard_map/ppermute | solution.py:497
  337.2 20.5 %inner_units.1 = (f32[1024,2048]{1,0:T(8,128)}, f32[1024,2048]{1,0:T(8,128)}, bf16[1024,2048]{1,0:T(8,128)(2,1)}) custom-call(bf16[1024,1536]{1,0:T(8,128)(2,1)} %pad_maximum_fusion.3.x_ref.refs_1_, bf16[4096,384]{1,0:T(8,128)(2,1)} %all-gather.8.cloned.1.call-done.refs_0_.refs_1_, bf16[4096,384]{1,0:T(8,128)(2,1)} %collective-permute-done.21.refs_1_.refs_2_, ...), custom_call_target="tpu_custom_call" | custom-call | flops 12884901888 | bytes 36700160 | tf_op jit(solution)/shard_map/inner_units/pallas_call | solution.py:330
  375.4 17.6 %inner_grads.1.refs_0_ = bf16[1024,4096]{1,0:T(8,128)(2,1)} custom-call(bf16[1024,1536]{1,0:T(8,128)(2,1)} %pad_maximum_fusion.x_ref.refs_1_, f32[1024,2048]{1,0:T(8,128)} %get-tuple-element.190.gate_ref, f32[1024,2048]{1,0:T(8,128)} %get-tuple-element.191.up_ref, bf16[2048,384]{1,0:T(8,128)(2,1)} %bitcast.168, ...), custom_call_target="tpu_custom_call" | custom-call | flops 6442450944 | bytes 34603008 | tf_op jit(solution)/shard_map/inner_grads/pallas_call | solution.py:357
  421.6 27.7 %combine.5 = (bf16[512,1536]{1,0:T(8,128)(2,1)}, f32[512,1536]{1,0:T(8,128)}) custom-call(s32[1]{0:T(128)} %bitcast.17.core_ref, bf16[1024,4096]{1,0:T(8,128)(2,1)} %inner_grads.1.refs_0_, bf16[4096,384]{1,0:T(8,128)(2,1)} %all-gather.8.cloned.1.call-done.refs_0_.refs_1_, bf16[4096,384]{1,0:T(8,128)(2,1)} %collective-permute-done.21.refs_1_.refs_2_, ...), custom_call_target="tpu_custom_call" | custom-call | flops 12884901888 | bytes 25690112 | tf_op jit(solution)/shard_map/combine/pallas_call | solution.py:267
  449.3 16.5 %combine.6 = (bf16[512,1536]{1,0:T(8,128)(2,1)}, f32[512,1536]{1,0:T(8,128)}) custom-call(s32[1]{0:T(128)} %bitcast.17.core_ref, bf16[1024,2048]{1,0:T(8,128)(2,1)} %get-tuple-element.207.refs_0_, bf16[2048,384]{1,0:T(8,128)(2,1)} %bitcast.169, bf16[2048,384]{1,0:T(8,128)(2,1)} %collective-permute-done.15.refs_1_.refs_2_, ...), custom_call_target="tpu_custom_call" | custom-call | flops 6442450944 | bytes 15204352 | tf_op jit(solution)/shard_map/combine/pallas_call | solution.py:267
  525.6 32.8 %shard_map.247 = (bf16[1024,768]{1,0:T(8,128)(2,1)}, bf16[1024,768]{1,0:T(8,128)(2,1)}, bf16[1024,768]{1,0:T(8,128)(2,1)}, f32[1024,768]{1,0:T(8,128)}) custom-call(s32[1]{0:T(128)} %bitcast.18.len_ref, bf16[1024,768]{1,0:T(8,128)(2,1)} %get-tuple-element.155.q_ref, bf16[1024,768]{1,0:T(8,128)(2,1)} %get-tuple-element.156.k_ref, ...), custom_call_target="tpu_custom_call" | custom-call | flops 16106127360 | bytes 18874368 | tf_op jit(solution)/shard_map/pallas_call | solution.py:169
  609.5 17.5 %collective-permute-done.49.refs_5_ = bf16[1184,384]{1,0:T(8,128)(2,1)S(1)} collective-permute-done((bf16[1184,384]{1,0:T(8,128)(2,1)S(1)}, bf16[1184,384]{1,0:T(8,128)(2,1)S(1)}, u32[]{:S(2)}, u32[]{:S(2)}) %collective-permute-start.49) | collective-permute-done | bytes 909344 | tf_op jit(solution)/shard_map/ppermute | solution.py:501
  638.2 12.3 %total_sum.6 = bf16[4096,384]{1,0:T(8,128)(2,1)} custom-call(bf16[1024,4096]{1,0:T(8,128)(2,1)} %inner_grads.1.refs_0_, bf16[1024,1536]{1,0:T(8,128)(2,1)} %pad_maximum_fusion.3.x_ref.refs_1_, bf16[2048,384]{1,0:T(8,128)(2,1)} %collective-permute-done.40.refs_2_, bf16[2048,384]{1,0:T(8,128)(2,1)} %collective-permute-done.37.refs_3_, ...), custom_call_target="tpu_custom_call" | custom-call | flops 3221225472 | bytes 9437184 | tf_op jit(solution)/shard_map/total_sum/pallas_call | solution.py:468
  653.9 20.0 %combine.7 = (bf16[512,1536]{1,0:T(8,128)(2,1)}, f32[512,1536]{1,0:T(8,128)}) custom-call(s32[1]{0:T(128)} %bitcast.17.core_ref, bf16[1024,768]{1,0:T(8,128)(2,1)} %get-tuple-element.243.refs_0_, bf16[1024,768]{1,0:T(8,128)(2,1)} %get-tuple-element.244.refs_1_, bf16[1024,768]{1,0:T(8,128)(2,1)} %get-tuple-element.245.refs_2_, ...), custom_call_target="tpu_custom_call" | custom-call | flops 7449083904 | bytes 16842752 | tf_op jit(solution)/shard_map/combine/pallas_call | solution.py:267
  688.9 7.5 collective-permute-start.51
  704.5 7.8 total_sum.4
  716.1 13.1 %reduce-scatter.7.cloned.1.call-done = bf16[1024,384]{1,0:T(8,128)(2,1)} async-done(((bf16[4096,384]{1,0:T(8,128)(2,1)}), bf16[1024,384]{1,0:T(8,128)(2,1)}) %reduce-scatter.7.cloned.1.call-update) | async-done | bytes 786448 | tf_op jit(solution)/shard_map/reduce_scatter | solution.py:583
  736.5 17.8 %reduce-scatter.9.cloned.1.call-done = bf16[192,384]{1,0:T(8,128)(2,1)} async-done(((bf16[768,384]{1,0:T(8,128)(2,1)}), bf16[192,384]{1,0:T(8,128)(2,1)}) %reduce-scatter.9.cloned.1.call-update) | async-done | bytes 147472 | tf_op jit(solution)/shard_map/reduce_scatter | solution.py:583
  762.2 50.9 %collective-permute-done.59 = f32[3096]{0:T(1024)S(1)} collective-permute-done((f32[3096]{0:T(1024)S(1)}, f32[3096]{0:T(1024)S(1)}, u32[]{:S(2)}, u32[]{:S(2)}) %collective-permute-start.59) | collective-permute-done | bytes 12416 | tf_op jit(solution)/shard_map/ppermute | solution.py:599
  814.4 7.5 collective-permute-done.60
  (456 shorter events, 360.3 us)
Async XLA Ops:
  7.2 50.7 %all-gather.4.cloned.1.call-start = ((), (), s32[]{:S(2)}) async-start(), calls=%async_computation.4 | async-start | bytes 2273280 | tf_op jit(solution)/shard_map/all_gather | solution.py:563
  14.1 132.1 %all-gather.6.cloned.1.call-start = ((), (), s32[]{:S(2)}) async-start(), calls=%async_computation.5 | async-start | bytes 2703360 | tf_op jit(solution)/shard_map/all_gather | solution.py:563
  20.1 186.0 %all-gather.8.cloned.1.call-start = ((), (), s32[]{:S(2)}) async-start(), calls=%async_computation.6 | async-start | bytes 3932160 | tf_op jit(solution)/shard_map/all_gather | solution.py:563
  106.6 543.9 %reduce-scatter.5.cloned.1.call-start = ((), (), s32[]{:S(2)}) async-start(), calls=%async_computation.7 | async-start | bytes 1966080 | tf_op jit(solution)/shard_map/reduce_scatter | solution.py:583
  152.6 80.7 %collective-permute-start.15 = (bf16[2048,384]{1,0:T(8,128)(2,1)S(1)}, bf16[2048,384]{1,0:T(8,128)(2,1)}, u32[]{:S(2)}, u32[]{:S(2)}) collective-permute-start(bf16[2048,384]{1,0:T(8,128)(2,1)S(1)} %bitcast.166), channel_id=1, source_target_pairs={{0,8},{4,12},{8,0},{12,4},{16,24},{20,28},{24,16},{28,20},{1,9},{5... | collective-permute-start | bytes 4718600 | tf_op jit(solution)/shard_map/ppermute | solution.py:501
  153.2 80.1 %collective-permute-start.16 = (bf16[2048,384]{1,0:T(8,128)(2,1)S(1)}, bf16[2048,384]{1,0:T(8,128)(2,1)}, u32[]{:S(2)}, u32[]{:S(2)}) collective-permute-start(bf16[2048,384]{1,0:T(8,128)(2,1)S(1)} %bitcast.167), channel_id=1, source_target_pairs={{0,16},{4,20},{8,24},{12,28},{16,0},{20,4},{24,8},{28,12},{1,17},{... | collective-permute-start | bytes 4718600 | tf_op jit(solution)/shard_map/ppermute | solution.py:501
  206.1 88.0 %collective-permute-start.21 = (bf16[4096,384]{1,0:T(8,128)(2,1)}, bf16[4096,384]{1,0:T(8,128)(2,1)}, u32[]{:S(2)}, u32[]{:S(2)}) collective-permute-start(bf16[4096,384]{1,0:T(8,128)(2,1)} %all-gather.8.cloned.1.call-done.refs_0_.refs_1_), channel_id=1, source_target_pairs={{0,8},{4,12},{8,0},{12,4},{16,24},{20,28},{24,16},{28,20},{1,9},{5... | collective-permute-start | bytes 9437192 | tf_op jit(solution)/shard_map/ppermute | solution.py:501
  206.7 87.5 %collective-permute-start.22 = (bf16[4096,384]{1,0:T(8,128)(2,1)}, bf16[4096,384]{1,0:T(8,128)(2,1)}, u32[]{:S(2)}, u32[]{:S(2)}) collective-permute-start(bf16[4096,384]{1,0:T(8,128)(2,1)} %all-gather.8.cloned.1.call-done.refs_0_.refs_1_), channel_id=1, source_target_pairs={{0,16},{4,20},{8,24},{12,28},{16,0},{20,4},{24,8},{28,12},{1,17},{... | collective-permute-start | bytes 9437192 | tf_op jit(solution)/shard_map/ppermute | solution.py:501
  413.7 52.0 %collective-permute-start.35 = (bf16[1024,384]{1,0:T(8,128)(2,1)}, bf16[1024,384]{1,0:T(8,128)(2,1)}, u32[]{:S(2)}, u32[]{:S(2)}) collective-permute-start(bf16[1024,384]{1,0:T(8,128)(2,1)} %term_sum.13), channel_id=1, source_target_pairs={{0,16},{4,20},{8,24},{12,28},{16,0},{20,4},{24,8},{28,12},{1,17},{... | collective-permute-start | bytes 2359304 | tf_op jit(solution)/shard_map/ppermute | solution.py:501
  418.1 47.7 %collective-permute-start.34 = (bf16[1024,384]{1,0:T(8,128)(2,1)}, bf16[1024,384]{1,0:T(8,128)(2,1)}, u32[]{:S(2)}, u32[]{:S(2)}) collective-permute-start(bf16[1024,384]{1,0:T(8,128)(2,1)} %term_sum.12), channel_id=1, source_target_pairs={{0,8},{4,12},{8,0},{12,4},{16,24},{20,28},{24,16},{28,20},{1,9},{5... | collective-permute-start | bytes 2359304 | tf_op jit(solution)/shard_map/ppermute | solution.py:501
  419.6 48.4 %collective-permute-start.32 = (bf16[2048,384]{1,0:T(8,128)(2,1)}, bf16[2048,384]{1,0:T(8,128)(2,1)}, u32[]{:S(2)}, u32[]{:S(2)}) collective-permute-start(bf16[2048,384]{1,0:T(8,128)(2,1)} %fusion.19), channel_id=1, source_target_pairs={{0,16},{4,20},{8,24},{12,28},{16,0},{20,4},{24,8},{28,12},{1,17},{... | collective-permute-start | bytes 4718600 | tf_op jit(solution)/shard_map/ppermute | solution.py:501
  421.1 51.0 %collective-permute-start.33 = (bf16[2048,384]{1,0:T(8,128)(2,1)}, bf16[2048,384]{1,0:T(8,128)(2,1)}, u32[]{:S(2)}, u32[]{:S(2)}) collective-permute-start(bf16[2048,384]{1,0:T(8,128)(2,1)} %fusion.25), channel_id=1, source_target_pairs={{0,8},{4,12},{8,0},{12,4},{16,24},{20,28},{24,16},{28,20},{1,9},{5... | collective-permute-start | bytes 4718600 | tf_op jit(solution)/shard_map/ppermute | solution.py:501
  483.9 76.9 %collective-permute-start.36 = (bf16[2048,384]{1,0:T(8,128)(2,1)}, bf16[2048,384]{1,0:T(8,128)(2,1)}, u32[]{:S(2)}, u32[]{:S(2)}) collective-permute-start(bf16[2048,384]{1,0:T(8,128)(2,1)} %fusion.28), channel_id=1, source_target_pairs={{0,8},{4,12},{8,0},{12,4},{16,24},{20,28},{24,16},{28,20},{1,9},{5... | collective-permute-start | bytes 4718600 | tf_op jit(solution)/shard_map/ppermute | solution.py:501
  485.4 76.8 %collective-permute-start.37 = (bf16[2048,384]{1,0:T(8,128)(2,1)}, bf16[2048,384]{1,0:T(8,128)(2,1)}, u32[]{:S(2)}, u32[]{:S(2)}) collective-permute-start(bf16[2048,384]{1,0:T(8,128)(2,1)} %fusion.22), channel_id=1, source_target_pairs={{0,16},{4,20},{8,24},{12,28},{16,0},{20,4},{24,8},{28,12},{1,17},{... | collective-permute-start | bytes 4718600 | tf_op jit(solution)/shard_map/ppermute | solution.py:501
  494.0 235.1 %reduce-scatter.7.cloned.1.call-start = ((), (), s32[]{:S(2)}) async-start(), calls=%async_computation.8 | async-start | bytes 3932160 | tf_op jit(solution)/shard_map/reduce_scatter | solution.py:583
  522.8 52.3 %collective-permute-start.40 = (bf16[2048,384]{1,0:T(8,128)(2,1)}, bf16[2048,384]{1,0:T(8,128)(2,1)}, u32[]{:S(2)}, u32[]{:S(2)}) collective-permute-start(bf16[2048,384]{1,0:T(8,128)(2,1)} %term_sum.14), channel_id=1, source_target_pairs={{0,8},{4,12},{8,0},{12,4},{16,24},{20,28},{24,16},{28,20},{1,9},{5... | collective-permute-start | bytes 4718600 | tf_op jit(solution)/shard_map/ppermute | solution.py:501
  523.6 51.6 %collective-permute-start.41 = (bf16[2048,384]{1,0:T(8,128)(2,1)}, bf16[2048,384]{1,0:T(8,128)(2,1)}, u32[]{:S(2)}, u32[]{:S(2)}) collective-permute-start(bf16[2048,384]{1,0:T(8,128)(2,1)} %term_sum.15), channel_id=1, source_target_pairs={{0,16},{4,20},{8,24},{12,28},{16,0},{20,4},{24,8},{28,12},{1,17},{... | collective-permute-start | bytes 4718600 | tf_op jit(solution)/shard_map/ppermute | solution.py:501
  650.5 103.8 %reduce-scatter.9.cloned.1.call-start = ((), (), s32[]{:S(2)}) async-start(), calls=%async_computation.9 | async-start | bytes 737280 | tf_op jit(solution)/shard_map/reduce_scatter | solution.py:583
  687.1 73.5 %collective-permute-start.52 = (bf16[256,1536]{1,0:T(8,128)(2,1)}, bf16[256,1536]{1,0:T(8,128)(2,1)}, u32[]{:S(2)}, u32[]{:S(2)}) collective-permute-start(bf16[256,1536]{1,0:T(8,128)(2,1)} %pad_maximum_fusion.21), channel_id=1, source_target_pairs={{2,0},{0,1},{6,2},{4,3},{3,4},{1,5},{7,6},{5,7},{10,8},{8,9},{14,1... | collective-permute-start | bytes 2359304 | tf_op jit(solution)/shard_map/ppermute | solution.py:541
  688.9 71.6 %collective-permute-start.51 = (bf16[256,1536]{1,0:T(8,128)(2,1)}, bf16[256,1536]{1,0:T(8,128)(2,1)}, u32[]{:S(2)}, u32[]{:S(2)}) collective-permute-start(bf16[256,1536]{1,0:T(8,128)(2,1)} %pad_maximum_fusion.20), channel_id=1, source_target_pairs={{0,0},{2,1},{4,2},{6,3},{1,4},{3,5},{5,6},{7,7},{8,8},{10,9},{12,1... | collective-permute-start | bytes 2359304 | tf_op jit(solution)/shard_map/ppermute | solution.py:541
  729.2 100.5 %reduce-scatter.11.cloned.1.call-start = ((), (), s32[]{:S(2)}) async-start(), calls=%async_computation.10 | async-start | bytes 2273280 | tf_op jit(solution)/shard_map/reduce_scatter | solution.py:583
  754.4 69.0 %collective-permute-start.55 = (bf16[256,1536]{1,0:T(8,128)(2,1)S(1)}, bf16[256,1536]{1,0:T(8,128)(2,1)S(1)}, u32[]{:S(2)}, u32[]{:S(2)}) collective-permute-start(bf16[256,1536]{1,0:T(8,128)(2,1)S(1)} %pad_maximum_fusion.23), channel_id=1, source_target_pairs={{2,0},{0,1},{6,2},{4,3},{3,4},{1,5},{7,6},{5,7},{10,8},{8,9},{14,1... | collective-permute-start | bytes 2359304 | tf_op jit(solution)/shard_map/ppermute | solution.py:541
  756.1 67.3 %collective-permute-start.54 = (bf16[256,1536]{1,0:T(8,128)(2,1)S(1)}, bf16[256,1536]{1,0:T(8,128)(2,1)S(1)}, u32[]{:S(2)}, u32[]{:S(2)}) collective-permute-start(bf16[256,1536]{1,0:T(8,128)(2,1)S(1)} %pad_maximum_fusion.22), channel_id=1, source_target_pairs={{0,0},{2,1},{4,2},{6,3},{1,4},{3,5},{5,6},{7,7},{8,8},{10,9},{12,1... | collective-permute-start | bytes 2359304 | tf_op jit(solution)/shard_map/ppermute | solution.py:541
  758.4 54.7 %collective-permute-start.59 = (f32[3096]{0:T(1024)S(1)}, f32[3096]{0:T(1024)S(1)}, u32[]{:S(2)}, u32[]{:S(2)}) collective-permute-start(f32[3096]{0:T(1024)S(1)} %add.351), channel_id=1, source_target_pairs={{0,1},{1,0},{2,3},{3,2},{4,5},{5,4},{6,7},{7,6},{8,9},{9,8},{10,11... | collective-permute-start | bytes 37160 | tf_op jit(solution)/shard_map/ppermute | solution.py:599
  (102 other events, 1939.5 us)
Sparse Core Ops, SparseCore 0:
  14.2 43.6 all-gather.3
  59.4 77.5 all-gather.5
  139.2 62.5 all-gather.7
  494.1 32.8 reduce-scatter.4
  650.7 78.4 reduce-scatter.6
  731.3 23.0 reduce-scatter.8
  756.6 56.4 reduce-scatter.10

commit v6 on v5

--- a/solution.py
+++ b/solution.py
@@ -233,22 +233,18 @@
     left_refs, w_refs, (give_ref, keep_ref) = refs[:lefts], refs[lefts:-2], refs[-2:]
     step = pl.program_id(0)
     wide = w_refs[0].shape[1]
-    for n, w in enumerate(w_refs):
-        got, at = None, 0
-        for left in left_refs:
-            deep = left.shape[1]
-            part = nn(left[...], w[at : at + deep, :])
-            got = part if got is None else got + part
-            at += deep
-        cols = slice(n * wide, (n + 1) * wide)
-
-        @pl.when(step < 2)
+    for out, cond in ((give_ref, step < 2), (keep_ref, step >= 2)):
+
+        @pl.when(cond)
         def _():
-            give_ref[:, cols] = got.astype(BF16)
-
-        @pl.when(step >= 2)
-        def _():
-            keep_ref[:, cols] = got
+            for n, w in enumerate(w_refs):
+                got, at = None, 0
+                for left in left_refs:
+                    deep = left.shape[1]
+                    part = nn(left[...], w[at : at + deep, :])
+                    got = part if got is None else got + part
+                    at += deep
+                out[:, n * wide : (n + 1) * wide] = got.astype(out.dtype)
 
 
 def combine(core, lefts, weights):
@@ -686,6 +682,35 @@
             total = jnp.concatenate(
                 [self.by_place(parts[0][:half]), self.by_place(parts[0][half:])], axis=0
             )
+        return total.astype(BF16)
+
+
+class Direct:
+    def __init__(self, plan, lefts, right):
+        self.plan, self.left, self.right = plan, lefts[0], right
+        self.wide = right.shape[1] // plan.chips
+        self.first = [self.term(r).astype(BF16) for r in range(1, plan.chips)]
+
+    def term(self, r):
+        return dot_first(self.left, self.right[:, r * self.wide : (r + 1) * self.wide])
+
+    def send_first(self):
+        ways = range(self.plan.ways_dp)
+        self.got = [
+            lax.ppermute(part, "dp", [(i, i ^ (2 * (n + 1))) for i in ways])
+            for n, part in enumerate(self.first)
+        ]
+
+    def prepare_second(self):
+        self.second = []
+
+    def send_second(self):
+        self.last = []
+
+    def finish(self):
+        total = self.term(0)
+        for part in self.got:
+            total = total + part.astype(F32)
         return total.astype(BF16)
 
 
@@ -831,7 +856,7 @@
     )
 
     grad_attn = plan.both_rows(grad_hidden.astype(BF16))
-    out_sum = Reduction(plan, [mixed_low], grad_attn)
+    out_sum = (Direct if plan.bits == 2 else Reduction)(plan, [mixed_low], grad_attn)
     two_sum.prepare_second()
     out_sum.first, two_sum.second, grad_attn = together(
         out_sum.first, two_sum.second, grad_attn
@@ -859,14 +884,14 @@
     ).reshape(seq_rows, -1)
     grad_one = [query_low, key_low, value_low, logit_low]
     one_sum = Reduction(plan, grad_one, normed_one)
-    one_sum.first, out_sum.last = together(one_sum.first, out_sum.last)
+    one_sum.first, out_sum.last, two_sum.last, outputs = together(
+        one_sum.first, out_sum.last, two_sum.last, outputs
+    )
     one_sum.send_first()
+    outputs = plan.from_chip(outputs)
     one_sum.prepare_second()
-    one_sum.second, grad_one, two_sum.last, outputs = together(
-        one_sum.second, grad_one, two_sum.last, outputs
-    )
+    one_sum.second, grad_one = together(one_sum.second, grad_one)
     one_sum.send_second()
-    outputs = plan.from_chip(outputs)
     down_pair = plan.scatter(down_sum.finish())
     two_total, down_pair = together(two_sum.finish(), down_pair)
     two_pair = plan.scatter(two_total)

time: 854 us -> 829 us (0.971)
  Pallas kernels: 278 us -> 259 us
  waiting for transfers between devices: 276 us -> 267 us
    reduce_scatter x4, waiting for transfers between devices: 30.9 us -> 14.6 us  [scatter(): return lax.psum_scatter(total, 'tensor', scatter_dimension=0, tiled=True)]
    ppermute x0 -> x3, waiting for transfers between devices: none -> 15.2 us  [send_first(): lax.ppermute(part, 'dp', [(i, i ^ 2 * (n + 1)) for i in ways])]
    pallas_call x4, Pallas kernels: 74.1 us -> 64.4 us  [combine(): pl.pallas_call(functools.partial(combine_kernel, lefts=len(lefts)), grid_...]
    ppermute x42 -> x36, waiting for transfers between devices: 125 us -> 117 us  [swap_chip(): return lax.ppermute(array, 'dp', perm)]
    ppermute x42 -> x36, starting transfers between devices: 48.3 us -> 41.1 us  [swap_chip(): return lax.ppermute(array, 'dp', perm)]
    pallas_call x12 -> x10, Pallas kernels: 53 us -> 47.3 us  [term_sum(): pl.pallas_call(functools.partial(term_kernel, narrow=narrow, side=side),...]
    pallas_call x4 -> x3, Pallas kernels: 31.2 us -> 27.3 us  [total_sum(): pl.pallas_call(functools.partial(total_kernel, narrow=narrow, steps=steps...]
  transfers between devices with their start and end apart: 76 -> 73, of which waited for: 28 -> 26; matrix products, arithmetic and copies ran while one was open for 16% -> 18% of each run, Pallas kernels for 32% -> 31%
where the time goes in v6:
time: 829 us; the launch traced here: 819 us
  waiting for transfers between devices  267 us (32%)
  Pallas kernels  259 us (31%)
  starting transfers between devices  98.9 us (12%)
  other arithmetic  77 us (9%)
  local copies, waits for them, and re-layouts  66.1 us (8%)
  matrix products  34.9 us (4%)
  between operations  15.8 us (2%)
    ppermute x36, waiting for transfers between devices, swap_chip(): return lax.ppermute(array, 'dp', perm)  117 us
    pallas_call x4, Pallas kernels, combine(): pl.pallas_call(functools.partial(combine_kernel, lefts=len(lefts)), grid_...  64.4 us
    ppermute x2, waiting for transfers between devices, sum_all(): vector = vector + lax.ppermute(vector, 'tensor', perm)  58.4 us
    pallas_call x10, Pallas kernels, term_sum(): pl.pallas_call(functools.partial(term_kernel, narrow=narrow, side=side),...  47.3 us
    ppermute x36, starting transfers between devices, swap_chip(): return lax.ppermute(array, 'dp', perm)  41.1 us
    all_gather x3, waiting for transfers between devices, line_gather(): return lax.all_gather(pair, 'tensor', axis=0, tiled=True)  37.6 us
    dot_general x12, matrix products, dot_first(): lax.dot_general(left, right, (((0,), (0,)), ((), ())), preferred_element_...  34.9 us
    pallas_call x1, Pallas kernels, attn_bwd(): pl.pallas_call(functools.partial(attn_bwd_kernel, blk=blk), grid=(pairs,)...  32.8 us
  transfers between devices with their start and end apart: 73, of which 26 were waited for; matrix products, arithmetic and copies ran while one was open for 18% of the time, Pallas kernels for 31%

profile of v6, /device:TPU:0, one launch (start us, length us, event | category | flops | bytes accessed | tf_op | source)
XLA Modules:
  0.0 818.8 jit_solution(11988097746308486473)
XLA Ops:
  20.2 37.6 %all-gather.4.cloned.1.call-done.refs_0_ = bf16[2368,384]{1,0:T(8,128)(2,1)} async-done(((bf16[592,384]{1,0:T(8,128)(2,1)}), bf16[2368,384]{1,0:T(8,128)(2,1)}) %all-gather.4.cloned.1.call-update) | async-done | bytes 1818640 | tf_op jit(solution)/shard_map/all_gather | solution.py:559
  80.2 18.9 %collective-permute-done.3.refs_1_ = bf16[2368,384]{1,0:T(8,128)(2,1)S(1)} collective-permute-done((bf16[2368,384]{1,0:T(8,128)(2,1)}, bf16[2368,384]{1,0:T(8,128)(2,1)S(1)}, u32[]{:S(2)}, u32[]{:S(2)}) %collective-permute-start.3) | collective-permute-done | bytes 1818656 | tf_op jit(solution)/shard_map/ppermute | solution.py:497
  130.3 15.6 %collective-permute-start.8 = (bf16[512,1536]{1,0:T(8,128)(2,1)}, bf16[512,1536]{1,0:T(8,128)(2,1)}, u32[]{:S(2)}, u32[]{:S(2)}) collective-permute-start(bf16[512,1536]{1,0:T(8,128)(2,1)} %fusion.10), channel_id=1, source_target_pairs={{0,4},{4,0},{8,12},{12,8},{16,20},{20,16},{24,28},{28,24},{1,5},{5... | collective-permute-start | bytes 4718600 | tf_op jit(solution)/shard_map/ppermute | solution.py:493
  157.9 16.3 %project.1 = (bf16[1024,768]{1,0:T(8,128)(2,1)}, bf16[1024,768]{1,0:T(8,128)(2,1)}, bf16[1024,768]{1,0:T(8,128)(2,1)}, f32[2,1024,32]{2,1,0:T(8,128)}) custom-call(bf16[1024,1536]{1,0:T(8,128)(2,1)} %pad_maximum_fusion.2.x_ref.refs_4_, bf16[2368,384]{1,0:T(8,128)(2,1)} %all-gather.4.cloned.1.call-done.refs_0_, bf16[2368,384]{1,0:T(8,128)(2,1)} %copy-done.12, ...), custom_call_target="tpu_custom_call" | custom-call | flops 7449083904 | bytes 15138816 | tf_op jit(solution)/shard_map/project/pallas_call | solution.py:217
  189.8 15.5 %collective-permute-done.12 = bf16[384,384]{1,0:T(8,128)(2,1)S(1)} collective-permute-done((bf16[384,384]{1,0:T(8,128)(2,1)S(1)}, bf16[384,384]{1,0:T(8,128)(2,1)S(1)}, u32[]{:S(2)}, u32[]{:S(2)}) %collective-permute-start.12) | collective-permute-done | bytes 294944 | tf_op jit(solution)/shard_map/ppermute | solution.py:497
  208.2 25.1 %shard_map.246 = (bf16[1024,768]{1,0:T(8,128)(2,1)}, f32[1024,768]{1,0:T(8,128)}) custom-call(s32[1]{0:T(128)} %bitcast.18.len_ref, bf16[1024,768]{1,0:T(8,128)(2,1)} %get-tuple-element.148.q_ref, bf16[1024,768]{1,0:T(8,128)(2,1)} %get-tuple-element.149.k_ref, bf16[1024,768]{1,0:T(8,128)(2,1)} %get-tuple-element.150.v_ref, f32[6,1024,2]{2,1,0:T(8,128)} %bitcast.181), custom_call_target="tpu_custom_call" | custom-call | flops 6442450944 | bytes 9437184 | tf_op jit(solution)/shard_map/pallas_call | solution.py:97
  233.6 7.7 combine.4
  257.9 35.0 %collective-permute-done.19 = bf16[1024,384]{1,0:T(8,128)(2,1)S(1)} collective-permute-done((bf16[1024,384]{1,0:T(8,128)(2,1)S(1)}, bf16[1024,384]{1,0:T(8,128)(2,1)S(1)}, u32[]{:S(2)}, u32[]{:S(2)}) %collective-permute-start.19) | collective-permute-done | bytes 786464 | tf_op jit(solution)/shard_map/ppermute | solution.py:497
  304.8 11.9 %collective-permute-done.26 = bf16[256,1536]{1,0:T(8,128)(2,1)S(1)} collective-permute-done((bf16[256,1536]{1,0:T(8,128)(2,1)S(1)}, bf16[256,1536]{1,0:T(8,128)(2,1)S(1)}, u32[]{:S(2)}, u32[]{:S(2)}) %collective-permute-start.26) | collective-permute-done | bytes 786464 | tf_op jit(solution)/shard_map/ppermute | solution.py:524
  318.3 14.1 %collective-permute-start.27 = (bf16[512,1536]{1,0:T(8,128)(2,1)}, bf16[512,1536]{1,0:T(8,128)(2,1)}, u32[]{:S(2)}, u32[]{:S(2)}) collective-permute-start(bf16[512,1536]{1,0:T(8,128)(2,1)} %fusion.18), channel_id=1, source_target_pairs={{0,4},{4,0},{8,12},{12,8},{16,20},{20,16},{24,28},{28,24},{1,5},{5... | collective-permute-start | bytes 4718600 | tf_op jit(solution)/shard_map/ppermute | solution.py:493
  337.2 20.4 %inner_units.1 = (f32[1024,2048]{1,0:T(8,128)}, f32[1024,2048]{1,0:T(8,128)}, bf16[1024,2048]{1,0:T(8,128)(2,1)}) custom-call(bf16[1024,1536]{1,0:T(8,128)(2,1)} %pad_maximum_fusion.3.x_ref.refs_1_, bf16[4096,384]{1,0:T(8,128)(2,1)} %all-gather.8.cloned.1.call-done.refs_0_.refs_1_, bf16[4096,384]{1,0:T(8,128)(2,1)} %collective-permute-done.21.refs_1_.refs_2_, ...), custom_call_target="tpu_custom_call" | custom-call | flops 12884901888 | bytes 36700160 | tf_op jit(solution)/shard_map/inner_units/pallas_call | solution.py:326
  375.4 17.8 %inner_grads.1.refs_0_ = bf16[1024,4096]{1,0:T(8,128)(2,1)} custom-call(bf16[1024,1536]{1,0:T(8,128)(2,1)} %pad_maximum_fusion.1.x_ref.refs_1_, f32[1024,2048]{1,0:T(8,128)} %get-tuple-element.183.gate_ref, f32[1024,2048]{1,0:T(8,128)} %get-tuple-element.184.up_ref, bf16[2048,384]{1,0:T(8,128)(2,1)} %bitcast.172, ...), custom_call_target="tpu_custom_call" | custom-call | flops 6442450944 | bytes 34603008 | tf_op jit(solution)/shard_map/inner_grads/pallas_call | solution.py:353
  421.8 25.3 %combine.5 = (bf16[512,1536]{1,0:T(8,128)(2,1)}, f32[512,1536]{1,0:T(8,128)}) custom-call(s32[1]{0:T(128)} %bitcast.17.core_ref, bf16[1024,4096]{1,0:T(8,128)(2,1)} %inner_grads.1.refs_0_, bf16[4096,384]{1,0:T(8,128)(2,1)} %all-gather.8.cloned.1.call-done.refs_0_.refs_1_, bf16[4096,384]{1,0:T(8,128)(2,1)} %collective-permute-done.21.refs_1_.refs_2_, ...), custom_call_target="tpu_custom_call" | custom-call | flops 12884901888 | bytes 25690112 | tf_op jit(solution)/shard_map/combine/pallas_call | solution.py:263
  447.2 14.4 %combine.6 = (bf16[512,1536]{1,0:T(8,128)(2,1)}, f32[512,1536]{1,0:T(8,128)}) custom-call(s32[1]{0:T(128)} %bitcast.17.core_ref, bf16[1024,2048]{1,0:T(8,128)(2,1)} %get-tuple-element.200.refs_0_, bf16[2048,384]{1,0:T(8,128)(2,1)} %bitcast.173, bf16[2048,384]{1,0:T(8,128)(2,1)} %collective-permute-done.15.refs_1_.refs_2_, ...), custom_call_target="tpu_custom_call" | custom-call | flops 6442450944 | bytes 15204352 | tf_op jit(solution)/shard_map/combine/pallas_call | solution.py:263
  528.5 32.8 %shard_map.247 = (bf16[1024,768]{1,0:T(8,128)(2,1)}, bf16[1024,768]{1,0:T(8,128)(2,1)}, bf16[1024,768]{1,0:T(8,128)(2,1)}, f32[1024,768]{1,0:T(8,128)}) custom-call(s32[1]{0:T(128)} %bitcast.18.len_ref, bf16[1024,768]{1,0:T(8,128)(2,1)} %get-tuple-element.148.q_ref, bf16[1024,768]{1,0:T(8,128)(2,1)} %get-tuple-element.149.k_ref, ...), custom_call_target="tpu_custom_call" | custom-call | flops 16106127360 | bytes 18874368 | tf_op jit(solution)/shard_map/pallas_call | solution.py:169
  568.1 13.2 %collective-permute-done.43 = bf16[768,384]{1,0:T(8,128)(2,1)} collective-permute-done((bf16[768,384]{1,0:T(8,128)(2,1)}, bf16[768,384]{1,0:T(8,128)(2,1)}, u32[]{:S(2)}, u32[]{:S(2)}) %collective-permute-start.43) | collective-permute-done | bytes 589856 | tf_op jit(solution)/shard_map/ppermute | solution.py:700
  605.2 12.3 %total_sum.4 = bf16[4096,384]{1,0:T(8,128)(2,1)} custom-call(bf16[1024,4096]{1,0:T(8,128)(2,1)} %inner_grads.1.refs_0_, bf16[1024,1536]{1,0:T(8,128)(2,1)} %pad_maximum_fusion.3.x_ref.refs_1_, bf16[2048,384]{1,0:T(8,128)(2,1)} %collective-permute-done.40.refs_2_, bf16[2048,384]{1,0:T(8,128)(2,1)} %collective-permute-done.37.refs_3_, ...), custom_call_target="tpu_custom_call" | custom-call | flops 3221225472 | bytes 9437184 | tf_op jit(solution)/shard_map/total_sum/pallas_call | solution.py:464
  627.3 13.7 %collective-permute-done.49.refs_5_ = bf16[1184,384]{1,0:T(8,128)(2,1)} collective-permute-done((bf16[1184,384]{1,0:T(8,128)(2,1)}, bf16[1184,384]{1,0:T(8,128)(2,1)}, u32[]{:S(2)}, u32[]{:S(2)}) %collective-permute-start.49) | collective-permute-done | bytes 909344 | tf_op jit(solution)/shard_map/ppermute | solution.py:497
  651.3 17.1 %combine.7 = (bf16[512,1536]{1,0:T(8,128)(2,1)}, f32[512,1536]{1,0:T(8,128)}) custom-call(s32[1]{0:T(128)} %bitcast.17.core_ref, bf16[1024,768]{1,0:T(8,128)(2,1)} %get-tuple-element.230.refs_0_, bf16[1024,768]{1,0:T(8,128)(2,1)} %get-tuple-element.231.refs_1_, bf16[1024,768]{1,0:T(8,128)(2,1)} %get-tuple-element.232.refs_2_, ...), custom_call_target="tpu_custom_call" | custom-call | flops 7449083904 | bytes 16842752 | tf_op jit(solution)/shard_map/combine/pallas_call | solution.py:263
  687.8 8.1 collective-permute-done.58.refs_5_
  696.8 7.9 total_sum.3
  714.9 14.6 %reduce-scatter.9.cloned.1.call-done = bf16[192,384]{1,0:T(8,128)(2,1)} async-done(((bf16[768,384]{1,0:T(8,128)(2,1)}), bf16[192,384]{1,0:T(8,128)(2,1)}) %reduce-scatter.9.cloned.1.call-update) | async-done | bytes 147472 | tf_op jit(solution)/shard_map/reduce_scatter | solution.py:579
  737.4 50.9 %collective-permute-done.56 = f32[3096]{0:T(1024)S(1)} collective-permute-done((f32[3096]{0:T(1024)S(1)}, f32[3096]{0:T(1024)S(1)}, u32[]{:S(2)}, u32[]{:S(2)}) %collective-permute-start.56) | collective-permute-done | bytes 12416 | tf_op jit(solution)/shard_map/ppermute | solution.py:595
  789.6 7.5 collective-permute-done.57
  (435 shorter events, 349.1 us)
Async XLA Ops:
  7.2 50.7 %all-gather.4.cloned.1.call-start = ((), (), s32[]{:S(2)}) async-start(), calls=%async_computation.4 | async-start | bytes 2273280 | tf_op jit(solution)/shard_map/all_gather | solution.py:559
  14.0 132.1 %all-gather.6.cloned.1.call-start = ((), (), s32[]{:S(2)}) async-start(), calls=%async_computation.5 | async-start | bytes 2703360 | tf_op jit(solution)/shard_map/all_gather | solution.py:559
  20.2 186.0 %all-gather.8.cloned.1.call-start = ((), (), s32[]{:S(2)}) async-start(), calls=%async_computation.6 | async-start | bytes 3932160 | tf_op jit(solution)/shard_map/all_gather | solution.py:559
  106.6 510.9 %reduce-scatter.5.cloned.1.call-start = ((), (), s32[]{:S(2)}) async-start(), calls=%async_computation.7 | async-start | bytes 1966080 | tf_op jit(solution)/shard_map/reduce_scatter | solution.py:579
  152.7 80.7 %collective-permute-start.15 = (bf16[2048,384]{1,0:T(8,128)(2,1)S(1)}, bf16[2048,384]{1,0:T(8,128)(2,1)}, u32[]{:S(2)}, u32[]{:S(2)}) collective-permute-start(bf16[2048,384]{1,0:T(8,128)(2,1)S(1)} %bitcast.170), channel_id=1, source_target_pairs={{0,8},{4,12},{8,0},{12,4},{16,24},{20,28},{24,16},{28,20},{1,9},{5... | collective-permute-start | bytes 4718600 | tf_op jit(solution)/shard_map/ppermute | solution.py:497
  153.3 80.1 %collective-permute-start.16 = (bf16[2048,384]{1,0:T(8,128)(2,1)S(1)}, bf16[2048,384]{1,0:T(8,128)(2,1)}, u32[]{:S(2)}, u32[]{:S(2)}) collective-permute-start(bf16[2048,384]{1,0:T(8,128)(2,1)S(1)} %bitcast.171), channel_id=1, source_target_pairs={{0,16},{4,20},{8,24},{12,28},{16,0},{20,4},{24,8},{28,12},{1,17},{... | collective-permute-start | bytes 4718600 | tf_op jit(solution)/shard_map/ppermute | solution.py:497
  206.2 88.0 %collective-permute-start.21 = (bf16[4096,384]{1,0:T(8,128)(2,1)}, bf16[4096,384]{1,0:T(8,128)(2,1)}, u32[]{:S(2)}, u32[]{:S(2)}) collective-permute-start(bf16[4096,384]{1,0:T(8,128)(2,1)} %all-gather.8.cloned.1.call-done.refs_0_.refs_1_), channel_id=1, source_target_pairs={{0,8},{4,12},{8,0},{12,4},{16,24},{20,28},{24,16},{28,20},{1,9},{5... | collective-permute-start | bytes 9437192 | tf_op jit(solution)/shard_map/ppermute | solution.py:497
  206.7 87.5 %collective-permute-start.22 = (bf16[4096,384]{1,0:T(8,128)(2,1)}, bf16[4096,384]{1,0:T(8,128)(2,1)}, u32[]{:S(2)}, u32[]{:S(2)}) collective-permute-start(bf16[4096,384]{1,0:T(8,128)(2,1)} %all-gather.8.cloned.1.call-done.refs_0_.refs_1_), channel_id=1, source_target_pairs={{0,16},{4,20},{8,24},{12,28},{16,0},{20,4},{24,8},{28,12},{1,17},{... | collective-permute-start | bytes 9437192 | tf_op jit(solution)/shard_map/ppermute | solution.py:497
  421.3 51.1 %collective-permute-start.33 = (bf16[2048,384]{1,0:T(8,128)(2,1)}, bf16[2048,384]{1,0:T(8,128)(2,1)}, u32[]{:S(2)}, u32[]{:S(2)}) collective-permute-start(bf16[2048,384]{1,0:T(8,128)(2,1)} %fusion.25), channel_id=1, source_target_pairs={{0,8},{4,12},{8,0},{12,4},{16,24},{20,28},{24,16},{28,20},{1,9},{5... | collective-permute-start | bytes 4718600 | tf_op jit(solution)/shard_map/ppermute | solution.py:497
  494.3 214.1 %reduce-scatter.7.cloned.1.call-start = ((), (), s32[]{:S(2)}) async-start(), calls=%async_computation.8 | async-start | bytes 3932160 | tf_op jit(solution)/shard_map/reduce_scatter | solution.py:579
  516.9 64.5 %collective-permute-start.40 = (bf16[2048,384]{1,0:T(8,128)(2,1)}, bf16[2048,384]{1,0:T(8,128)(2,1)}, u32[]{:S(2)}, u32[]{:S(2)}) collective-permute-start(bf16[2048,384]{1,0:T(8,128)(2,1)} %term_sum.12), channel_id=1, source_target_pairs={{0,8},{4,12},{8,0},{12,4},{16,24},{20,28},{24,16},{28,20},{1,9},{5... | collective-permute-start | bytes 4718600 | tf_op jit(solution)/shard_map/ppermute | solution.py:497
  517.5 63.9 %collective-permute-start.41 = (bf16[2048,384]{1,0:T(8,128)(2,1)}, bf16[2048,384]{1,0:T(8,128)(2,1)}, u32[]{:S(2)}, u32[]{:S(2)}) collective-permute-start(bf16[2048,384]{1,0:T(8,128)(2,1)} %term_sum.13), channel_id=1, source_target_pairs={{0,16},{4,20},{8,24},{12,28},{16,0},{20,4},{24,8},{28,12},{1,17},{... | collective-permute-start | bytes 4718600 | tf_op jit(solution)/shard_map/ppermute | solution.py:497
  526.7 54.7 %collective-permute-start.43 = (bf16[768,384]{1,0:T(8,128)(2,1)}, bf16[768,384]{1,0:T(8,128)(2,1)}, u32[]{:S(2)}, u32[]{:S(2)}) collective-permute-start(bf16[768,384]{1,0:T(8,128)(2,1)} %convolution_convert_fusion.1), channel_id=1, source_target_pairs={{0,16},{4,20},{8,24},{12,28},{16,0},{20,4},{24,8},{28,12},{1,17},{... | collective-permute-start | bytes 1769480 | tf_op jit(solution)/shard_map/ppermute | solution.py:700
  528.0 53.3 %collective-permute-start.44 = (bf16[768,384]{1,0:T(8,128)(2,1)}, bf16[768,384]{1,0:T(8,128)(2,1)}, u32[]{:S(2)}, u32[]{:S(2)}) collective-permute-start(bf16[768,384]{1,0:T(8,128)(2,1)} %convolution_convert_fusion), channel_id=1, source_target_pairs={{0,24},{4,28},{8,16},{12,20},{16,8},{20,12},{24,0},{28,4},{1,25},{... | collective-permute-start | bytes 1769480 | tf_op jit(solution)/shard_map/ppermute | solution.py:700
  617.5 112.0 %reduce-scatter.9.cloned.1.call-start = ((), (), s32[]{:S(2)}) async-start(), calls=%async_computation.9 | async-start | bytes 737280 | tf_op jit(solution)/shard_map/reduce_scatter | solution.py:579
  621.4 52.8 %collective-permute-start.65 = (bf16[512,192]{1,0:T(8,128)(2,1)}, bf16[512,192]{1,0:T(8,128)(2,1)}, u32[]{:S(2)}, u32[]{:S(2)}) collective-permute-start(bf16[512,192]{1,0:T(8,128)(2,1)} %constant_dynamic-slice_fusion), channel_id=1, source_target_pairs={{0,4},{4,0},{8,12},{12,8},{16,20},{20,16},{24,28},{28,24},{1,5},{5... | collective-permute-start | bytes 589832 | tf_op jit(solution)/shard_map/ppermute | solution.py:493
  621.4 57.4 %collective-permute-start.59 = (bf16[1184,384]{1,0:T(8,128)(2,1)}, bf16[1184,384]{1,0:T(8,128)(2,1)}, u32[]{:S(2)}, u32[]{:S(2)}) collective-permute-start(bf16[1184,384]{1,0:T(8,128)(2,1)} %term_sum.17), channel_id=1, source_target_pairs={{0,16},{4,20},{8,24},{12,28},{16,0},{20,4},{24,8},{28,12},{1,17},{... | collective-permute-start | bytes 2727944 | tf_op jit(solution)/shard_map/ppermute | solution.py:497
  622.6 57.8 %collective-permute-start.60 = (bf16[1184,384]{1,0:T(8,128)(2,1)}, bf16[1184,384]{1,0:T(8,128)(2,1)}, u32[]{:S(2)}, u32[]{:S(2)}) collective-permute-start(bf16[1184,384]{1,0:T(8,128)(2,1)} %term_sum.16), channel_id=1, source_target_pairs={{0,8},{4,12},{8,0},{12,4},{16,24},{20,28},{24,16},{28,20},{1,9},{5... | collective-permute-start | bytes 2727944 | tf_op jit(solution)/shard_map/ppermute | solution.py:497
  678.8 57.0 %collective-permute-start.47 = (bf16[256,1536]{1,0:T(8,128)(2,1)}, bf16[256,1536]{1,0:T(8,128)(2,1)}, u32[]{:S(2)}, u32[]{:S(2)}) collective-permute-start(bf16[256,1536]{1,0:T(8,128)(2,1)} %pad_maximum_fusion.21), channel_id=1, source_target_pairs={{2,0},{0,1},{6,2},{4,3},{3,4},{1,5},{7,6},{5,7},{10,8},{8,9},{14,1... | collective-permute-start | bytes 2359304 | tf_op jit(solution)/shard_map/ppermute | solution.py:537
  680.4 55.4 %collective-permute-start.46 = (bf16[256,1536]{1,0:T(8,128)(2,1)}, bf16[256,1536]{1,0:T(8,128)(2,1)}, u32[]{:S(2)}, u32[]{:S(2)}) collective-permute-start(bf16[256,1536]{1,0:T(8,128)(2,1)} %pad_maximum_fusion.20), channel_id=1, source_target_pairs={{0,0},{2,1},{4,2},{6,3},{1,4},{3,5},{5,6},{7,7},{8,8},{10,9},{12,1... | collective-permute-start | bytes 2359304 | tf_op jit(solution)/shard_map/ppermute | solution.py:537
  708.5 96.3 %reduce-scatter.11.cloned.1.call-start = ((), (), s32[]{:S(2)}) async-start(), calls=%async_computation.10 | async-start | bytes 2273280 | tf_op jit(solution)/shard_map/reduce_scatter | solution.py:579
  729.6 69.0 %collective-permute-start.52 = (bf16[256,1536]{1,0:T(8,128)(2,1)S(1)}, bf16[256,1536]{1,0:T(8,128)(2,1)S(1)}, u32[]{:S(2)}, u32[]{:S(2)}) collective-permute-start(bf16[256,1536]{1,0:T(8,128)(2,1)S(1)} %pad_maximum_fusion.23), channel_id=1, source_target_pairs={{2,0},{0,1},{6,2},{4,3},{3,4},{1,5},{7,6},{5,7},{10,8},{8,9},{14,1... | collective-permute-start | bytes 2359304 | tf_op jit(solution)/shard_map/ppermute | solution.py:537
  731.3 67.2 %collective-permute-start.51 = (bf16[256,1536]{1,0:T(8,128)(2,1)S(1)}, bf16[256,1536]{1,0:T(8,128)(2,1)S(1)}, u32[]{:S(2)}, u32[]{:S(2)}) collective-permute-start(bf16[256,1536]{1,0:T(8,128)(2,1)S(1)} %pad_maximum_fusion.22), channel_id=1, source_target_pairs={{0,0},{2,1},{4,2},{6,3},{1,4},{3,5},{5,6},{7,7},{8,8},{10,9},{12,1... | collective-permute-start | bytes 2359304 | tf_op jit(solution)/shard_map/ppermute | solution.py:537
  733.5 54.8 %collective-permute-start.56 = (f32[3096]{0:T(1024)S(1)}, f32[3096]{0:T(1024)S(1)}, u32[]{:S(2)}, u32[]{:S(2)}) collective-permute-start(f32[3096]{0:T(1024)S(1)} %add.360), channel_id=1, source_target_pairs={{0,1},{1,0},{2,3},{3,2},{4,5},{5,4},{6,7},{7,6},{8,9},{9,8},{10,11... | collective-permute-start | bytes 37160 | tf_op jit(solution)/shard_map/ppermute | solution.py:595
  (93 other events, 1923.6 us)
Sparse Core Ops, SparseCore 0:
  14.2 43.6 all-gather.3
  59.4 77.5 all-gather.5
  139.2 62.5 all-gather.7
  494.5 32.7 reduce-scatter.4
  617.6 58.7 reduce-scatter.6
  708.6 20.8 reduce-scatter.8
  731.8 56.4 reduce-scatter.10

commit v7 on v6

--- a/solution.py
+++ b/solution.py
@@ -873,8 +873,11 @@
         two_sum.got, two_sum.last, out_sum.got, query_low, key_low, value_low, grad_cumul
     )
     out_sum.prepare_second()
-    out_sum.second, grad_cumul = together(out_sum.second, grad_cumul)
     out_sum.send_second()
+    out_total, grad_cumul = together(out_sum.finish(), grad_cumul)
+    down_pair = plan.scatter(down_sum.finish())
+    out_total, down_pair = together(out_total, down_pair)
+    out_pair = plan.scatter(out_total)
     grad_logf = jnp.flip(jnp.cumsum(jnp.flip(grad_cumul, 0), axis=0), 0)
     grad_logit = grad_logf * jax.nn.sigmoid(-forget_logit)
     bias_term = jnp.sum(grad_logit, axis=0)
@@ -884,17 +887,15 @@
     ).reshape(seq_rows, -1)
     grad_one = [query_low, key_low, value_low, logit_low]
     one_sum = Reduction(plan, grad_one, normed_one)
-    one_sum.first, out_sum.last, two_sum.last, outputs = together(
-        one_sum.first, out_sum.last, two_sum.last, outputs
-    )
+    one_sum.first, two_sum.last, outputs = together(one_sum.first, two_sum.last, outputs)
     one_sum.send_first()
     outputs = plan.from_chip(outputs)
     one_sum.prepare_second()
-    one_sum.second, grad_one = together(one_sum.second, grad_one)
     one_sum.send_second()
-    down_pair = plan.scatter(down_sum.finish())
-    two_total, down_pair = together(two_sum.finish(), down_pair)
+    two_total, out_pair = together(two_sum.finish(), out_pair)
     two_pair = plan.scatter(two_total)
+    one_total, two_pair, grad_one = together(one_sum.finish(), two_pair, grad_one)
+    one_pair = plan.scatter(one_total)
     grad_normed_one = plan.sum_rows(*combine(core, grad_one, kinds_one))
     gain_one_term = jnp.sum(grad_normed_one * rows_in * scale_one, axis=0)
     input_grad = plan.from_chip(
@@ -909,10 +910,6 @@
         jnp.concatenate([plan.by_chip(gain_one_term), plan.by_chip(gain_two_term), bias_full])
     )
 
-    out_total, two_pair = together(out_sum.finish(), two_pair)
-    out_pair = plan.scatter(out_total)
-    one_total, out_pair = together(one_sum.finish(), out_pair)
-    one_pair = plan.scatter(one_total)
     down_shard, two_shard = plan.share(down_pair), plan.share(two_pair)
     out_shard, one_shard = plan.share(out_pair), plan.share(one_pair)
 

time: 829 us -> 825 us (level)
    ppermute x2, waiting for transfers between devices: 58.4 us -> 48.1 us  [sum_all(): vector = vector + lax.ppermute(vector, 'tensor', perm)]
    ppermute x36, waiting for transfers between devices: 117 us -> 127 us  [swap_chip(): return lax.ppermute(array, 'dp', perm)]
where the time goes in v7:
time: 825 us; the launch traced here: 814 us
  waiting for transfers between devices  260 us (32%)
  Pallas kernels  259 us (31%)
  starting transfers between devices  101 us (12%)
  other arithmetic  76.4 us (9%)
  local copies, waits for them, and re-layouts  67.1 us (8%)
  matrix products  34.8 us (4%)
  between operations  15.8 us (2%)
    ppermute x36, waiting for transfers between devices, swap_chip(): return lax.ppermute(array, 'dp', perm)  127 us
    pallas_call x4, Pallas kernels, combine(): pl.pallas_call(functools.partial(combine_kernel, lefts=len(lefts)), grid_...  64.3 us
    ppermute x2, waiting for transfers between devices, sum_all(): vector = vector + lax.ppermute(vector, 'tensor', perm)  48.1 us
    pallas_call x10, Pallas kernels, term_sum(): pl.pallas_call(functools.partial(term_kernel, narrow=narrow, side=side),...  47.4 us
    ppermute x36, starting transfers between devices, swap_chip(): return lax.ppermute(array, 'dp', perm)  42 us
    all_gather x3, waiting for transfers between devices, line_gather(): return lax.all_gather(pair, 'tensor', axis=0, tiled=True)  37.7 us
    dot_general x12, matrix products, dot_first(): lax.dot_general(left, right, (((0,), (0,)), ((), ())), preferred_element_...  34.8 us
    pallas_call x1, Pallas kernels, attn_bwd(): pl.pallas_call(functools.partial(attn_bwd_kernel, blk=blk), grid=(pairs,)...  32.8 us
  transfers between devices with their start and end apart: 73, of which 26 were waited for; matrix products, arithmetic and copies ran while one was open for 18% of the time, Pallas kernels for 31%

profile of v7, /device:TPU:0, one launch (start us, length us, event | category | flops | bytes accessed | tf_op | source)
XLA Modules:
  0.0 814.3 jit_solution(4753382246878358434)
XLA Ops:
  20.1 37.7 %all-gather.4.cloned.1.call-done.refs_0_ = bf16[2368,384]{1,0:T(8,128)(2,1)} async-done(((bf16[592,384]{1,0:T(8,128)(2,1)}), bf16[2368,384]{1,0:T(8,128)(2,1)}) %all-gather.4.cloned.1.call-update) | async-done | bytes 1818640 | tf_op jit(solution)/shard_map/all_gather | solution.py:559
  71.6 7.4 collective-permute-start.1
  80.3 18.9 %collective-permute-done.3.refs_1_ = bf16[2368,384]{1,0:T(8,128)(2,1)S(1)} collective-permute-done((bf16[2368,384]{1,0:T(8,128)(2,1)}, bf16[2368,384]{1,0:T(8,128)(2,1)S(1)}, u32[]{:S(2)}, u32[]{:S(2)}) %collective-permute-start.3) | collective-permute-done | bytes 1818656 | tf_op jit(solution)/shard_map/ppermute | solution.py:497
  130.2 15.6 %collective-permute-start.8 = (bf16[512,1536]{1,0:T(8,128)(2,1)}, bf16[512,1536]{1,0:T(8,128)(2,1)}, u32[]{:S(2)}, u32[]{:S(2)}) collective-permute-start(bf16[512,1536]{1,0:T(8,128)(2,1)} %fusion.10), channel_id=1, source_target_pairs={{0,4},{4,0},{8,12},{12,8},{16,20},{20,16},{24,28},{28,24},{1,5},{5... | collective-permute-start | bytes 4718600 | tf_op jit(solution)/shard_map/ppermute | solution.py:493
  157.8 16.3 %project.1 = (bf16[1024,768]{1,0:T(8,128)(2,1)}, bf16[1024,768]{1,0:T(8,128)(2,1)}, bf16[1024,768]{1,0:T(8,128)(2,1)}, f32[2,1024,32]{2,1,0:T(8,128)}) custom-call(bf16[1024,1536]{1,0:T(8,128)(2,1)} %pad_maximum_fusion.2.x_ref.refs_4_, bf16[2368,384]{1,0:T(8,128)(2,1)} %all-gather.4.cloned.1.call-done.refs_0_, bf16[2368,384]{1,0:T(8,128)(2,1)} %copy-done.14, ...), custom_call_target="tpu_custom_call" | custom-call | flops 7449083904 | bytes 15138816 | tf_op jit(solution)/shard_map/project/pallas_call | solution.py:217
  189.8 15.4 %collective-permute-done.12 = bf16[384,384]{1,0:T(8,128)(2,1)S(1)} collective-permute-done((bf16[384,384]{1,0:T(8,128)(2,1)S(1)}, bf16[384,384]{1,0:T(8,128)(2,1)S(1)}, u32[]{:S(2)}, u32[]{:S(2)}) %collective-permute-start.12) | collective-permute-done | bytes 294944 | tf_op jit(solution)/shard_map/ppermute | solution.py:497
  208.2 25.2 %shard_map.246 = (bf16[1024,768]{1,0:T(8,128)(2,1)}, f32[1024,768]{1,0:T(8,128)}) custom-call(s32[1]{0:T(128)} %bitcast.18.len_ref, bf16[1024,768]{1,0:T(8,128)(2,1)} %get-tuple-element.148.q_ref, bf16[1024,768]{1,0:T(8,128)(2,1)} %get-tuple-element.149.k_ref, bf16[1024,768]{1,0:T(8,128)(2,1)} %get-tuple-element.150.v_ref, f32[6,1024,2]{2,1,0:T(8,128)} %bitcast.181), custom_call_target="tpu_custom_call" | custom-call | flops 6442450944 | bytes 9437184 | tf_op jit(solution)/shard_map/pallas_call | solution.py:97
  233.6 7.7 combine.4
  257.8 35.0 %collective-permute-done.19 = bf16[1024,384]{1,0:T(8,128)(2,1)S(1)} collective-permute-done((bf16[1024,384]{1,0:T(8,128)(2,1)S(1)}, bf16[1024,384]{1,0:T(8,128)(2,1)S(1)}, u32[]{:S(2)}, u32[]{:S(2)}) %collective-permute-start.19) | collective-permute-done | bytes 786464 | tf_op jit(solution)/shard_map/ppermute | solution.py:497
  304.7 11.9 %collective-permute-done.26 = bf16[256,1536]{1,0:T(8,128)(2,1)S(1)} collective-permute-done((bf16[256,1536]{1,0:T(8,128)(2,1)S(1)}, bf16[256,1536]{1,0:T(8,128)(2,1)S(1)}, u32[]{:S(2)}, u32[]{:S(2)}) %collective-permute-start.26) | collective-permute-done | bytes 786464 | tf_op jit(solution)/shard_map/ppermute | solution.py:524
  318.2 14.0 %collective-permute-start.27 = (bf16[512,1536]{1,0:T(8,128)(2,1)}, bf16[512,1536]{1,0:T(8,128)(2,1)}, u32[]{:S(2)}, u32[]{:S(2)}) collective-permute-start(bf16[512,1536]{1,0:T(8,128)(2,1)} %fusion.18), channel_id=1, source_target_pairs={{0,4},{4,0},{8,12},{12,8},{16,20},{20,16},{24,28},{28,24},{1,5},{5... | collective-permute-start | bytes 4718600 | tf_op jit(solution)/shard_map/ppermute | solution.py:493
  337.1 20.5 %inner_units.1 = (f32[1024,2048]{1,0:T(8,128)}, f32[1024,2048]{1,0:T(8,128)}, bf16[1024,2048]{1,0:T(8,128)(2,1)}) custom-call(bf16[1024,1536]{1,0:T(8,128)(2,1)} %pad_maximum_fusion.3.x_ref.refs_1_, bf16[4096,384]{1,0:T(8,128)(2,1)} %all-gather.8.cloned.1.call-done.refs_0_.refs_1_, bf16[4096,384]{1,0:T(8,128)(2,1)} %collective-permute-done.21.refs_1_.refs_2_, ...), custom_call_target="tpu_custom_call" | custom-call | flops 12884901888 | bytes 36700160 | tf_op jit(solution)/shard_map/inner_units/pallas_call | solution.py:326
  375.3 17.8 %inner_grads.1.refs_0_ = bf16[1024,4096]{1,0:T(8,128)(2,1)} custom-call(bf16[1024,1536]{1,0:T(8,128)(2,1)} %pad_maximum_fusion.1.x_ref.refs_1_, f32[1024,2048]{1,0:T(8,128)} %get-tuple-element.183.gate_ref, f32[1024,2048]{1,0:T(8,128)} %get-tuple-element.184.up_ref, bf16[2048,384]{1,0:T(8,128)(2,1)} %bitcast.172, ...), custom_call_target="tpu_custom_call" | custom-call | flops 6442450944 | bytes 34603008 | tf_op jit(solution)/shard_map/inner_grads/pallas_call | solution.py:353
  421.8 25.3 %combine.5 = (bf16[512,1536]{1,0:T(8,128)(2,1)}, f32[512,1536]{1,0:T(8,128)}) custom-call(s32[1]{0:T(128)} %bitcast.17.core_ref, bf16[1024,4096]{1,0:T(8,128)(2,1)} %inner_grads.1.refs_0_, bf16[4096,384]{1,0:T(8,128)(2,1)} %all-gather.8.cloned.1.call-done.refs_0_.refs_1_, bf16[4096,384]{1,0:T(8,128)(2,1)} %collective-permute-done.21.refs_1_.refs_2_, ...), custom_call_target="tpu_custom_call" | custom-call | flops 12884901888 | bytes 25690112 | tf_op jit(solution)/shard_map/combine/pallas_call | solution.py:263
  447.1 14.4 %combine.6 = (bf16[512,1536]{1,0:T(8,128)(2,1)}, f32[512,1536]{1,0:T(8,128)}) custom-call(s32[1]{0:T(128)} %bitcast.17.core_ref, bf16[1024,2048]{1,0:T(8,128)(2,1)} %get-tuple-element.200.refs_0_, bf16[2048,384]{1,0:T(8,128)(2,1)} %bitcast.173, bf16[2048,384]{1,0:T(8,128)(2,1)} %collective-permute-done.15.refs_1_.refs_2_, ...), custom_call_target="tpu_custom_call" | custom-call | flops 6442450944 | bytes 15204352 | tf_op jit(solution)/shard_map/combine/pallas_call | solution.py:263
  528.5 32.8 %shard_map.247 = (bf16[1024,768]{1,0:T(8,128)(2,1)}, bf16[1024,768]{1,0:T(8,128)(2,1)}, bf16[1024,768]{1,0:T(8,128)(2,1)}, f32[1024,768]{1,0:T(8,128)}) custom-call(s32[1]{0:T(128)} %bitcast.18.len_ref, bf16[1024,768]{1,0:T(8,128)(2,1)} %get-tuple-element.148.q_ref, bf16[1024,768]{1,0:T(8,128)(2,1)} %get-tuple-element.149.k_ref, ...), custom_call_target="tpu_custom_call" | custom-call | flops 16106127360 | bytes 18874368 | tf_op jit(solution)/shard_map/pallas_call | solution.py:169
  568.1 13.2 %collective-permute-done.43 = bf16[768,384]{1,0:T(8,128)(2,1)} collective-permute-done((bf16[768,384]{1,0:T(8,128)(2,1)}, bf16[768,384]{1,0:T(8,128)(2,1)}, u32[]{:S(2)}, u32[]{:S(2)}) %collective-permute-start.43) | collective-permute-done | bytes 589856 | tf_op jit(solution)/shard_map/ppermute | solution.py:700
  609.1 12.3 %total_sum.4 = bf16[4096,384]{1,0:T(8,128)(2,1)} custom-call(bf16[1024,4096]{1,0:T(8,128)(2,1)} %inner_grads.1.refs_0_, bf16[1024,1536]{1,0:T(8,128)(2,1)} %pad_maximum_fusion.3.x_ref.refs_1_, bf16[2048,384]{1,0:T(8,128)(2,1)} %collective-permute-done.40.refs_2_, bf16[2048,384]{1,0:T(8,128)(2,1)} %collective-permute-done.37.refs_3_, ...), custom_call_target="tpu_custom_call" | custom-call | flops 3221225472 | bytes 9437184 | tf_op jit(solution)/shard_map/total_sum/pallas_call | solution.py:464
  631.1 13.8 %collective-permute-done.52.refs_5_ = bf16[1184,384]{1,0:T(8,128)(2,1)} collective-permute-done((bf16[1184,384]{1,0:T(8,128)(2,1)}, bf16[1184,384]{1,0:T(8,128)(2,1)}, u32[]{:S(2)}, u32[]{:S(2)}) %collective-permute-start.52) | collective-permute-done | bytes 909344 | tf_op jit(solution)/shard_map/ppermute | solution.py:497
  667.4 15.9 %collective-permute-done.53.refs_8_ = bf16[1184,384]{1,0:T(8,128)(2,1)} collective-permute-done((bf16[1184,384]{1,0:T(8,128)(2,1)}, bf16[1184,384]{1,0:T(8,128)(2,1)}, u32[]{:S(2)}, u32[]{:S(2)}) %collective-permute-start.53) | collective-permute-done | bytes 909344 | tf_op jit(solution)/shard_map/ppermute | solution.py:497
  683.3 8.1 total_sum.3
  699.3 16.9 %combine.7 = (bf16[512,1536]{1,0:T(8,128)(2,1)}, f32[512,1536]{1,0:T(8,128)}) custom-call(s32[1]{0:T(128)} %bitcast.17.core_ref, bf16[1024,768]{1,0:T(8,128)(2,1)} %get-tuple-element.247.refs_0_, bf16[1024,768]{1,0:T(8,128)(2,1)} %get-tuple-element.248.refs_1_, bf16[1024,768]{1,0:T(8,128)(2,1)} %get-tuple-element.249.refs_2_, ...), custom_call_target="tpu_custom_call" | custom-call | flops 7449083904 | bytes 16842752 | tf_op jit(solution)/shard_map/combine/pallas_call | solution.py:263
  733.2 7.4 collective-permute-start.55
  744.7 43.4 %collective-permute-done.60 = f32[3096]{0:T(1024)S(1)} collective-permute-done((f32[3096]{0:T(1024)S(1)}, f32[3096]{0:T(1024)S(1)}, u32[]{:S(2)}, u32[]{:S(2)}) %collective-permute-start.60) | collective-permute-done | bytes 12416 | tf_op jit(solution)/shard_map/ppermute | solution.py:595
  (447 shorter events, 351.2 us)
Async XLA Ops:
  7.2 50.7 %all-gather.4.cloned.1.call-start = ((), (), s32[]{:S(2)}) async-start(), calls=%async_computation.4 | async-start | bytes 2273280 | tf_op jit(solution)/shard_map/all_gather | solution.py:559
  14.0 132.1 %all-gather.6.cloned.1.call-start = ((), (), s32[]{:S(2)}) async-start(), calls=%async_computation.5 | async-start | bytes 2703360 | tf_op jit(solution)/shard_map/all_gather | solution.py:559
  20.1 186.0 %all-gather.8.cloned.1.call-start = ((), (), s32[]{:S(2)}) async-start(), calls=%async_computation.6 | async-start | bytes 3932160 | tf_op jit(solution)/shard_map/all_gather | solution.py:559
  106.6 478.5 %reduce-scatter.5.cloned.1.call-start = ((), (), s32[]{:S(2)}) async-start(), calls=%async_computation.7 | async-start | bytes 1966080 | tf_op jit(solution)/shard_map/reduce_scatter | solution.py:579
  152.6 80.7 %collective-permute-start.15 = (bf16[2048,384]{1,0:T(8,128)(2,1)S(1)}, bf16[2048,384]{1,0:T(8,128)(2,1)}, u32[]{:S(2)}, u32[]{:S(2)}) collective-permute-start(bf16[2048,384]{1,0:T(8,128)(2,1)S(1)} %bitcast.170), channel_id=1, source_target_pairs={{0,8},{4,12},{8,0},{12,4},{16,24},{20,28},{24,16},{28,20},{1,9},{5... | collective-permute-start | bytes 4718600 | tf_op jit(solution)/shard_map/ppermute | solution.py:497
  153.2 80.1 %collective-permute-start.16 = (bf16[2048,384]{1,0:T(8,128)(2,1)S(1)}, bf16[2048,384]{1,0:T(8,128)(2,1)}, u32[]{:S(2)}, u32[]{:S(2)}) collective-permute-start(bf16[2048,384]{1,0:T(8,128)(2,1)S(1)} %bitcast.171), channel_id=1, source_target_pairs={{0,16},{4,20},{8,24},{12,28},{16,0},{20,4},{24,8},{28,12},{1,17},{... | collective-permute-start | bytes 4718600 | tf_op jit(solution)/shard_map/ppermute | solution.py:497
  206.1 88.0 %collective-permute-start.21 = (bf16[4096,384]{1,0:T(8,128)(2,1)}, bf16[4096,384]{1,0:T(8,128)(2,1)}, u32[]{:S(2)}, u32[]{:S(2)}) collective-permute-start(bf16[4096,384]{1,0:T(8,128)(2,1)} %all-gather.8.cloned.1.call-done.refs_0_.refs_1_), channel_id=1, source_target_pairs={{0,8},{4,12},{8,0},{12,4},{16,24},{20,28},{24,16},{28,20},{1,9},{5... | collective-permute-start | bytes 9437192 | tf_op jit(solution)/shard_map/ppermute | solution.py:497
  206.7 87.5 %collective-permute-start.22 = (bf16[4096,384]{1,0:T(8,128)(2,1)}, bf16[4096,384]{1,0:T(8,128)(2,1)}, u32[]{:S(2)}, u32[]{:S(2)}) collective-permute-start(bf16[4096,384]{1,0:T(8,128)(2,1)} %all-gather.8.cloned.1.call-done.refs_0_.refs_1_), channel_id=1, source_target_pairs={{0,16},{4,20},{8,24},{12,28},{16,0},{20,4},{24,8},{28,12},{1,17},{... | collective-permute-start | bytes 9437192 | tf_op jit(solution)/shard_map/ppermute | solution.py:497
  244.6 48.3 %collective-permute-start.19 = (bf16[1024,384]{1,0:T(8,128)(2,1)S(1)}, bf16[1024,384]{1,0:T(8,128)(2,1)S(1)}, u32[]{:S(2)}, u32[]{:S(2)}) collective-permute-start(bf16[1024,384]{1,0:T(8,128)(2,1)S(1)} %slice.183), channel_id=1, source_target_pairs={{0,16},{4,20},{8,24},{12,28},{16,0},{20,4},{24,8},{28,12},{1,17},{... | collective-permute-start | bytes 2359304 | tf_op jit(solution)/shard_map/ppermute | solution.py:497
  413.9 47.6 %collective-permute-start.35 = (bf16[1024,384]{1,0:T(8,128)(2,1)}, bf16[1024,384]{1,0:T(8,128)(2,1)}, u32[]{:S(2)}, u32[]{:S(2)}) collective-permute-start(bf16[1024,384]{1,0:T(8,128)(2,1)} %term_sum.11), channel_id=1, source_target_pairs={{0,16},{4,20},{8,24},{12,28},{16,0},{20,4},{24,8},{28,12},{1,17},{... | collective-permute-start | bytes 2359304 | tf_op jit(solution)/shard_map/ppermute | solution.py:497
  419.8 48.4 %collective-permute-start.32 = (bf16[2048,384]{1,0:T(8,128)(2,1)}, bf16[2048,384]{1,0:T(8,128)(2,1)}, u32[]{:S(2)}, u32[]{:S(2)}) collective-permute-start(bf16[2048,384]{1,0:T(8,128)(2,1)} %fusion.19), channel_id=1, source_target_pairs={{0,16},{4,20},{8,24},{12,28},{16,0},{20,4},{24,8},{28,12},{1,17},{... | collective-permute-start | bytes 4718600 | tf_op jit(solution)/shard_map/ppermute | solution.py:497
  421.3 51.0 %collective-permute-start.33 = (bf16[2048,384]{1,0:T(8,128)(2,1)}, bf16[2048,384]{1,0:T(8,128)(2,1)}, u32[]{:S(2)}, u32[]{:S(2)}) collective-permute-start(bf16[2048,384]{1,0:T(8,128)(2,1)} %fusion.25), channel_id=1, source_target_pairs={{0,8},{4,12},{8,0},{12,4},{16,24},{20,28},{24,16},{28,20},{1,9},{5... | collective-permute-start | bytes 4718600 | tf_op jit(solution)/shard_map/ppermute | solution.py:497
  494.3 127.1 %reduce-scatter.7.cloned.1.call-start = ((), (), s32[]{:S(2)}) async-start(), calls=%async_computation.8 | async-start | bytes 737280 | tf_op jit(solution)/shard_map/reduce_scatter | solution.py:579
  516.9 64.4 %collective-permute-start.40 = (bf16[2048,384]{1,0:T(8,128)(2,1)}, bf16[2048,384]{1,0:T(8,128)(2,1)}, u32[]{:S(2)}, u32[]{:S(2)}) collective-permute-start(bf16[2048,384]{1,0:T(8,128)(2,1)} %term_sum.12), channel_id=1, source_target_pairs={{0,8},{4,12},{8,0},{12,4},{16,24},{20,28},{24,16},{28,20},{1,9},{5... | collective-permute-start | bytes 4718600 | tf_op jit(solution)/shard_map/ppermute | solution.py:497
  517.6 63.7 %collective-permute-start.41 = (bf16[2048,384]{1,0:T(8,128)(2,1)}, bf16[2048,384]{1,0:T(8,128)(2,1)}, u32[]{:S(2)}, u32[]{:S(2)}) collective-permute-start(bf16[2048,384]{1,0:T(8,128)(2,1)} %term_sum.13), channel_id=1, source_target_pairs={{0,16},{4,20},{8,24},{12,28},{16,0},{20,4},{24,8},{28,12},{1,17},{... | collective-permute-start | bytes 4718600 | tf_op jit(solution)/shard_map/ppermute | solution.py:497
  518.0 50.1 %collective-permute-start.42 = (bf16[768,384]{1,0:T(8,128)(2,1)}, bf16[768,384]{1,0:T(8,128)(2,1)}, u32[]{:S(2)}, u32[]{:S(2)}) collective-permute-start(bf16[768,384]{1,0:T(8,128)(2,1)} %convolution_convert_fusion.2), channel_id=1, source_target_pairs={{0,8},{4,12},{8,0},{12,4},{16,24},{20,28},{24,16},{28,20},{1,9},{5... | collective-permute-start | bytes 1769480 | tf_op jit(solution)/shard_map/ppermute | solution.py:700
  526.7 54.6 %collective-permute-start.43 = (bf16[768,384]{1,0:T(8,128)(2,1)}, bf16[768,384]{1,0:T(8,128)(2,1)}, u32[]{:S(2)}, u32[]{:S(2)}) collective-permute-start(bf16[768,384]{1,0:T(8,128)(2,1)} %convolution_convert_fusion.1), channel_id=1, source_target_pairs={{0,16},{4,20},{8,24},{12,28},{16,0},{20,4},{24,8},{28,12},{1,17},{... | collective-permute-start | bytes 1769480 | tf_op jit(solution)/shard_map/ppermute | solution.py:700
  528.1 53.3 %collective-permute-start.44 = (bf16[768,384]{1,0:T(8,128)(2,1)}, bf16[768,384]{1,0:T(8,128)(2,1)}, u32[]{:S(2)}, u32[]{:S(2)}) collective-permute-start(bf16[768,384]{1,0:T(8,128)(2,1)} %convolution_convert_fusion), channel_id=1, source_target_pairs={{0,24},{4,28},{8,16},{12,20},{16,8},{20,12},{24,0},{28,4},{1,25},{... | collective-permute-start | bytes 1769480 | tf_op jit(solution)/shard_map/ppermute | solution.py:700
  585.2 113.3 %reduce-scatter.9.cloned.1.call-start = ((), (), s32[]{:S(2)}) async-start(), calls=%async_computation.9 | async-start | bytes 3932160 | tf_op jit(solution)/shard_map/reduce_scatter | solution.py:579
  621.5 178.9 %reduce-scatter.11.cloned.1.call-start = ((), (), s32[]{:S(2)}) async-start(), calls=%async_computation.10 | async-start | bytes 2273280 | tf_op jit(solution)/shard_map/reduce_scatter | solution.py:579
  657.5 58.8 %collective-permute-start.47 = (bf16[256,1536]{1,0:T(8,128)(2,1)}, bf16[256,1536]{1,0:T(8,128)(2,1)}, u32[]{:S(2)}, u32[]{:S(2)}) collective-permute-start(bf16[256,1536]{1,0:T(8,128)(2,1)} %pad_maximum_fusion.21), channel_id=1, source_target_pairs={{2,0},{0,1},{6,2},{4,3},{3,4},{1,5},{7,6},{5,7},{10,8},{8,9},{14,1... | collective-permute-start | bytes 2359304 | tf_op jit(solution)/shard_map/ppermute | solution.py:537
  665.6 50.7 %collective-permute-start.46 = (bf16[256,1536]{1,0:T(8,128)(2,1)}, bf16[256,1536]{1,0:T(8,128)(2,1)S(1)}, u32[]{:S(2)}, u32[]{:S(2)}) collective-permute-start(bf16[256,1536]{1,0:T(8,128)(2,1)} %pad_maximum_fusion.20), channel_id=1, source_target_pairs={{0,0},{2,1},{4,2},{6,3},{1,4},{3,5},{5,6},{7,7},{8,8},{10,9},{12,1... | collective-permute-start | bytes 2359304 | tf_op jit(solution)/shard_map/ppermute | solution.py:537
  730.3 68.6 %collective-permute-start.56 = (bf16[256,1536]{1,0:T(8,128)(2,1)S(1)}, bf16[256,1536]{1,0:T(8,128)(2,1)}, u32[]{:S(2)}, u32[]{:S(2)}) collective-permute-start(bf16[256,1536]{1,0:T(8,128)(2,1)S(1)} %pad_maximum_fusion.23), channel_id=1, source_target_pairs={{2,0},{0,1},{6,2},{4,3},{3,4},{1,5},{7,6},{5,7},{10,8},{8,9},{14,1... | collective-permute-start | bytes 2359304 | tf_op jit(solution)/shard_map/ppermute | solution.py:537
  733.2 65.7 %collective-permute-start.55 = (bf16[256,1536]{1,0:T(8,128)(2,1)}, bf16[256,1536]{1,0:T(8,128)(2,1)}, u32[]{:S(2)}, u32[]{:S(2)}) collective-permute-start(bf16[256,1536]{1,0:T(8,128)(2,1)} %pad_maximum_fusion.22), channel_id=1, source_target_pairs={{0,0},{2,1},{4,2},{6,3},{1,4},{3,5},{5,6},{7,7},{8,8},{10,9},{12,1... | collective-permute-start | bytes 2359304 | tf_op jit(solution)/shard_map/ppermute | solution.py:537
  (99 other events, 1801.4 us)
Sparse Core Ops, SparseCore 0:
  14.2 43.6 all-gather.3
  59.4 77.5 all-gather.5
  139.2 62.5 all-gather.7
  494.4 32.8 reduce-scatter.4
  585.3 20.4 reduce-scatter.6
  621.6 76.8 reduce-scatter.8
  723.7 63.3 reduce-scatter.10

commit v8 on v7

--- a/solution.py
+++ b/solution.py
@@ -887,16 +887,19 @@
     ).reshape(seq_rows, -1)
     grad_one = [query_low, key_low, value_low, logit_low]
     one_sum = Reduction(plan, grad_one, normed_one)
-    one_sum.first, two_sum.last, outputs = together(one_sum.first, two_sum.last, outputs)
+    give_one, keep_one = combine(core, grad_one, kinds_one)
+    one_sum.first, two_sum.last, outputs, give_one = together(
+        one_sum.first, two_sum.last, outputs, give_one
+    )
     one_sum.send_first()
     outputs = plan.from_chip(outputs)
     one_sum.prepare_second()
     one_sum.send_second()
     two_total, out_pair = together(two_sum.finish(), out_pair)
     two_pair = plan.scatter(two_total)
-    one_total, two_pair, grad_one = together(one_sum.finish(), two_pair, grad_one)
+    one_total, two_pair = together(one_sum.finish(), two_pair)
     one_pair = plan.scatter(one_total)
-    grad_normed_one = plan.sum_rows(*combine(core, grad_one, kinds_one))
+    grad_normed_one = plan.sum_rows(give_one, keep_one)
     gain_one_term = jnp.sum(grad_normed_one * rows_in * scale_one, axis=0)
     input_grad = plan.from_chip(
         (grad_hidden + norm_back(rows_in, scale_one, gain_one, grad_normed_one)).astype(BF16)

time: 825 us -> 876 us (1.062)
  waiting for transfers between devices: 260 us -> 292 us
  starting transfers between devices: 101 us -> 117 us
    ppermute x4, waiting for transfers between devices: 0.01 us -> 50.9 us  [from_chip(): got.append(lax.ppermute(self.by_chip(part), ('dp', 'tensor'), back))]
    ppermute x4, starting transfers between devices: 10.8 us -> 29.6 us  [from_chip(): got.append(lax.ppermute(self.by_chip(part), ('dp', 'tensor'), back))]
    ppermute x36, waiting for transfers between devices: 127 us -> 117 us  [swap_chip(): return lax.ppermute(array, 'dp', perm)]
  transfers between devices with their start and end apart: 73 -> 73, of which waited for: 26 -> 25; matrix products, arithmetic and copies ran while one was open for 18% -> 17% of each run, Pallas kernels for 31% -> 29%
where the time goes in v8:
time: 876 us; the launch traced here: 865 us
  waiting for transfers between devices  292 us (33%)
  Pallas kernels  258 us (29%)
  starting transfers between devices  117 us (13%)
  other arithmetic  78.9 us (9%)
  local copies, waits for them, and re-layouts  67.9 us (8%)
  matrix products  34.9 us (4%)
  between operations  15.8 us (2%)
    ppermute x36, waiting for transfers between devices, swap_chip(): return lax.ppermute(array, 'dp', perm)  117 us
    pallas_call x4, Pallas kernels, combine(): pl.pallas_call(functools.partial(combine_kernel, lefts=len(lefts)), grid_...  64.1 us
    ppermute x4, waiting for transfers between devices, from_chip(): got.append(lax.ppermute(self.by_chip(part), ('dp', 'tensor'), back))  50.9 us
    ppermute x2, waiting for transfers between devices, sum_all(): vector = vector + lax.ppermute(vector, 'tensor', perm)  48.3 us
    pallas_call x10, Pallas kernels, term_sum(): pl.pallas_call(functools.partial(term_kernel, narrow=narrow, side=side),...  47.4 us
    ppermute x36, starting transfers between devices, swap_chip(): return lax.ppermute(array, 'dp', perm)  41.6 us
    all_gather x3, waiting for transfers between devices, line_gather(): return lax.all_gather(pair, 'tensor', axis=0, tiled=True)  37.6 us
    dot_general x12, matrix products, dot_first(): lax.dot_general(left, right, (((0,), (0,)), ((), ())), preferred_element_...  34.9 us
  transfers between devices with their start and end apart: 73, of which 25 were waited for; matrix products, arithmetic and copies ran while one was open for 17% of the time, Pallas kernels for 29%

profile of v8, /device:TPU:0, one launch (start us, length us, event | category | flops | bytes accessed | tf_op | source)
XLA Modules:
  0.0 865.5 jit_solution(8897889012765455275)
XLA Ops:
  20.2 37.6 %all-gather.4.cloned.1.call-done.refs_0_ = bf16[2368,384]{1,0:T(8,128)(2,1)} async-done(((bf16[592,384]{1,0:T(8,128)(2,1)}), bf16[2368,384]{1,0:T(8,128)(2,1)}) %all-gather.4.cloned.1.call-update) | async-done | bytes 1818640 | tf_op jit(solution)/shard_map/all_gather | solution.py:559
  80.2 18.9 %collective-permute-done.3.refs_1_ = bf16[2368,384]{1,0:T(8,128)(2,1)S(1)} collective-permute-done((bf16[2368,384]{1,0:T(8,128)(2,1)}, bf16[2368,384]{1,0:T(8,128)(2,1)S(1)}, u32[]{:S(2)}, u32[]{:S(2)}) %collective-permute-start.3) | collective-permute-done | bytes 1818656 | tf_op jit(solution)/shard_map/ppermute | solution.py:497
  130.0 15.7 %collective-permute-start.8 = (bf16[512,1536]{1,0:T(8,128)(2,1)}, bf16[512,1536]{1,0:T(8,128)(2,1)}, u32[]{:S(2)}, u32[]{:S(2)}) collective-permute-start(bf16[512,1536]{1,0:T(8,128)(2,1)} %fusion.10), channel_id=1, source_target_pairs={{0,4},{4,0},{8,12},{12,8},{16,20},{20,16},{24,28},{28,24},{1,5},{5... | collective-permute-start | bytes 4718600 | tf_op jit(solution)/shard_map/ppermute | solution.py:493
  157.6 16.3 %project.1 = (bf16[1024,768]{1,0:T(8,128)(2,1)}, bf16[1024,768]{1,0:T(8,128)(2,1)}, bf16[1024,768]{1,0:T(8,128)(2,1)}, f32[2,1024,32]{2,1,0:T(8,128)}) custom-call(bf16[1024,1536]{1,0:T(8,128)(2,1)} %pad_maximum_fusion.2.x_ref.refs_4_, bf16[2368,384]{1,0:T(8,128)(2,1)} %all-gather.4.cloned.1.call-done.refs_0_, bf16[2368,384]{1,0:T(8,128)(2,1)} %copy-done.12, ...), custom_call_target="tpu_custom_call" | custom-call | flops 7449083904 | bytes 15138816 | tf_op jit(solution)/shard_map/project/pallas_call | solution.py:217
  189.5 15.5 %collective-permute-done.12 = bf16[384,384]{1,0:T(8,128)(2,1)S(1)} collective-permute-done((bf16[384,384]{1,0:T(8,128)(2,1)S(1)}, bf16[384,384]{1,0:T(8,128)(2,1)S(1)}, u32[]{:S(2)}, u32[]{:S(2)}) %collective-permute-start.12) | collective-permute-done | bytes 294944 | tf_op jit(solution)/shard_map/ppermute | solution.py:497
  207.9 25.1 %shard_map.246 = (bf16[1024,768]{1,0:T(8,128)(2,1)}, f32[1024,768]{1,0:T(8,128)}) custom-call(s32[1]{0:T(128)} %bitcast.18.len_ref, bf16[1024,768]{1,0:T(8,128)(2,1)} %get-tuple-element.145.q_ref, bf16[1024,768]{1,0:T(8,128)(2,1)} %get-tuple-element.146.k_ref, bf16[1024,768]{1,0:T(8,128)(2,1)} %get-tuple-element.147.v_ref, f32[6,1024,2]{2,1,0:T(8,128)} %bitcast.181), custom_call_target="tpu_custom_call" | custom-call | flops 6442450944 | bytes 9437184 | tf_op jit(solution)/shard_map/pallas_call | solution.py:97
  257.6 35.0 %collective-permute-done.19 = bf16[1024,384]{1,0:T(8,128)(2,1)S(1)} collective-permute-done((bf16[1024,384]{1,0:T(8,128)(2,1)S(1)}, bf16[1024,384]{1,0:T(8,128)(2,1)S(1)}, u32[]{:S(2)}, u32[]{:S(2)}) %collective-permute-start.19) | collective-permute-done | bytes 786464 | tf_op jit(solution)/shard_map/ppermute | solution.py:497
  304.5 11.9 %collective-permute-done.26 = bf16[256,1536]{1,0:T(8,128)(2,1)S(1)} collective-permute-done((bf16[256,1536]{1,0:T(8,128)(2,1)S(1)}, bf16[256,1536]{1,0:T(8,128)(2,1)S(1)}, u32[]{:S(2)}, u32[]{:S(2)}) %collective-permute-start.26) | collective-permute-done | bytes 786464 | tf_op jit(solution)/shard_map/ppermute | solution.py:524
  318.0 14.0 %collective-permute-start.27 = (bf16[512,1536]{1,0:T(8,128)(2,1)}, bf16[512,1536]{1,0:T(8,128)(2,1)}, u32[]{:S(2)}, u32[]{:S(2)}) collective-permute-start(bf16[512,1536]{1,0:T(8,128)(2,1)} %fusion.18), channel_id=1, source_target_pairs={{0,4},{4,0},{8,12},{12,8},{16,20},{20,16},{24,28},{28,24},{1,5},{5... | collective-permute-start | bytes 4718600 | tf_op jit(solution)/shard_map/ppermute | solution.py:493
  336.9 20.5 %inner_units.1 = (f32[1024,2048]{1,0:T(8,128)}, f32[1024,2048]{1,0:T(8,128)}, bf16[1024,2048]{1,0:T(8,128)(2,1)}) custom-call(bf16[1024,1536]{1,0:T(8,128)(2,1)} %pad_maximum_fusion.3.x_ref.refs_1_, bf16[4096,384]{1,0:T(8,128)(2,1)} %all-gather.8.cloned.1.call-done.refs_0_.refs_1_, bf16[4096,384]{1,0:T(8,128)(2,1)} %collective-permute-done.21.refs_1_.refs_2_, ...), custom_call_target="tpu_custom_call" | custom-call | flops 12884901888 | bytes 36700160 | tf_op jit(solution)/shard_map/inner_units/pallas_call | solution.py:326
  375.1 17.8 %inner_grads.1.refs_0_ = bf16[1024,4096]{1,0:T(8,128)(2,1)} custom-call(bf16[1024,1536]{1,0:T(8,128)(2,1)} %pad_maximum_fusion.1.x_ref.refs_1_, f32[1024,2048]{1,0:T(8,128)} %get-tuple-element.180.gate_ref, f32[1024,2048]{1,0:T(8,128)} %get-tuple-element.181.up_ref, bf16[2048,384]{1,0:T(8,128)(2,1)} %bitcast.172, ...), custom_call_target="tpu_custom_call" | custom-call | flops 6442450944 | bytes 34603008 | tf_op jit(solution)/shard_map/inner_grads/pallas_call | solution.py:353
  421.5 25.3 %combine.5 = (bf16[512,1536]{1,0:T(8,128)(2,1)}, f32[512,1536]{1,0:T(8,128)}) custom-call(s32[1]{0:T(128)} %bitcast.17.core_ref, bf16[1024,4096]{1,0:T(8,128)(2,1)} %inner_grads.1.refs_0_, bf16[4096,384]{1,0:T(8,128)(2,1)} %all-gather.8.cloned.1.call-done.refs_0_.refs_1_, bf16[4096,384]{1,0:T(8,128)(2,1)} %collective-permute-done.21.refs_1_.refs_2_, ...), custom_call_target="tpu_custom_call" | custom-call | flops 12884901888 | bytes 25690112 | tf_op jit(solution)/shard_map/combine/pallas_call | solution.py:263
  446.8 14.4 %combine.6 = (bf16[512,1536]{1,0:T(8,128)(2,1)}, f32[512,1536]{1,0:T(8,128)}) custom-call(s32[1]{0:T(128)} %bitcast.17.core_ref, bf16[1024,2048]{1,0:T(8,128)(2,1)} %get-tuple-element.197.refs_0_, bf16[2048,384]{1,0:T(8,128)(2,1)} %bitcast.173, bf16[2048,384]{1,0:T(8,128)(2,1)} %collective-permute-done.15.refs_1_.refs_2_, ...), custom_call_target="tpu_custom_call" | custom-call | flops 6442450944 | bytes 15204352 | tf_op jit(solution)/shard_map/combine/pallas_call | solution.py:263
  528.2 32.8 %shard_map.247 = (bf16[1024,768]{1,0:T(8,128)(2,1)}, bf16[1024,768]{1,0:T(8,128)(2,1)}, bf16[1024,768]{1,0:T(8,128)(2,1)}, f32[1024,768]{1,0:T(8,128)}) custom-call(s32[1]{0:T(128)} %bitcast.18.len_ref, bf16[1024,768]{1,0:T(8,128)(2,1)} %get-tuple-element.145.q_ref, bf16[1024,768]{1,0:T(8,128)(2,1)} %get-tuple-element.146.k_ref, ...), custom_call_target="tpu_custom_call" | custom-call | flops 16106127360 | bytes 18874368 | tf_op jit(solution)/shard_map/pallas_call | solution.py:169
  567.8 13.2 %collective-permute-done.43 = bf16[768,384]{1,0:T(8,128)(2,1)} collective-permute-done((bf16[768,384]{1,0:T(8,128)(2,1)}, bf16[768,384]{1,0:T(8,128)(2,1)}, u32[]{:S(2)}, u32[]{:S(2)}) %collective-permute-start.43) | collective-permute-done | bytes 589856 | tf_op jit(solution)/shard_map/ppermute | solution.py:700
  608.7 16.7 %combine.7 = (bf16[512,1536]{1,0:T(8,128)(2,1)}, f32[512,1536]{1,0:T(8,128)}) custom-call(s32[1]{0:T(128)} %bitcast.17.core_ref, bf16[1024,768]{1,0:T(8,128)(2,1)} %get-tuple-element.216.refs_0_, bf16[1024,768]{1,0:T(8,128)(2,1)} %get-tuple-element.217.refs_1_, bf16[1024,768]{1,0:T(8,128)(2,1)} %get-tuple-element.218.refs_2_, ...), custom_call_target="tpu_custom_call" | custom-call | flops 7449083904 | bytes 16842752 | tf_op jit(solution)/shard_map/combine/pallas_call | solution.py:263
  625.4 12.3 %total_sum.4 = bf16[4096,384]{1,0:T(8,128)(2,1)} custom-call(bf16[1024,4096]{1,0:T(8,128)(2,1)} %inner_grads.1.refs_0_, bf16[1024,1536]{1,0:T(8,128)(2,1)} %pad_maximum_fusion.3.x_ref.refs_1_, bf16[2048,384]{1,0:T(8,128)(2,1)} %collective-permute-done.40.refs_2_, bf16[2048,384]{1,0:T(8,128)(2,1)} %collective-permute-done.37.refs_3_, ...), custom_call_target="tpu_custom_call" | custom-call | flops 3221225472 | bytes 9437184 | tf_op jit(solution)/shard_map/total_sum/pallas_call | solution.py:464
  657.2 50.9 %collective-permute-done.47 = bf16[256,1536]{1,0:T(8,128)(2,1)} collective-permute-done((bf16[256,1536]{1,0:T(8,128)(2,1)}, bf16[256,1536]{1,0:T(8,128)(2,1)}, u32[]{:S(2)}, u32[]{:S(2)}) %collective-permute-start.47) | collective-permute-done | bytes 786464 | tf_op jit(solution)/shard_map/ppermute | solution.py:537
  733.0 8.3 collective-permute-done.61.refs_8_
  741.2 10.1 %collective-permute-done.57.refs_5_ = bf16[1184,384]{1,0:T(8,128)(2,1)} collective-permute-done((bf16[1184,384]{1,0:T(8,128)(2,1)}, bf16[1184,384]{1,0:T(8,128)(2,1)}, u32[]{:S(2)}, u32[]{:S(2)}) %collective-permute-start.57) | collective-permute-done | bytes 909344 | tf_op jit(solution)/shard_map/ppermute | solution.py:497
  751.3 7.9 total_sum.3
  765.2 19.0 %collective-permute-start.50 = (bf16[256,1536]{1,0:T(8,128)(2,1)S(1)}, bf16[256,1536]{1,0:T(8,128)(2,1)S(1)}, u32[]{:S(2)}, u32[]{:S(2)}) collective-permute-start(bf16[256,1536]{1,0:T(8,128)(2,1)S(1)} %pad_maximum_fusion.23), channel_id=1, source_target_pairs={{2,0},{0,1},{6,2},{4,3},{3,4},{1,5},{7,6},{5,7},{10,8},{8,9},{14,1... | collective-permute-start | bytes 2359304 | tf_op jit(solution)/shard_map/ppermute | solution.py:537
  792.5 35.8 %collective-permute-done.54 = f32[3096]{0:T(1024)S(1)} collective-permute-done((f32[3096]{0:T(1024)S(1)}, f32[3096]{0:T(1024)S(1)}, u32[]{:S(2)}, u32[]{:S(2)}) %collective-permute-start.54) | collective-permute-done | bytes 12416 | tf_op jit(solution)/shard_map/ppermute | solution.py:595
  829.2 12.5 %collective-permute-done.55 = f32[3096]{0:T(1024)} collective-permute-done((f32[3096]{0:T(1024)S(1)}, f32[3096]{0:T(1024)}, u32[]{:S(2)}, u32[]{:S(2)}) %collective-permute-start.55) | collective-permute-done | bytes 12416 | tf_op jit(solution)/shard_map/ppermute | solution.py:595
  (434 shorter events, 362.2 us)
Async XLA Ops:
  14.0 131.8 %all-gather.6.cloned.1.call-start = ((), (), s32[]{:S(2)}) async-start(), calls=%async_computation.5 | async-start | bytes 2703360 | tf_op jit(solution)/shard_map/all_gather | solution.py:559
  20.2 185.7 %all-gather.8.cloned.1.call-start = ((), (), s32[]{:S(2)}) async-start(), calls=%async_computation.6 | async-start | bytes 3932160 | tf_op jit(solution)/shard_map/all_gather | solution.py:559
  106.6 478.2 %reduce-scatter.5.cloned.1.call-start = ((), (), s32[]{:S(2)}) async-start(), calls=%async_computation.7 | async-start | bytes 1966080 | tf_op jit(solution)/shard_map/reduce_scatter | solution.py:579
  152.4 80.7 %collective-permute-start.15 = (bf16[2048,384]{1,0:T(8,128)(2,1)S(1)}, bf16[2048,384]{1,0:T(8,128)(2,1)}, u32[]{:S(2)}, u32[]{:S(2)}) collective-permute-start(bf16[2048,384]{1,0:T(8,128)(2,1)S(1)} %bitcast.170), channel_id=1, source_target_pairs={{0,8},{4,12},{8,0},{12,4},{16,24},{20,28},{24,16},{28,20},{1,9},{5... | collective-permute-start | bytes 4718600 | tf_op jit(solution)/shard_map/ppermute | solution.py:497
  153.0 80.1 %collective-permute-start.16 = (bf16[2048,384]{1,0:T(8,128)(2,1)S(1)}, bf16[2048,384]{1,0:T(8,128)(2,1)}, u32[]{:S(2)}, u32[]{:S(2)}) collective-permute-start(bf16[2048,384]{1,0:T(8,128)(2,1)S(1)} %bitcast.171), channel_id=1, source_target_pairs={{0,16},{4,20},{8,24},{12,28},{16,0},{20,4},{24,8},{28,12},{1,17},{... | collective-permute-start | bytes 4718600 | tf_op jit(solution)/shard_map/ppermute | solution.py:497
  205.9 88.0 %collective-permute-start.21 = (bf16[4096,384]{1,0:T(8,128)(2,1)}, bf16[4096,384]{1,0:T(8,128)(2,1)}, u32[]{:S(2)}, u32[]{:S(2)}) collective-permute-start(bf16[4096,384]{1,0:T(8,128)(2,1)} %all-gather.8.cloned.1.call-done.refs_0_.refs_1_), channel_id=1, source_target_pairs={{0,8},{4,12},{8,0},{12,4},{16,24},{20,28},{24,16},{28,20},{1,9},{5... | collective-permute-start | bytes 9437192 | tf_op jit(solution)/shard_map/ppermute | solution.py:497
  206.4 87.5 %collective-permute-start.22 = (bf16[4096,384]{1,0:T(8,128)(2,1)}, bf16[4096,384]{1,0:T(8,128)(2,1)}, u32[]{:S(2)}, u32[]{:S(2)}) collective-permute-start(bf16[4096,384]{1,0:T(8,128)(2,1)} %all-gather.8.cloned.1.call-done.refs_0_.refs_1_), channel_id=1, source_target_pairs={{0,16},{4,20},{8,24},{12,28},{16,0},{20,4},{24,8},{28,12},{1,17},{... | collective-permute-start | bytes 9437192 | tf_op jit(solution)/shard_map/ppermute | solution.py:497
  420.9 51.1 %collective-permute-start.33 = (bf16[2048,384]{1,0:T(8,128)(2,1)}, bf16[2048,384]{1,0:T(8,128)(2,1)}, u32[]{:S(2)}, u32[]{:S(2)}) collective-permute-start(bf16[2048,384]{1,0:T(8,128)(2,1)} %fusion.25), channel_id=1, source_target_pairs={{0,8},{4,12},{8,0},{12,4},{16,24},{20,28},{24,16},{28,20},{1,9},{5... | collective-permute-start | bytes 4718600 | tf_op jit(solution)/shard_map/ppermute | solution.py:497
  493.9 143.8 %reduce-scatter.7.cloned.1.call-start = ((), (), s32[]{:S(2)}) async-start(), calls=%async_computation.8 | async-start | bytes 737280 | tf_op jit(solution)/shard_map/reduce_scatter | solution.py:579
  516.5 64.5 %collective-permute-start.40 = (bf16[2048,384]{1,0:T(8,128)(2,1)}, bf16[2048,384]{1,0:T(8,128)(2,1)}, u32[]{:S(2)}, u32[]{:S(2)}) collective-permute-start(bf16[2048,384]{1,0:T(8,128)(2,1)} %term_sum.12), channel_id=1, source_target_pairs={{0,8},{4,12},{8,0},{12,4},{16,24},{20,28},{24,16},{28,20},{1,9},{5... | collective-permute-start | bytes 4718600 | tf_op jit(solution)/shard_map/ppermute | solution.py:497
  517.2 63.8 %collective-permute-start.41 = (bf16[2048,384]{1,0:T(8,128)(2,1)}, bf16[2048,384]{1,0:T(8,128)(2,1)}, u32[]{:S(2)}, u32[]{:S(2)}) collective-permute-start(bf16[2048,384]{1,0:T(8,128)(2,1)} %term_sum.13), channel_id=1, source_target_pairs={{0,16},{4,20},{8,24},{12,28},{16,0},{20,4},{24,8},{28,12},{1,17},{... | collective-permute-start | bytes 4718600 | tf_op jit(solution)/shard_map/ppermute | solution.py:497
  526.3 54.7 %collective-permute-start.43 = (bf16[768,384]{1,0:T(8,128)(2,1)}, bf16[768,384]{1,0:T(8,128)(2,1)}, u32[]{:S(2)}, u32[]{:S(2)}) collective-permute-start(bf16[768,384]{1,0:T(8,128)(2,1)} %convolution_convert_fusion.1), channel_id=1, source_target_pairs={{0,16},{4,20},{8,24},{12,28},{16,0},{20,4},{24,8},{28,12},{1,17},{... | collective-permute-start | bytes 1769480 | tf_op jit(solution)/shard_map/ppermute | solution.py:700
  527.7 53.3 %collective-permute-start.44 = (bf16[768,384]{1,0:T(8,128)(2,1)}, bf16[768,384]{1,0:T(8,128)(2,1)}, u32[]{:S(2)}, u32[]{:S(2)}) collective-permute-start(bf16[768,384]{1,0:T(8,128)(2,1)} %convolution_convert_fusion), channel_id=1, source_target_pairs={{0,24},{4,28},{8,16},{12,20},{16,8},{20,12},{24,0},{28,4},{1,25},{... | collective-permute-start | bytes 1769480 | tf_op jit(solution)/shard_map/ppermute | solution.py:700
  584.8 174.4 %reduce-scatter.9.cloned.1.call-start = ((), (), s32[]{:S(2)}) async-start(), calls=%async_computation.9 | async-start | bytes 3932160 | tf_op jit(solution)/shard_map/reduce_scatter | solution.py:579
  637.8 209.3 %reduce-scatter.11.cloned.1.call-start = ((), (), s32[]{:S(2)}) async-start(), calls=%async_computation.10 | async-start | bytes 2273280 | tf_op jit(solution)/shard_map/reduce_scatter | solution.py:579
  639.6 74.0 %collective-permute-start.60 = (bf16[1184,384]{1,0:T(8,128)(2,1)S(1)}, bf16[1184,384]{1,0:T(8,128)(2,1)}, u32[]{:S(2)}, u32[]{:S(2)}) collective-permute-start(bf16[1184,384]{1,0:T(8,128)(2,1)S(1)} %copy-done.19), channel_id=1, source_target_pairs={{0,8},{4,12},{8,0},{12,4},{16,24},{20,28},{24,16},{28,20},{1,9},{5... | collective-permute-start | bytes 2727944 | tf_op jit(solution)/shard_map/ppermute | solution.py:497
  640.8 78.5 %collective-permute-start.56 = (bf16[1184,384]{1,0:T(8,128)(2,1)}, bf16[1184,384]{1,0:T(8,128)(2,1)}, u32[]{:S(2)}, u32[]{:S(2)}) collective-permute-start(bf16[1184,384]{1,0:T(8,128)(2,1)} %term_sum.14), channel_id=1, source_target_pairs={{0,16},{4,20},{8,24},{12,28},{16,0},{20,4},{24,8},{28,12},{1,17},{... | collective-permute-start | bytes 2727944 | tf_op jit(solution)/shard_map/ppermute | solution.py:497
  644.0 64.1 %collective-permute-start.47 = (bf16[256,1536]{1,0:T(8,128)(2,1)}, bf16[256,1536]{1,0:T(8,128)(2,1)}, u32[]{:S(2)}, u32[]{:S(2)}) collective-permute-start(bf16[256,1536]{1,0:T(8,128)(2,1)} %pad_maximum_fusion.21), channel_id=1, source_target_pairs={{2,0},{0,1},{6,2},{4,3},{3,4},{1,5},{7,6},{5,7},{10,8},{8,9},{14,1... | collective-permute-start | bytes 2359304 | tf_op jit(solution)/shard_map/ppermute | solution.py:537
  646.4 63.2 %collective-permute-start.46 = (bf16[256,1536]{1,0:T(8,128)(2,1)}, bf16[256,1536]{1,0:T(8,128)(2,1)}, u32[]{:S(2)}, u32[]{:S(2)}) collective-permute-start(bf16[256,1536]{1,0:T(8,128)(2,1)} %pad_maximum_fusion.20), channel_id=1, source_target_pairs={{0,0},{2,1},{4,2},{6,3},{1,4},{3,5},{5,6},{7,7},{8,8},{10,9},{12,1... | collective-permute-start | bytes 2359304 | tf_op jit(solution)/shard_map/ppermute | solution.py:537
  654.5 70.8 %collective-permute-start.48 = (bf16[512,1536]{1,0:T(8,128)(2,1)}, bf16[512,1536]{1,0:T(8,128)(2,1)S(1)}, u32[]{:S(2)}, u32[]{:S(2)}) collective-permute-start(bf16[512,1536]{1,0:T(8,128)(2,1)} %get-tuple-element.235), channel_id=1, source_target_pairs={{0,4},{4,0},{8,12},{12,8},{16,20},{20,16},{24,28},{28,24},{1,5},{5... | collective-permute-start | bytes 4718600 | tf_op jit(solution)/shard_map/ppermute | solution.py:493
  725.3 64.8 %collective-permute-start.63 = (bf16[192,192]{1,0:T(8,128)(2,1)}, bf16[192,192]{1,0:T(8,128)(2,1)}, u32[]{:S(2)}, u32[]{:S(2)}) collective-permute-start(bf16[192,192]{1,0:T(8,128)(2,1)} %constant_dynamic-slice_fusion.2), channel_id=1, source_target_pairs={{0,4},{4,0},{8,12},{12,8},{16,20},{20,16},{24,28},{28,24},{1,5},{5... | collective-permute-start | bytes 221192 | tf_op jit(solution)/shard_map/ppermute | solution.py:493
  729.0 55.2 %collective-permute-start.51 = (f32[3096]{0:T(1024)S(1)}, f32[3096]{0:T(1024)}, u32[]{:S(2)}, u32[]{:S(2)}) collective-permute-start(f32[3096]{0:T(1024)S(1)} %constant_dynamic-update-slice_fusion.3), channel_id=1, source_target_pairs={{0,4},{4,0},{8,12},{12,8},{16,20},{20,16},{24,28},{28,24},{1,5},{5... | collective-permute-start | bytes 37160 | tf_op jit(solution)/shard_map/ppermute | solution.py:493
  765.2 78.7 %collective-permute-start.50 = (bf16[256,1536]{1,0:T(8,128)(2,1)S(1)}, bf16[256,1536]{1,0:T(8,128)(2,1)S(1)}, u32[]{:S(2)}, u32[]{:S(2)}) collective-permute-start(bf16[256,1536]{1,0:T(8,128)(2,1)S(1)} %pad_maximum_fusion.23), channel_id=1, source_target_pairs={{2,0},{0,1},{6,2},{4,3},{3,4},{1,5},{7,6},{5,7},{10,8},{8,9},{14,1... | collective-permute-start | bytes 2359304 | tf_op jit(solution)/shard_map/ppermute | solution.py:537
  786.5 57.4 %collective-permute-start.49 = (bf16[256,1536]{1,0:T(8,128)(2,1)S(1)}, bf16[256,1536]{1,0:T(8,128)(2,1)}, u32[]{:S(2)}, u32[]{:S(2)}) collective-permute-start(bf16[256,1536]{1,0:T(8,128)(2,1)S(1)} %pad_maximum_fusion.22), channel_id=1, source_target_pairs={{0,0},{2,1},{4,2},{6,3},{1,4},{3,5},{5,6},{7,7},{8,8},{10,9},{12,1... | collective-permute-start | bytes 2359304 | tf_op jit(solution)/shard_map/ppermute | solution.py:537
  (93 other events, 1929.0 us)
Sparse Core Ops, SparseCore 0:
  14.2 43.6 all-gather.3
  59.4 77.5 all-gather.5
  139.2 62.5 all-gather.7
  494.1 32.8 reduce-scatter.4
  584.9 20.4 reduce-scatter.6
  637.9 83.4 reduce-scatter.8
  759.4 74.8 reduce-scatter.10
